TPU v7x, 256 devices: a whole 4x4x8 slice. The times are simulated.
256 devices in a mesh: leaf: 64 (over y, z, core), probe: 4 (over x).
Axes of the slice: x: 4, y: 4, z: 8, core: 2. Of those that a mesh axis runs over, the one named last changes fastest.
Arguments:
- coords: float32 [3, 262144], P(None, 'leaf')
- site_order: int32 [1024, 256], P('leaf'), may hold values from 0 to 255, each once within a row
- leaf_pairs: int32 [2, 6144], P(None, 'leaf'), may hold values from 0 to 1023, as said below
- pair_count: int32 [64], P('leaf'), may hold values from 31 to 96, as said below
- probes: float32 [64, 262144], P('probe', 'leaf'), may hold values from -16 to 16
Outputs:
- solution: float32 [64, 262144], P('probe', 'leaf')
- residual: float32 [64, 262144], P('probe', 'leaf')
Inputs may be any that keep to these rules, and one draw needn't show every extreme that they name: `leaf_pairs`: each leaf index owns 96 slots; its first pair_count slots hold distinct pairs (i, j) with i among that index's own 16 leaves and i <= j <= i + 5, j < 1024, every own leaf listed with itself once and with the next leaf where there is one; the later slots hold the index's first leaf twice. `pair_count`: pairs listed for each leaf index; some index lists 96 in every draw. Each row of site_order lists 0 to 255 once.
All inputs are finite; a program needn't handle non-finite values.
Results may differ from a plain program's by a relative error of at most 0.0003.
Values sent between devices are 32-bit elements; how exact they have to be, the bound alone decides.
No kernel may reach another device: no remote copies, remote signals or barrier semaphores. Data moves between devices by JAX's collectives and lax.ppermute only.
A program may use at most 64 MiB of HBM per device.

v0:
```python
import math

import jax
import jax.numpy as jnp
from jax import lax
from jax.sharding import PartitionSpec as P

REACH = 5
ITERS = 2


UNIT = 0.025
LENGTH = 0.12
NUGGET = 0.5
UPPER_LIMIT = lax.Precision.HIGHEST


def from_behind(value, axis, by):
    length = lax.axis_size(axis)
    pairs = [(i, i + by) for i in range(length) if 0 <= i + by < length]
    return lax.ppermute(value, axis, pairs)


def in_order(parts, dim):
    lengths = list(parts.shape[1:])
    lengths[dim] *= parts.shape[0]
    return jnp.moveaxis(parts, 0, dim).reshape(lengths)


def sent_to_all(value, axis):
    copies = jnp.broadcast_to(value, (lax.axis_size(axis), *value.shape))
    return lax.all_to_all(copies, axis, split_axis=0, concat_axis=0, tiled=True)


def collect(value, axis, dim):
    return in_order(sent_to_all(value, axis), dim)


def in_one_piece(arrays, axis, dim, along):
    widths = [a.shape[along] for a in arrays]
    both = jnp.concatenate(arrays, axis=along)
    out = collect(both, axis, dim)
    return tuple(jnp.split(out, [sum(widths[:k]) for k in range(1, len(widths))], axis=along))


def split_up(value, dim, length):
    before, after = (value.shape[:dim], value.shape[dim + 1 :])
    return jnp.moveaxis(value.reshape(*before, length, -1, *after), dim, 0)


def sum_at_owner(value, axis, dim):
    parts = split_up(value, dim, lax.axis_size(axis))
    arrived = lax.all_to_all(parts, axis, split_axis=0, concat_axis=0, tiled=True)
    return arrived.sum(axis=0)


def over_copies(value, axis):
    everything = sent_to_all(value, axis)
    return jnp.sum(everything, axis=0)


def together(arrays, axis):
    ends = [0]
    for a in arrays:
        ends.append(ends[-1] + a.size)
    total = over_copies(jnp.concatenate([a.ravel() for a in arrays]), axis)
    return tuple((total[b:e].reshape(a.shape) for a, b, e in zip(arrays, ends, ends[1:])))


def kernel_tiles(left, right):
    diff = left[:, :, :, None] - right[:, :, None, :]
    dist = jnp.sqrt(jnp.sum(diff * diff, axis=0))
    taper = REACH * UNIT
    scaled = dist * (math.sqrt(3.0) / LENGTH)
    remain = jnp.maximum(1.0 - dist / taper, 0.0)
    return (1.0 + scaled) * jnp.exp(-scaled) * remain**4 * (1.0 + 4.0 * dist / taper)


def body(coords, site_order, leaf_pairs, pair_count, probes):
    leaf_dev, width = site_order.shape
    columns = probes.shape[0]
    points = jnp.take_along_axis(coords.reshape(3, leaf_dev, width), site_order[None], axis=2)
    next_points = from_behind(points[:, :REACH], "leaf", -1)
    all_points = jnp.concatenate([points, next_points], axis=1)
    base = lax.axis_index("leaf") * leaf_dev
    local_rows = leaf_pairs[0] - base
    leaf_local_columns = leaf_pairs[1] - base
    count = pair_count[0]
    extent = leaf_dev + REACH
    span = 8
    blocks = (count + span - 1) // span
    spots = jnp.arange(extent)
    right = probes.reshape(columns, leaf_dev, width)
    solution = jnp.zeros_like(right)
    residual = right
    direction = right
    norm_now = over_copies(jnp.sum(residual * residual, axis=(1, 2)), "leaf")
    for step in range(ITERS):
        rim = from_behind(direction[:, :REACH], "leaf", -1)
        whole, far = in_one_piece((direction, rim), "probe", 0, 1)
        values = jnp.concatenate([whole, far], axis=1)
        first = lax.axis_index("probe")

        def one_block(turn, grand_total):
            start = (first + turn * lax.axis_size("probe")) * span
            rows = lax.dynamic_slice_in_dim(local_rows, start, span)
            cols = lax.dynamic_slice_in_dim(leaf_local_columns, start, span)
            live = (start + jnp.arange(span) < count).astype(jnp.float32)
            tiles = kernel_tiles(
                jnp.take(all_points, rows, axis=1), jnp.take(all_points, cols, axis=1)
            )
            tiles = tiles * live[:, None, None]
            to_row = jnp.einsum(
                "bak,cbk->cba", tiles, jnp.take(values, cols, axis=1), precision=UPPER_LIMIT
            )
            apart = (rows != cols).astype(jnp.float32)
            column_target = jnp.einsum(
                "bak,cba->cbk", tiles, jnp.take(values, rows, axis=1), precision=UPPER_LIMIT
            )
            column_target = column_target * apart[None, :, None]
            row_onehot = (rows[:, None] == spots[None, :]).astype(jnp.float32)
            column_onehot = (cols[:, None] == spots[None, :]).astype(jnp.float32)
            grand_total = grand_total + jnp.einsum(
                "cba,bl->cla", to_row, row_onehot, precision=UPPER_LIMIT
            )
            return grand_total + jnp.einsum(
                "egs,gu->eus", column_target, column_onehot, precision=UPPER_LIMIT
            )

        turns = (blocks - first + lax.axis_size("probe") - 1) // lax.axis_size("probe")
        summed = lax.fori_loop(0, turns, one_block, jnp.zeros(values.shape, jnp.float32))
        reduced = sum_at_owner(summed, "probe", 0)
        operator_back = from_behind(reduced[:, leaf_dev:], "leaf", 1)
        front = reduced[:, :leaf_dev]
        own = jnp.concatenate([front[:, :REACH] + operator_back, front[:, REACH:]], axis=1)
        image = NUGGET * direction + own
        curve, cross, square = together(
            (
                jnp.sum(direction * image, axis=(1, 2)),
                jnp.sum(residual * image, axis=(1, 2)),
                jnp.sum(image * image, axis=(1, 2)),
            ),
            "leaf",
        )
        alpha = norm_now / curve
        solution = solution + alpha[:, None, None] * direction
        residual = residual - alpha[:, None, None] * image
        if step + 1 < ITERS:
            norm_next = norm_now - 2.0 * alpha * cross + alpha * alpha * square
            direction = residual + (norm_next / norm_now)[:, None, None] * direction
            norm_now = norm_next
    return (
        solution.reshape(columns, leaf_dev * width),
        residual.reshape(columns, leaf_dev * width),
    )


def solution(mesh):
    in_specs = (P(None, "leaf"), P("leaf", None), P(None, "leaf"), P("leaf"), P("probe", "leaf"))
    out_specs = (P("probe", "leaf"), P("probe", "leaf"))
    return jax.shard_map(body, mesh=mesh, in_specs=in_specs, out_specs=out_specs, check_vma=False)
```

profile of v0, /device:TPU:1, one launch (start us, length us, event | category | flops | bytes accessed | tf_op | source)
XLA Modules:
  0.0 312.4 jit_solution(12520317104991195902)
XLA Ops:
  1.7 5.1 %collective-permute-start = (f32[16,5,256]{2,1,0:T(8,128)S(1)}, f32[16,5,256]{2,1,0:T(8,128)S(1)}, u32[]{:S(2)}, u32[]{:S(2)}) collective-permute-start(f32[16,5,256]{2,1,0:T(8,128)S(1)} %slice.86), channel_id=1, source_target_pairs={{4,0},{8,4},{12,8},{16,12},{20,16},{24,20},{28,24},{32,28},{36,32}... | collective-permute-start | bytes 245768 | tf_op jit(solution)/shard_map/ppermute | solution.py:21
  10.7 4.1 %all-to-all-start.1 = ((f32[4,16,21,256]{3,1,2,0:T(8,128)}), f32[4,16,21,256]{3,1,2,0:T(8,128)S(1)}, u32[]{:S(2)}, u32[]{:S(2)}) async-start(f32[4,16,21,256]{3,1,2,0:T(8,128)} %broadcast_in_dim.45), calls=%async_computation.1 | async-start | bytes 2752512 | tf_op jit(solution)/shard_map/all_to_all | solution.py:32
  15.5 44.4 %gather_fusion.8 = f32[4096,3]{1,0:T(8,128)} fusion(f32[3,16,256]{0,2,1:T(8,128)S(1)} %bitcast.145, s32[4096]{0:T(1024)S(1)} %bitcast.137), kind=kCustom, calls=%fused_computation.8 | custom fusion | bytes 131072 | tf_op jit(solution)/shard_map/jit(take_along_axis)/gather | solution.py:82
  68.7 57.1 %while.28 = (s32[]{:T(128)}, f32[64,21,256]{2,1,0:T(8,128)S(1)}, s32[]{:T(128)}, s32[]{:T(128)}, s32[96]{0:T(128)S(1)}, /*index=5*/s32[96]{0:T(128)S(1)}, f32[64...) while((s32[]{:T(128)}, f32[64,21,256]{2,1,0:T(8,128)S(1)}, ...), condition=%wide.region_4.7_spmd.clone.clone, body=%wide.region_2.0_spmd.clone.clone.sunk | while | flops 891337280 | bytes 25781260 | solution.py:131
  74.1 3.6 %convolution_bitcast_fusion.4 = f32[64,8,256]{2,0,1:T(8,128)S(1)} fusion(f32[8,64,256]{2,1,0:T(8,128)S(1)} %gather_fusion, pred[8]{0:T(512)(128)(4,1)S(1)} %compare_and_fusion.9, f32[8,256,256]{2,1,0:T(8,128)S(1)} %multiply_reduce_fusion.10, f32[8]{0:T(128)S(1)} %get-tuple-element.530), kind=kOutput, calls=%fused_computation.15.clone.1 | convolution fusion | flops 410124288 | bytes 3145768 | tf_op jit(solution)/shard_map/while/body/bak,cbk->cba/dot_general | solution.py:113
  78.7 2.7 gather_fusion.3
  81.4 4.7 %fusion.73 = f32[64,8,256]{2,0,1:T(8,128)S(1)} fusion(f32[8,64,256]{2,1,0:T(8,128)} %gather_fusion.3, f32[8]{0:T(128)S(1)} %get-tuple-element.531, pred[8]{0:T(512)(128)(4,1)S(1)} %compare_and_fusion.10, f32[8,256,256]{2,1,0:T(8,128)} %copy-done, f32[8]{0:T(128)S(1)} %get-tuple-element.530), kind=kOutput, calls=%fused_computation.17.clone.1 | convolution fusion | flops 410255360 | bytes 3145800 | tf_op jit(solution)/shard_map/while/body/bak,cba->cbk/dot_general | solution.py:117
  93.1 3.6 %convolution_bitcast_fusion.4 = f32[64,8,256]{2,0,1:T(8,128)S(1)} fusion(f32[8,64,256]{2,1,0:T(8,128)S(1)} %gather_fusion, pred[8]{0:T(512)(128)(4,1)S(1)} %compare_and_fusion.9, f32[8,256,256]{2,1,0:T(8,128)S(1)} %multiply_reduce_fusion.10, f32[8]{0:T(128)S(1)} %get-tuple-element.530), kind=kOutput, calls=%fused_computation.15.clone.1 | convolution fusion | flops 410124288 | bytes 3145768 | tf_op jit(solution)/shard_map/while/body/bak,cbk->cba/dot_general | solution.py:113
  97.7 2.7 gather_fusion.3
  100.4 4.7 %fusion.73 = f32[64,8,256]{2,0,1:T(8,128)S(1)} fusion(f32[8,64,256]{2,1,0:T(8,128)} %gather_fusion.3, f32[8]{0:T(128)S(1)} %get-tuple-element.531, pred[8]{0:T(512)(128)(4,1)S(1)} %compare_and_fusion.10, f32[8,256,256]{2,1,0:T(8,128)} %copy-done, f32[8]{0:T(128)S(1)} %get-tuple-element.530), kind=kOutput, calls=%fused_computation.17.clone.1 | convolution fusion | flops 410255360 | bytes 3145800 | tf_op jit(solution)/shard_map/while/body/bak,cba->cbk/dot_general | solution.py:117
  112.1 3.6 %convolution_bitcast_fusion.4 = f32[64,8,256]{2,0,1:T(8,128)S(1)} fusion(f32[8,64,256]{2,1,0:T(8,128)S(1)} %gather_fusion, pred[8]{0:T(512)(128)(4,1)S(1)} %compare_and_fusion.9, f32[8,256,256]{2,1,0:T(8,128)S(1)} %multiply_reduce_fusion.10, f32[8]{0:T(128)S(1)} %get-tuple-element.530), kind=kOutput, calls=%fused_computation.15.clone.1 | convolution fusion | flops 410124288 | bytes 3145768 | tf_op jit(solution)/shard_map/while/body/bak,cbk->cba/dot_general | solution.py:113
  116.7 2.7 gather_fusion.3
  119.4 4.7 %fusion.73 = f32[64,8,256]{2,0,1:T(8,128)S(1)} fusion(f32[8,64,256]{2,1,0:T(8,128)} %gather_fusion.3, f32[8]{0:T(128)S(1)} %get-tuple-element.531, pred[8]{0:T(512)(128)(4,1)S(1)} %compare_and_fusion.10, f32[8,256,256]{2,1,0:T(8,128)} %copy-done, f32[8]{0:T(128)S(1)} %get-tuple-element.530), kind=kOutput, calls=%fused_computation.17.clone.1 | convolution fusion | flops 410255360 | bytes 3145800 | tf_op jit(solution)/shard_map/while/body/bak,cba->cbk/dot_general | solution.py:117
  126.3 15.5 %all_to_all.38 = f32[4,16,21,256]{3,1,2,0:T(8,128)S(1)} all-to-all(f32[4,16,21,256]{3,1,2,0:T(8,128)S(1)} %copy.171), channel_id=1, replica_groups=mesh['leaf'=64,'probe'=4] {'probe'}, dimensions={0} | all-to-all | bytes 2752512 | tf_op jit(solution)/shard_map/all_to_all | solution.py:53
  147.0 16.2 %all-to-all-start = ((f32[64,1,16]{2,1,0:T(1,128)}), f32[64,1,16]{2,1,0:T(1,128)S(1)}, u32[]{:S(2)}, u32[]{:S(2)}) async-start(f32[64,1,16]{2,1,0:T(1,128)} %broadcast_in_dim.44), calls=%async_computation | async-start | bytes 65536 | tf_op jit(solution)/shard_map/all_to_all | solution.py:32
  163.3 9.1 %all-to-all-done = f32[64,1,16]{2,1,0:T(1,128)S(1)} async-done(((f32[64,1,16]{2,1,0:T(1,128)}), f32[64,1,16]{2,1,0:T(1,128)S(1)}, u32[]{:S(2)}, u32[]{:S(2)}) %all-to-all-start) | async-done | bytes 4128 | tf_op jit(solution)/shard_map/all_to_all | solution.py:32
  173.0 4.9 %all-to-all-start.3 = ((f32[64,1,48]{2,1,0:T(1,128)}), f32[64,1,48]{2,1,0:T(1,128)S(1)}, u32[]{:S(2)}, u32[]{:S(2)}) async-start(f32[64,1,48]{2,1,0:T(1,128)} %broadcast_in_dim.56), calls=%async_computation.3 | async-start | bytes 65536 | tf_op jit(solution)/shard_map/all_to_all | solution.py:32
  178.0 9.2 %all-to-all-done.3 = f32[64,1,48]{2,1,0:T(1,128)S(1)} async-done(((f32[64,1,48]{2,1,0:T(1,128)}), f32[64,1,48]{2,1,0:T(1,128)S(1)}, u32[]{:S(2)}, u32[]{:S(2)}) %all-to-all-start.3) | async-done | bytes 12320 | tf_op jit(solution)/shard_map/all_to_all | solution.py:32
  190.2 3.2 %collective-permute-done.3 = f32[16,5,256]{2,0,1:T(8,128)S(1)} collective-permute-done((f32[16,5,256]{2,0,1:T(8,128)S(1)}, f32[16,5,256]{2,0,1:T(8,128)S(1)}, u32[]{:S(2)}, u32[]{:S(2)}) %collective-permute-start.3) | collective-permute-done | bytes 81952 | tf_op jit(solution)/shard_map/ppermute | solution.py:21
  194.6 3.5 %all-to-all-start.4 = ((f32[4,16,21,256]{3,1,2,0:T(8,128)}), f32[4,16,21,256]{3,1,2,0:T(8,128)S(1)}, u32[]{:S(2)}, u32[]{:S(2)}) async-start(f32[4,16,21,256]{3,1,2,0:T(8,128)} %broadcast_in_dim.57), calls=%async_computation.4 | async-start | bytes 2752512 | tf_op jit(solution)/shard_map/all_to_all | solution.py:32
  198.2 17.4 %all-to-all-done.4 = f32[4,16,21,256]{3,1,2,0:T(8,128)S(1)} async-done(((f32[4,16,21,256]{3,1,2,0:T(8,128)}), f32[4,16,21,256]{3,1,2,0:T(8,128)S(1)}, u32[]{:S(2)}, u32[]{:S(2)}) %all-to-all-start.4) | async-done | bytes 1376288 | tf_op jit(solution)/shard_map/all_to_all | solution.py:32
  216.9 56.9 %while.29 = (s32[]{:T(128)}, f32[64,21,256]{2,1,0:T(8,128)S(1)}, s32[]{:T(128)}, s32[]{:T(128)}, s32[96]{0:T(128)S(1)}, /*index=5*/s32[96]{0:T(128)S(1)}, f32[64...) while((s32[]{:T(128)}, f32[64,21,256]{2,1,0:T(8,128)S(1)}, ...), condition=%wide.region_11.14_spmd.clone.clone, body=%wide.region_9.13_spmd.clone.clone.sunk | while | flops 891337280 | bytes 25781260 | solution.py:131
  222.1 3.6 %convolution_bitcast_fusion.5 = f32[64,8,256]{2,0,1:T(8,128)S(1)} fusion(f32[8,64,256]{2,1,0:T(8,128)S(1)} %gather_fusion.4, pred[8]{0:T(512)(128)(4,1)S(1)} %compare_and_fusion.11, f32[8,256,256]{2,1,0:T(8,128)S(1)} %multiply_reduce_fusion.11, f32[8]{0:T(128)S(1)} %get-tuple-element.543), kind=kOutput, calls=%fused_computation.51.clone.1 | convolution fusion | flops 410124288 | bytes 3145768 | tf_op jit(solution)/shard_map/while/body/bak,cbk->cba/dot_general | solution.py:113
  226.7 2.7 gather_fusion.7
  229.4 4.7 %fusion.81 = f32[64,8,256]{2,0,1:T(8,128)S(1)} fusion(f32[8,64,256]{2,1,0:T(8,128)} %gather_fusion.7, f32[8]{0:T(128)S(1)} %get-tuple-element.544, pred[8]{0:T(512)(128)(4,1)S(1)} %compare_and_fusion.12, f32[8,256,256]{2,1,0:T(8,128)} %copy-done.1, f32[8]{0:T(128)S(1)} %get-tuple-element.543), kind=kOutput, calls=%fused_computation.53.clone.1 | convolution fusion | flops 410255360 | bytes 3145800 | tf_op jit(solution)/shard_map/while/body/bak,cba->cbk/dot_general | solution.py:117
  241.1 3.6 %convolution_bitcast_fusion.5 = f32[64,8,256]{2,0,1:T(8,128)S(1)} fusion(f32[8,64,256]{2,1,0:T(8,128)S(1)} %gather_fusion.4, pred[8]{0:T(512)(128)(4,1)S(1)} %compare_and_fusion.11, f32[8,256,256]{2,1,0:T(8,128)S(1)} %multiply_reduce_fusion.11, f32[8]{0:T(128)S(1)} %get-tuple-element.543), kind=kOutput, calls=%fused_computation.51.clone.1 | convolution fusion | flops 410124288 | bytes 3145768 | tf_op jit(solution)/shard_map/while/body/bak,cbk->cba/dot_general | solution.py:113
  245.6 2.7 gather_fusion.7
  248.4 4.7 %fusion.81 = f32[64,8,256]{2,0,1:T(8,128)S(1)} fusion(f32[8,64,256]{2,1,0:T(8,128)} %gather_fusion.7, f32[8]{0:T(128)S(1)} %get-tuple-element.544, pred[8]{0:T(512)(128)(4,1)S(1)} %compare_and_fusion.12, f32[8,256,256]{2,1,0:T(8,128)} %copy-done.1, f32[8]{0:T(128)S(1)} %get-tuple-element.543), kind=kOutput, calls=%fused_computation.53.clone.1 | convolution fusion | flops 410255360 | bytes 3145800 | tf_op jit(solution)/shard_map/while/body/bak,cba->cbk/dot_general | solution.py:117
  260.1 3.6 %convolution_bitcast_fusion.5 = f32[64,8,256]{2,0,1:T(8,128)S(1)} fusion(f32[8,64,256]{2,1,0:T(8,128)S(1)} %gather_fusion.4, pred[8]{0:T(512)(128)(4,1)S(1)} %compare_and_fusion.11, f32[8,256,256]{2,1,0:T(8,128)S(1)} %multiply_reduce_fusion.11, f32[8]{0:T(128)S(1)} %get-tuple-element.543), kind=kOutput, calls=%fused_computation.51.clone.1 | convolution fusion | flops 410124288 | bytes 3145768 | tf_op jit(solution)/shard_map/while/body/bak,cbk->cba/dot_general | solution.py:113
  267.3 4.7 %fusion.81 = f32[64,8,256]{2,0,1:T(8,128)S(1)} fusion(f32[8,64,256]{2,1,0:T(8,128)} %gather_fusion.7, f32[8]{0:T(128)S(1)} %get-tuple-element.544, pred[8]{0:T(512)(128)(4,1)S(1)} %compare_and_fusion.12, f32[8,256,256]{2,1,0:T(8,128)} %copy-done.1, f32[8]{0:T(128)S(1)} %get-tuple-element.543), kind=kOutput, calls=%fused_computation.53.clone.1 | convolution fusion | flops 410255360 | bytes 3145800 | tf_op jit(solution)/shard_map/while/body/bak,cba->cbk/dot_general | solution.py:117
  274.2 13.9 %all_to_all.39 = f32[4,16,21,256]{3,1,2,0:T(8,128)S(1)} all-to-all(f32[4,16,21,256]{3,1,2,0:T(8,128)S(1)} %copy.179), channel_id=1, replica_groups=mesh['leaf'=64,'probe'=4] {'probe'}, dimensions={0} | all-to-all | bytes 2752512 | tf_op jit(solution)/shard_map/all_to_all | solution.py:53
  292.2 19.1 %all_to_all.40 = f32[64,1,48]{2,1,0:T(1,128)S(1)} all-to-all(f32[64,1,48]{2,1,0:T(1,128)S(1)} %broadcast_in_dim.58), channel_id=1, replica_groups=mesh['leaf'=64,'probe'=4] {'leaf'}, dimensions={0} | all-to-all | bytes 24576 | tf_op jit(solution)/shard_map/all_to_all | solution.py:32
  (187 shorter events, 80.6 us)
Async XLA Ops:
  1.7 7.6 %collective-permute-start = (f32[16,5,256]{2,1,0:T(8,128)S(1)}, f32[16,5,256]{2,1,0:T(8,128)S(1)}, u32[]{:S(2)}, u32[]{:S(2)}) collective-permute-start(f32[16,5,256]{2,1,0:T(8,128)S(1)} %slice.86), channel_id=1, source_target_pairs={{4,0},{8,4},{12,8},{16,12},{20,16},{24,20},{28,24},{32,28},{36,32}... | collective-permute-start | bytes 245768 | tf_op jit(solution)/shard_map/ppermute | solution.py:21
  9.4 5.4 %copy-start.5 = (f32[3,4096]{1,0:T(4,128)S(1)}, f32[3,4096]{1,0:T(4,128)}, u32[]{:S(2)}) copy-start(f32[3,4096]{1,0:T(4,128)} %param.13) | copy-start | bytes 147460
  10.7 4.8 %copy-start.6 = (s32[16,256]{1,0:T(8,128)S(1)}, s32[16,256]{1,0:T(8,128)}, u32[]{:S(2)}) copy-start(s32[16,256]{1,0:T(8,128)} %param.14) | copy-start | bytes 49156
  10.7 56.7 %all-to-all-start.1 = ((f32[4,16,21,256]{3,1,2,0:T(8,128)}), f32[4,16,21,256]{3,1,2,0:T(8,128)S(1)}, u32[]{:S(2)}, u32[]{:S(2)}) async-start(f32[4,16,21,256]{3,1,2,0:T(8,128)} %broadcast_in_dim.45), calls=%async_computation.1 | async-start | bytes 2752512 | tf_op jit(solution)/shard_map/all_to_all | solution.py:32
  15.5 46.7 %copy-start.7 = (s32[16,256]{1,0:T(8,128)S(1)}, s32[16,256]{1,0:T(8,128)}, u32[]{:S(2)}) copy-start(s32[16,256]{1,0:T(8,128)} %param.14) | copy-start | bytes 49156
  15.5 48.7 %copy-start.8 = (s32[2,96]{1,0:T(2,128)S(1)}, s32[2,96]{1,0:T(2,128)}, u32[]{:S(2)}) copy-start(s32[2,96]{1,0:T(2,128)} %param.15) | copy-start | bytes 2308
  62.3 5.1 %collective-permute-start.1 = (f32[3,5,256]{2,0,1:T(4,128)S(1)}, f32[3,5,256]{2,0,1:T(4,128)S(1)}, u32[]{:S(2)}, u32[]{:S(2)}) collective-permute-start(f32[3,5,256]{2,0,1:T(4,128)S(1)} %slice.87), channel_id=1, source_target_pairs={{4,0},{8,4},{12,8},{16,12},{20,16},{24,20},{28,24},{32,28},{36,32}... | collective-permute-start | bytes 46088 | tf_op jit(solution)/shard_map/ppermute | solution.py:21
  74.1 3.6 %copy-start = (f32[8,256,256]{2,1,0:T(8,128)}, f32[8,256,256]{2,1,0:T(8,128)S(1)}, u32[]{:S(2)}) copy-start(f32[8,256,256]{2,1,0:T(8,128)S(1)} %multiply_reduce_fusion.10) | copy-start | bytes 6291460 | tf_op jit(solution)/shard_map/while
  93.1 3.6 %copy-start = (f32[8,256,256]{2,1,0:T(8,128)}, f32[8,256,256]{2,1,0:T(8,128)S(1)}, u32[]{:S(2)}) copy-start(f32[8,256,256]{2,1,0:T(8,128)S(1)} %multiply_reduce_fusion.10) | copy-start | bytes 6291460 | tf_op jit(solution)/shard_map/while
  112.1 3.6 %copy-start = (f32[8,256,256]{2,1,0:T(8,128)}, f32[8,256,256]{2,1,0:T(8,128)S(1)}, u32[]{:S(2)}) copy-start(f32[8,256,256]{2,1,0:T(8,128)S(1)} %multiply_reduce_fusion.10) | copy-start | bytes 6291460 | tf_op jit(solution)/shard_map/while
  141.8 4.3 %copy-start.2 = (f32[16,4096]{1,0:T(8,128)S(1)}, f32[16,4096]{1,0:T(8,128)}, u32[]{:S(2)}) copy-start(f32[16,4096]{1,0:T(8,128)} %param.17) | copy-start | bytes 786436
  142.0 3.4 %collective-permute-start.2 = (f32[16,5,256]{2,0,1:T(8,128)S(1)}, f32[16,5,256]{2,0,1:T(8,128)S(1)}, u32[]{:S(2)}, u32[]{:S(2)}) collective-permute-start(f32[16,5,256]{2,0,1:T(8,128)S(1)} %slice.89), channel_id=1, source_target_pairs={{0,4},{4,8},{8,12},{12,16},{16,20},{20,24},{24,28},{28,32},{32,36}... | collective-permute-start | bytes 245768 | tf_op jit(solution)/shard_map/ppermute | solution.py:21
  145.4 0.7 copy-start.3
  147.0 25.4 %all-to-all-start = ((f32[64,1,16]{2,1,0:T(1,128)}), f32[64,1,16]{2,1,0:T(1,128)S(1)}, u32[]{:S(2)}, u32[]{:S(2)}) async-start(f32[64,1,16]{2,1,0:T(1,128)} %broadcast_in_dim.44), calls=%async_computation | async-start | bytes 65536 | tf_op jit(solution)/shard_map/all_to_all | solution.py:32
  173.0 14.2 %all-to-all-start.3 = ((f32[64,1,48]{2,1,0:T(1,128)}), f32[64,1,48]{2,1,0:T(1,128)S(1)}, u32[]{:S(2)}, u32[]{:S(2)}) async-start(f32[64,1,48]{2,1,0:T(1,128)} %broadcast_in_dim.56), calls=%async_computation.3 | async-start | bytes 65536 | tf_op jit(solution)/shard_map/all_to_all | solution.py:32
  187.6 5.8 %collective-permute-start.3 = (f32[16,5,256]{2,0,1:T(8,128)S(1)}, f32[16,5,256]{2,0,1:T(8,128)S(1)}, u32[]{:S(2)}, u32[]{:S(2)}) collective-permute-start(f32[16,5,256]{2,0,1:T(8,128)S(1)} %slice.91), channel_id=1, source_target_pairs={{4,0},{8,4},{12,8},{16,12},{20,16},{24,20},{28,24},{32,28},{36,32}... | collective-permute-start | bytes 245768 | tf_op jit(solution)/shard_map/ppermute | solution.py:21
  194.6 20.9 %all-to-all-start.4 = ((f32[4,16,21,256]{3,1,2,0:T(8,128)}), f32[4,16,21,256]{3,1,2,0:T(8,128)S(1)}, u32[]{:S(2)}, u32[]{:S(2)}) async-start(f32[4,16,21,256]{3,1,2,0:T(8,128)} %broadcast_in_dim.57), calls=%async_computation.4 | async-start | bytes 2752512 | tf_op jit(solution)/shard_map/all_to_all | solution.py:32
  222.1 3.6 %copy-start.1 = (f32[8,256,256]{2,1,0:T(8,128)}, f32[8,256,256]{2,1,0:T(8,128)S(1)}, u32[]{:S(2)}) copy-start(f32[8,256,256]{2,1,0:T(8,128)S(1)} %multiply_reduce_fusion.11) | copy-start | bytes 6291460 | tf_op jit(solution)/shard_map/while
  241.1 3.6 %copy-start.1 = (f32[8,256,256]{2,1,0:T(8,128)}, f32[8,256,256]{2,1,0:T(8,128)S(1)}, u32[]{:S(2)}) copy-start(f32[8,256,256]{2,1,0:T(8,128)S(1)} %multiply_reduce_fusion.11) | copy-start | bytes 6291460 | tf_op jit(solution)/shard_map/while
  260.0 3.6 %copy-start.1 = (f32[8,256,256]{2,1,0:T(8,128)}, f32[8,256,256]{2,1,0:T(8,128)S(1)}, u32[]{:S(2)}) copy-start(f32[8,256,256]{2,1,0:T(8,128)S(1)} %multiply_reduce_fusion.11) | copy-start | bytes 6291460 | tf_op jit(solution)/shard_map/while
  288.2 3.6 %copy-start.4 = (f32[16,2,8,256]{3,2,0,1:T(8,128)S(1)}, f32[16,2,8,256]{3,2,0,1:T(8,128)}, u32[]{:S(2)}) copy-start(f32[16,2,8,256]{3,2,0,1:T(8,128)} %copy-done.3) | copy-start | bytes 786436
  288.3 3.4 %collective-permute-start.4 = (f32[16,5,256]{2,0,1:T(8,128)S(1)}, f32[16,5,256]{2,0,1:T(8,128)S(1)}, u32[]{:S(2)}, u32[]{:S(2)}) collective-permute-start(f32[16,5,256]{2,0,1:T(8,128)S(1)} %slice.93), channel_id=1, source_target_pairs={{0,4},{4,8},{8,12},{12,16},{16,20},{20,24},{24,28},{28,32},{32,36}... | collective-permute-start | bytes 245768 | tf_op jit(solution)/shard_map/ppermute | solution.py:21
where the time goes:
time: 314 us; the launch traced here: 312 us
  local copies, waits for them, and re-layouts  91.4 us (29%)
  matrix products  66.1 us (21%)
  blocking collectives  48.5 us (15%)
  waiting for transfers between devices  46.7 us (15%)
  starting transfers between devices  42.3 us (13%)
  other arithmetic  14.9 us (5%)
    gather x2, local copies, waits for them, and re-layouts, body(): jnp.take_along_axis(coords.reshape(3, leaf_dev, width), site_order[None],...  46.6 us
    all_to_all x4, waiting for transfers between devices, sent_to_all(): return lax.all_to_all(copies, axis, split_axis=0, concat_axis=0, tiled=True)  35.8 us
    all_to_all x2, blocking collectives, sum_at_owner(): lax.all_to_all(parts, axis, split_axis=0, concat_axis=0, tiled=True)  29.5 us
    all_to_all x4, starting transfers between devices, sent_to_all(): return lax.all_to_all(copies, axis, split_axis=0, concat_axis=0, tiled=True)  28.8 us
    dot_general x6, matrix products, one_block(): jnp.einsum('bak,cba->cbk', tiles, jnp.take(values, rows, axis=1), precisi...  28.4 us
    dot_general x6, matrix products, one_block(): jnp.einsum('bak,cbk->cba', tiles, jnp.take(values, cols, axis=1), precisi...  21.4 us
    all_to_all x1, blocking collectives, sent_to_all(): return lax.all_to_all(copies, axis, split_axis=0, concat_axis=0, tiled=True)  19.1 us
    gather x6, local copies, waits for them, and re-layouts, one_block(): jnp.take(values, rows, axis=1)  16.3 us
  transfers between devices with their start and end apart: 9, of which 8 were waited for; matrix products, arithmetic and copies ran while one was open for 15% of the time, Pallas kernels for 0%

commit v1 on v0

v1 whole, which is shorter than its diff:
```python
import functools
import math

import jax
import jax.numpy as jnp
from jax import lax
from jax.experimental import pallas as pl
from jax.experimental.pallas import tpu as pltpu
from jax.sharding import PartitionSpec as P

REACH = 5
STEPS = REACH + 1
UNIT = 0.025
LENGTH = 0.12
NUGGET = 0.5
W = 256
TAPER = REACH * UNIT
DECAY = math.sqrt(3.0) * TAPER / LENGTH
LOG2E = math.log2(math.e)
CHUNK = 16
FLOOR_INV = 1e18


def split2(x):
    hi = x.astype(jnp.bfloat16)
    lo = (x - hi.astype(jnp.float32)).astype(jnp.bfloat16)
    return hi, lo


def split3(x):
    hi = x.astype(jnp.bfloat16)
    rest = x - hi.astype(jnp.float32)
    mid = rest.astype(jnp.bfloat16)
    lo = (rest - mid.astype(jnp.float32)).astype(jnp.bfloat16)
    return hi, mid, lo


def load_values(v_ref, src_ref, leaves, first):
    for k in range(leaves):
        hi, lo = split2(src_ref[:, k * W : (k + 1) * W])
        v_ref[first + k] = jnp.concatenate([hi, lo], axis=0)


def place_points(pts_ref, coords_ref, order_ref, leaves, first):
    sub = lax.broadcasted_iota(jnp.int32, (W, W), 0)
    for k in range(leaves):
        sel = (sub == order_ref[k : k + 1, :]).astype(jnp.float32).astype(jnp.bfloat16)
        hi, mid, lo = split3(coords_ref[:, k * W : (k + 1) * W])
        dot = functools.partial(jnp.dot, preferred_element_type=jnp.float32)
        got = dot(hi, sel) + dot(mid, sel) + dot(lo, sel)
        pts_ref[first + k, 0:3, :] = got * (1.0 / TAPER)


def spread_rows(bc_ref, pts_ref, leaf):
    cols = jnp.transpose(pts_ref[leaf])
    for c in range(3):
        bc_ref[c] = jnp.broadcast_to(cols[:, c : c + 1], (W, 128))


def make_tile(t_ref, bc_ref, other, scale):
    f0 = scale
    f1 = scale * (4.0 + DECAY)
    f2 = scale * (4.0 * DECAY)
    b = [jnp.broadcast_to(other[c : c + 1, :], (CHUNK, W)) for c in range(3)]
    for k in range(W // CHUNK):
        rows = slice(k * CHUNK, (k + 1) * CHUNK)
        u = None
        for c in range(3):
            a = bc_ref[c, rows, :]
            d = jnp.concatenate([a, a], axis=1) - b[c]
            u = d * d if u is None else u + d * d
        u = jnp.minimum(u, 1.0)
        q = u * jnp.minimum(lax.rsqrt(u), FLOOR_INV)
        t = 1.0 - q
        t = t * t
        t = t * t
        e = jnp.exp2(q * (-DECAY * LOG2E))
        x = (q * f1 + f0 + u * f2) * (t * e)
        hi, lo = split2(x)
        t_ref[rows, 0:W] = hi
        t_ref[rows, W : 2 * W] = lo


def use_tile(t_ref, v_ref, acc_ref, i, j):
    hi = t_ref[:, 0:W]
    lo = t_ref[:, W : 2 * W]
    dot = functools.partial(lax.dot_general, preferred_element_type=jnp.float32)
    nt = (((1,), (1,)), ((), ()))
    nn = (((1,), (0,)), ((), ()))
    n = acc_ref.shape[1]
    vj = v_ref[j]
    vi = v_ref[i]
    p = dot(vj, hi, nt)
    acc_ref[i] += p[:n] + p[n:] + dot(vj[:n], lo, nt)
    p = dot(vi, hi, nn)
    acc_ref[j] += p[:n] + p[n:] + dot(vi[:n], lo, nn)


def list_weights(flag_ref, pairs_ref, count_ref, base_ref, leaf_dev):
    def clear(s, _):
        flag_ref[s] = 0.0
        return 0

    lax.fori_loop(0, leaf_dev * STEPS, clear, 0)

    def put(s, _):
        row = pairs_ref[0, s] - base_ref[0]
        step = pairs_ref[1, s] - pairs_ref[0, s]
        flag_ref[row * STEPS + step] = jnp.where(step == 0, 0.5, 1.0)
        return 0

    lax.fori_loop(0, count_ref[0], put, 0)


def first_kernel(
    i0, i1, leaf_dev, with_prev, pairs_ref, count_ref, base_ref, coords_ref, order_ref, b_ref, *rest
):
    rest = list(rest)
    halo = i1 + REACH > leaf_dev
    if halo:
        hc_ref, ho_ref, hb_ref = rest[:3]
        rest = rest[3:]
    if with_prev:
        prev_ref = rest.pop(0)
    tiles_ref, acc_ref, flag_ref, pts_ref, bc_ref, v_ref = rest
    list_weights(flag_ref, pairs_ref, count_ref, base_ref, leaf_dev)
    load_values(v_ref, b_ref, leaf_dev, 0)
    place_points(pts_ref, coords_ref, order_ref, leaf_dev, 0)
    if halo:
        load_values(v_ref, hb_ref, REACH, leaf_dev)
        place_points(pts_ref, hc_ref, ho_ref, REACH, leaf_dev)
    if with_prev:
        acc_ref[...] = prev_ref[...]
    else:
        acc_ref[...] = jnp.zeros_like(acc_ref)

    def one_leaf(i, _):
        spread_rows(bc_ref, pts_ref, i)

        def one_step(d, _):
            j = i + d
            t_ref = tiles_ref.at[(i - i0) * STEPS + d]
            make_tile(t_ref, bc_ref, pts_ref[j], flag_ref[i * STEPS + d])
            use_tile(t_ref, v_ref, acc_ref, i, j)
            return 0

        return lax.fori_loop(0, STEPS, one_step, 0)

    lax.fori_loop(i0, i1, one_leaf, 0)


def second_kernel(i0, i1, leaf_dev, with_prev, tiles_ref, w_ref, *rest):
    rest = list(rest)
    halo = i1 + REACH > leaf_dev
    if halo:
        hw_ref = rest.pop(0)
    if with_prev:
        prev_ref = rest.pop(0)
    acc_ref, v_ref = rest
    load_values(v_ref, w_ref, leaf_dev, 0)
    if halo:
        load_values(v_ref, hw_ref, REACH, leaf_dev)
    if with_prev:
        acc_ref[...] = prev_ref[...]
    else:
        acc_ref[...] = jnp.zeros_like(acc_ref)

    def one_leaf(i, _):
        def one_step(d, _):
            use_tile(tiles_ref.at[(i - i0) * STEPS + d], v_ref, acc_ref, i, i + d)
            return 0

        return lax.fori_loop(0, STEPS, one_step, 0)

    lax.fori_loop(i0, i1, one_leaf, 0)


VM = pl.BlockSpec(memory_space=pltpu.VMEM)
SM = pl.BlockSpec(memory_space=pltpu.SMEM)


def first_call(i0, i1, leaf_dev, n, smem, own, halo, prev):
    extent = leaf_dev + REACH
    tiles = (i1 - i0) * STEPS
    ops = [*smem, *own, *halo, *([] if prev is None else [prev])]
    return pl.pallas_call(
        functools.partial(first_kernel, i0, i1, leaf_dev, prev is not None),
        out_shape=(
            jax.ShapeDtypeStruct((tiles, W, 2 * W), jnp.bfloat16),
            jax.ShapeDtypeStruct((extent, n, W), jnp.float32),
        ),
        in_specs=[SM] * len(smem) + [VM] * (len(ops) - len(smem)),
        out_specs=(VM, VM),
        scratch_shapes=[
            pltpu.SMEM((leaf_dev * STEPS,), jnp.float32),
            pltpu.VMEM((extent, 8, W), jnp.float32),
            pltpu.VMEM((3, W, 128), jnp.float32),
            pltpu.VMEM((extent, 2 * n, W), jnp.bfloat16),
        ],
        compiler_params=pltpu.CompilerParams(vmem_limit_bytes=40 << 20),
        cost_estimate=pl.CostEstimate(flops=tiles << 26, transcendentals=tiles << 17, bytes_accessed=tiles << 18),
        name=f"evaluate_{i0}",
    )(*ops)


def second_call(i0, i1, leaf_dev, n, tiles, own, halo, prev):
    extent = leaf_dev + REACH
    ops = [tiles, own, *halo, *([] if prev is None else [prev])]
    return pl.pallas_call(
        functools.partial(second_kernel, i0, i1, leaf_dev, prev is not None),
        out_shape=jax.ShapeDtypeStruct((extent, n, W), jnp.float32),
        in_specs=[VM] * len(ops),
        out_specs=VM,
        scratch_shapes=[pltpu.VMEM((extent, 2 * n, W), jnp.bfloat16)],
        compiler_params=pltpu.CompilerParams(vmem_limit_bytes=40 << 20),
        cost_estimate=pl.CostEstimate(flops=tiles.shape[0] << 26, transcendentals=0, bytes_accessed=tiles.size * 2),
        name=f"apply_{i0}",
    )(*ops)


def shift(value, by):
    length = lax.axis_size("leaf")
    return lax.ppermute(value, "leaf", [(i, i + by) for i in range(length) if 0 <= i + by < length])


def sum_over_leaf(value):
    length = lax.axis_size("leaf")
    value = value + lax.ppermute(value, "leaf", [(i, i ^ 1) for i in range(length)])
    copies = jnp.broadcast_to(value, (length // 2, *value.shape))
    groups = [[i for i in range(length) if i % 2 == c] for c in range(2)]
    got = lax.all_to_all(
        copies, "leaf", split_axis=0, concat_axis=0, tiled=True, axis_index_groups=groups
    )
    return jnp.sum(got, axis=0)


def to_rows(acc):
    return jnp.moveaxis(acc, 1, 0).reshape(acc.shape[1], -1)


def body(coords, site_order, leaf_pairs, pair_count, probes):
    leaf_dev, width = site_order.shape
    n = probes.shape[0]
    edge = REACH * width
    base = (lax.axis_index("leaf") * leaf_dev).astype(jnp.int32).reshape(1)
    packed = jnp.concatenate(
        [probes[:, :edge], coords[:, :edge], site_order[:REACH].reshape(1, edge).astype(jnp.float32)]
    )
    arrived = shift(packed, -1)
    halo = (arrived[n : n + 3], arrived[n + 3].reshape(REACH, width).astype(jnp.int32), arrived[:n])
    smem = (leaf_pairs, pair_count, base)
    own = (coords, site_order, probes)
    cut0, cut1 = leaf_dev // 2, leaf_dev - REACH

    def operator(run, far, field):
        t0, acc = run(0, cut0, (), None)
        t1, acc = run(cut1, leaf_dev, far, acc)
        back = shift(to_rows(acc[leaf_dev:]), 1)
        part_far = acc[leaf_dev:]
        t2, acc = run(cut0, cut1, (), acc)
        part_own = to_rows(acc[:leaf_dev])
        return (t0, t1, t2), part_own, part_far, back

    def run_first(i0, i1, far, prev):
        return first_call(i0, i1, leaf_dev, n, smem, own, far, prev)

    tiles, part, _, back = operator(run_first, halo, probes)
    image = NUGGET * probes + part
    image = jnp.concatenate([image[:, :edge] + back, image[:, edge:]], axis=1)
    image_far = shift(image[:, :edge], -1)
    by_start = {0: tiles[0], cut1: tiles[1], cut0: tiles[2]}

    def run_second(i0, i1, far, prev):
        return None, second_call(i0, i1, leaf_dev, n, by_start[i0], image, far, prev)

    _, part2, part2_far, back2 = operator(run_second, (image_far,), image)
    image2_here = NUGGET * image + part2
    far_dot = jnp.sum(jnp.moveaxis(part2_far, 1, 0) * image_far.reshape(n, REACH, width), axis=(1, 2))
    sums = jnp.stack(
        [
            jnp.sum(probes * probes, axis=1),
            jnp.sum(probes * image, axis=1),
            jnp.sum(image * image, axis=1),
            jnp.sum(image * image2_here, axis=1) + far_dot,
        ]
    )
    rr, bw, ww, wz = sum_over_leaf(sums)
    image2 = jnp.concatenate([image2_here[:, :edge] + back2, image2_here[:, edge:]], axis=1)
    alpha = rr / bw
    rr1 = rr - 2.0 * alpha * bw + alpha * alpha * ww
    beta = rr1 / rr
    g = 1.0 + beta
    curve = g * g * bw - 2.0 * g * alpha * ww + alpha * alpha * wz
    alpha1 = rr1 / curve
    c = lambda x: x[:, None]
    direction1 = c(g) * probes - c(alpha) * image
    image1 = c(g) * image - c(alpha) * image2
    solution = c(alpha) * probes + c(alpha1) * direction1
    residual = probes - c(alpha) * image - c(alpha1) * image1
    return solution, residual


def solution(mesh):
    in_specs = (P(None, "leaf"), P("leaf", None), P(None, "leaf"), P("leaf"), P("probe", "leaf"))
    out_specs = (P("probe", "leaf"), P("probe", "leaf"))
    return jax.shard_map(body, mesh=mesh, in_specs=in_specs, out_specs=out_specs, check_vma=False)
```

time: 314 us -> 133 us (0.42)
  Pallas kernels: 0 us -> 77.8 us
  local copies, waits for them, and re-layouts: 91.4 us -> 17.1 us
  matrix products: 66.1 us -> 0 us
  blocking collectives: 48.5 us -> 0 us
  waiting for transfers between devices: 46.7 us -> 7.6 us
  starting transfers between devices: 42.3 us -> 25.7 us
  other arithmetic: 14.9 us -> 2.49 us
    gather x26 -> x0, local copies, waits for them, and re-layouts: 81.3 us -> none  [the longest x2 46.6 us: body(): jnp.take_along_axis(coords.reshape(3, leaf_dev, width), site_order[None],...]
    pallas_call x0 -> x6, Pallas kernels: none -> 77.8 us  [the longest x3 53.3 us: first_call(): pl.pallas_call(functools.partial(first_kernel, i0, i1, leaf_dev, prev is...]
    dot_general x24 -> x0, matrix products: 66.1 us -> none  [the longest x6 28.4 us: one_block(): jnp.einsum('bak,cba->cbk', tiles, jnp.take(values, rows, axis=1), precisi...]
    all_to_all x3 -> x0, blocking collectives: 48.5 us -> none  [the longest x2 29.5 us: sum_at_owner(): lax.all_to_all(parts, axis, split_axis=0, concat_axis=0, tiled=True)]
    all_to_all x4 -> x1, waiting for transfers between devices: 35.8 us -> 5.04 us  [sum_over_leaf(): lax.all_to_all(copies, 'leaf', split_axis=0, concat_axis=0, tiled=True, a...]
    all_to_all x4 -> x1, starting transfers between devices: 28.8 us -> 12.2 us  [sum_over_leaf(): lax.all_to_all(copies, 'leaf', split_axis=0, concat_axis=0, tiled=True, a...]
    unnamed x17 -> x31, local copies, waits for them, and re-layouts: 2.41 us -> 14.7 us
    ppermute x5, waiting for transfers between devices: 10.9 us -> 2.56 us  [the longest x4 1.42 us: shift(): lax.ppermute(value, 'leaf', [(i, i + by) for i in range(length) if 0 <= i...]
  transfers between devices with their start and end apart: 9 -> 6, of which waited for: 8 -> 4; matrix products, arithmetic and copies ran while one was open for 15% -> 0% of each run, Pallas kernels for 0% -> 28%
where the time goes in v1:
time: 133 us; the launch traced here: 132 us
  Pallas kernels  77.8 us (58%)
  starting transfers between devices  25.7 us (19%)
  local copies, waits for them, and re-layouts  17.1 us (13%)
  waiting for transfers between devices  7.6 us (6%)
  other arithmetic  2.49 us (2%)
  between operations  1.63 us (1%)
    pallas_call x3, Pallas kernels, first_call(): pl.pallas_call(functools.partial(first_kernel, i0, i1, leaf_dev, prev is...  53.3 us
    pallas_call x3, Pallas kernels, second_call(): pl.pallas_call(functools.partial(second_kernel, i0, i1, leaf_dev, prev is...  24.4 us
    unnamed x31, local copies, waits for them, and re-layouts  14.7 us
    ppermute x4, starting transfers between devices, shift(): lax.ppermute(value, 'leaf', [(i, i + by) for i in range(length) if 0 <= i...  13.4 us
    all_to_all x1, starting transfers between devices, sum_over_leaf(): lax.all_to_all(copies, 'leaf', split_axis=0, concat_axis=0, tiled=True, a...  12.2 us
    all_to_all x1, waiting for transfers between devices, sum_over_leaf(): lax.all_to_all(copies, 'leaf', split_axis=0, concat_axis=0, tiled=True, a...  5.04 us
  transfers between devices with their start and end apart: 6, of which 4 were waited for; matrix products, arithmetic and copies ran while one was open for 0% of the time, Pallas kernels for 28%

profile of v1, /device:TPU:1, one launch (start us, length us, event | category | flops | bytes accessed | tf_op | source)
XLA Modules:
  0.0 132.3 jit_solution(9033944048503955186)
XLA Ops:
  0.7 0.7 convert_bitcast_fusion
  1.4 0.7 slice.44
  2.2 0.9 slice.43
  3.1 5.1 %collective-permute-start = (f32[20,1280]{1,0:T(8,128)S(1)}, f32[20,1280]{1,0:T(8,128)S(1)}, u32[]{:S(2)}, u32[]{:S(2)}) collective-permute-start(f32[20,1280]{1,0:T(8,128)S(1)} %pad_maximum_fusion.1), channel_id=1, source_target_pairs={{4,0},{8,4},{12,8},{16,12},{20,16},{24,20},{28,24},{32,28},{36,32}... | collective-permute-start | bytes 307208 | tf_op jit(solution)/shard_map/ppermute | solution.py:223
  8.9 0.9 copy-done.3
  9.8 0.8 copy-done.5
  10.7 0.7 copy-done.7
  11.4 0.7 copy-done.9
  12.1 25.3 %evaluate_0.1 = (bf16[48,256,512]{2,1,0:T(8,128)(2,1)S(1)}, f32[21,16,256]{2,1,0:T(8,128)S(1)}) custom-call(s32[2,96]{1,0:T(2,128)S(1)} %copy-done.9, s32[1]{0:T(128)S(6)} %copy.50.count_ref, s32[1]{0:T(128)} %bitcast.1.base_ref, f32[3,4096]{1,0:T(4,128)S(1)} %copy-done.5, s32[16,256]{1,0:T(8,128)S(1)} %copy-done.7, f32[16,4096]{1,0:T(8,128)S(1)} %copy-done.3), custom_call_target="tpu_custom_call" | custom-call | flops 3221225472 | bytes 12582912 | tf_op jit(solution)/shard_map/evaluate_0/pallas_call | solution.py:186
  37.4 4.6 %copy-done = bf16[48,256,512]{2,1,0:T(8,128)(2,1)} copy-done((bf16[48,256,512]{2,1,0:T(8,128)(2,1)}, bf16[48,256,512]{2,1,0:T(8,128)(2,1)S(1)}, u32[]{:S(2)}) %copy-start) | copy-done | bytes 12582936
  42.1 17.0 %evaluate_11.1 = (bf16[30,256,512]{2,1,0:T(8,128)(2,1)S(1)}, f32[21,16,256]{2,1,0:T(8,128)S(1)}) custom-call(s32[2,96]{1,0:T(2,128)S(1)} %copy-done.10, s32[1]{0:T(128)S(6)} %copy.50.count_ref, s32[1]{0:T(128)} %bitcast.1.base_ref, f32[3,4096]{1,0:T(4,128)S(1)} %copy-done.6, s32[16,256]{1,0:T(8,128)S(1)} %copy-done.8, f32[16,4096]{1,0:T(8,128)S(1)} %copy-done.4, ...), custom_call_target="tpu_custom_call" | custom-call | flops 2013265920 | bytes 7864320 | tf_op jit(solution)/shard_map/evaluate_11/pallas_call | solution.py:186
  59.1 0.1 slice_bitcast_fusion.2
  59.1 11.1 %evaluate_8.1 = (bf16[18,256,512]{2,1,0:T(8,128)(2,1)S(1)}, f32[21,16,256]{2,1,0:T(8,128)S(1)}) custom-call(s32[2,96]{1,0:T(2,128)S(1)} %copy-done.10, s32[1]{0:T(128)S(6)} %copy.50.count_ref, s32[1]{0:T(128)} %bitcast.1.base_ref, f32[3,4096]{1,0:T(4,128)S(1)} %copy-done.6, s32[16,256]{1,0:T(8,128)S(1)} %copy-done.8, f32[16,4096]{1,0:T(8,128)S(1)} %copy-done.4, ...), custom_call_target="tpu_custom_call" | custom-call | flops 1207959552 | bytes 4718592 | tf_op jit(solution)/shard_map/evaluate_8/pallas_call | solution.py:186
  70.2 2.1 %copy-done.2 = bf16[18,256,512]{2,1,0:T(8,128)(2,1)} copy-done((bf16[18,256,512]{2,1,0:T(8,128)(2,1)}, bf16[18,256,512]{2,1,0:T(8,128)(2,1)S(1)}, u32[]{:S(2)}) %copy-start.2) | copy-done | bytes 4718616
  72.4 2.6 %collective-permute-start.1 = (f32[16,1280]{1,0:T(8,128)S(1)}, f32[16,1280]{1,0:T(8,128)S(1)}, u32[]{:S(2)}, u32[]{:S(2)}) collective-permute-start(f32[16,1280]{1,0:T(8,128)S(1)} %bitcast.84), channel_id=1, source_target_pairs={{0,4},{4,8},{8,12},{12,16},{16,20},{20,24},{24,28},{28,32},{32,36}... | collective-permute-start | bytes 245768 | tf_op jit(solution)/shard_map/ppermute | solution.py:223
  75.1 1.4 %collective-permute-done.1 = f32[16,1280]{1,0:T(8,128)S(1)} collective-permute-done((f32[16,1280]{1,0:T(8,128)S(1)}, f32[16,1280]{1,0:T(8,128)S(1)}, u32[]{:S(2)}, u32[]{:S(2)}) %collective-permute-start.1) | collective-permute-done | bytes 81952 | tf_op jit(solution)/shard_map/ppermute | solution.py:223
  76.5 1.9 %collective-permute-start.2 = (f32[16,1280]{1,0:T(8,128)S(1)}, f32[16,1280]{1,0:T(8,128)S(1)}, u32[]{:S(2)}, u32[]{:S(2)}) collective-permute-start(f32[16,1280]{1,0:T(8,128)S(1)} %slice_add_fusion.1), channel_id=1, source_target_pairs={{4,0},{8,4},{12,8},{16,12},{20,16},{24,20},{28,24},{32,28},{36,32}... | collective-permute-start | bytes 245768 | tf_op jit(solution)/shard_map/ppermute | solution.py:223
  78.4 4.6 %copy-done.1 = bf16[48,256,512]{2,1,0:T(8,128)(2,1)S(1)} copy-done((bf16[48,256,512]{2,1,0:T(8,128)(2,1)S(1)}, bf16[48,256,512]{2,1,0:T(8,128)(2,1)}, u32[]{:S(2)}) %copy-start.1) | copy-done | bytes 12582936
  83.0 12.2 %apply_0.1.rest_1_ = f32[21,16,256]{2,1,0:T(8,128)S(1)} custom-call(bf16[48,256,512]{2,1,0:T(8,128)(2,1)S(1)} %copy-done.1, f32[16,4096]{1,0:T(8,128)S(1)} %pad_maximum_fusion.w_ref), custom_call_target="tpu_custom_call" | custom-call | flops 3221225472 | bytes 12582912 | tf_op jit(solution)/shard_map/apply_0/pallas_call | solution.py:209
  95.2 0.1 collective-permute-done.2.rest_0_
  95.3 7.6 %apply_11.1.rest_0_ = f32[21,16,256]{2,1,0:T(8,128)S(1)} custom-call(bf16[30,256,512]{2,1,0:T(8,128)(2,1)S(1)} %get-tuple-element.12.tiles_ref, f32[16,4096]{1,0:T(8,128)S(1)} %pad_maximum_fusion.w_ref, f32[16,1280]{1,0:T(8,128)S(1)} %collective-permute-done.2.rest_0_, f32[21,16,256]{2,1,0:T(8,128)S(1)} %apply_0.1.rest_1_), custom_call_target="tpu_custom_call" | custom-call | flops 2013265920 | bytes 7864320 | tf_op jit(solution)/shard_map/apply_11/pallas_call | solution.py:209
  103.0 4.6 %apply_8.1 = f32[21,16,256]{2,1,0:T(8,128)S(1)} custom-call(bf16[18,256,512]{2,1,0:T(8,128)(2,1)S(1)} %bitcast.79, f32[16,4096]{1,0:T(8,128)S(1)} %pad_maximum_fusion.w_ref, f32[21,16,256]{2,1,0:T(8,128)S(1)} %apply_11.1.rest_0_), custom_call_target="tpu_custom_call" | custom-call | flops 1207959552 | bytes 4718592 | tf_op jit(solution)/shard_map/apply_8/pallas_call | solution.py:209
  107.6 0.2 fusion.5
  107.8 0.2 fusion
  108.0 0.2 multiply_reduce_fusion.2
  108.3 0.1 collective-permute-start.3
  108.4 1.1 collective-permute-done.3
  109.5 0.6 broadcast_in_dim.2
  110.2 12.2 %all-to-all-start = ((f32[32,4,16]{2,1,0:T(4,128)}), f32[32,4,16]{2,1,0:T(4,128)S(1)}, u32[]{:S(2)}, u32[]{:S(2)}) async-start(f32[32,4,16]{2,1,0:T(4,128)} %broadcast_in_dim.2), calls=%async_computation | async-start | bytes 131072 | tf_op jit(solution)/shard_map/all_to_all | solution.py:231
  122.4 3.8 %collective-permute-start.4 = (f32[16,1280]{1,0:T(8,128)S(1)}, f32[16,1280]{1,0:T(8,128)S(1)}, u32[]{:S(2)}, u32[]{:S(2)}) collective-permute-start(f32[16,1280]{1,0:T(8,128)S(1)} %bitcast.83), channel_id=1, source_target_pairs={{0,4},{4,8},{8,12},{12,16},{16,20},{20,24},{24,28},{28,32},{32,36}... | collective-permute-start | bytes 245768 | tf_op jit(solution)/shard_map/ppermute | solution.py:223
  126.2 5.0 %all-to-all-done = f32[32,4,16]{2,1,0:T(4,128)S(1)} async-done(((f32[32,4,16]{2,1,0:T(4,128)}), f32[32,4,16]{2,1,0:T(4,128)S(1)}, u32[]{:S(2)}, u32[]{:S(2)}) %all-to-all-start) | async-done | bytes 8224 | tf_op jit(solution)/shard_map/all_to_all | solution.py:231
  131.3 1.0 fusion.4
  (47 shorter events, 0.6 us)
Async XLA Ops:
  0.6 41.4 %copy-start.8 = (s32[16,256]{1,0:T(8,128)S(1)}, s32[16,256]{1,0:T(8,128)}, u32[]{:S(2)}) copy-start(s32[16,256]{1,0:T(8,128)} %order_ref.5) | copy-start | bytes 49156
  0.6 41.4 %copy-start.6 = (f32[3,4096]{1,0:T(4,128)S(1)}, f32[3,4096]{1,0:T(4,128)}, u32[]{:S(2)}) copy-start(f32[3,4096]{1,0:T(4,128)} %coords_ref.5) | copy-start | bytes 147460
  0.7 41.4 %copy-start.4 = (f32[16,4096]{1,0:T(8,128)S(1)}, f32[16,4096]{1,0:T(8,128)}, u32[]{:S(2)}) copy-start(f32[16,4096]{1,0:T(8,128)} %b_ref.5) | copy-start | bytes 786436
  0.7 41.4 %copy-start.10 = (s32[2,96]{1,0:T(2,128)S(1)}, s32[2,96]{1,0:T(2,128)}, u32[]{:S(2)}) copy-start(s32[2,96]{1,0:T(2,128)} %pairs_ref.5) | copy-start | bytes 2308
  3.1 38.9 %collective-permute-start = (f32[20,1280]{1,0:T(8,128)S(1)}, f32[20,1280]{1,0:T(8,128)S(1)}, u32[]{:S(2)}, u32[]{:S(2)}) collective-permute-start(f32[20,1280]{1,0:T(8,128)S(1)} %pad_maximum_fusion.1), channel_id=1, source_target_pairs={{4,0},{8,4},{12,8},{16,12},{20,16},{24,20},{28,24},{32,28},{36,32}... | collective-permute-start | bytes 307208 | tf_op jit(solution)/shard_map/ppermute | solution.py:223
  8.9 1.0 copy-start.3
  9.8 0.8 copy-start.5
  10.7 0.7 copy-start.7
  11.4 0.7 copy-start.9
  37.3 4.6 %copy-start = (bf16[48,256,512]{2,1,0:T(8,128)(2,1)}, bf16[48,256,512]{2,1,0:T(8,128)(2,1)S(1)}, u32[]{:S(2)}) copy-start(bf16[48,256,512]{2,1,0:T(8,128)(2,1)S(1)} %get-tuple-element.13.tiles_ref) | copy-start | bytes 37748740
  70.2 2.2 %copy-start.2 = (bf16[18,256,512]{2,1,0:T(8,128)(2,1)}, bf16[18,256,512]{2,1,0:T(8,128)(2,1)S(1)}, u32[]{:S(2)}) copy-start(bf16[18,256,512]{2,1,0:T(8,128)(2,1)S(1)} %get-tuple-element.11.tiles_ref) | copy-start | bytes 14155780
  72.4 4.1 %collective-permute-start.1 = (f32[16,1280]{1,0:T(8,128)S(1)}, f32[16,1280]{1,0:T(8,128)S(1)}, u32[]{:S(2)}, u32[]{:S(2)}) collective-permute-start(f32[16,1280]{1,0:T(8,128)S(1)} %bitcast.84), channel_id=1, source_target_pairs={{0,4},{4,8},{8,12},{12,16},{16,20},{20,24},{24,28},{28,32},{32,36}... | collective-permute-start | bytes 245768 | tf_op jit(solution)/shard_map/ppermute | solution.py:223
  76.5 18.8 %collective-permute-start.2 = (f32[16,1280]{1,0:T(8,128)S(1)}, f32[16,1280]{1,0:T(8,128)S(1)}, u32[]{:S(2)}, u32[]{:S(2)}) collective-permute-start(f32[16,1280]{1,0:T(8,128)S(1)} %slice_add_fusion.1), channel_id=1, source_target_pairs={{4,0},{8,4},{12,8},{16,12},{20,16},{24,20},{28,24},{32,28},{36,32}... | collective-permute-start | bytes 245768 | tf_op jit(solution)/shard_map/ppermute | solution.py:223
  78.4 4.6 %copy-start.1 = (bf16[48,256,512]{2,1,0:T(8,128)(2,1)S(1)}, bf16[48,256,512]{2,1,0:T(8,128)(2,1)}, u32[]{:S(2)}) copy-start(bf16[48,256,512]{2,1,0:T(8,128)(2,1)} %copy-done) | copy-start | bytes 37748740
  95.2 7.7 %slice-start = ((s8[4718592]{0:T(1024)(128)(4,1)}), s8[4194304]{0:T(1024)(128)(4,1)S(1)}, s32[]{:S(2)}) async-start(s8[4718592]{0:T(1024)(128)(4,1)} %bitcast.78), calls=%async_computation.1 | async-start | bytes 8388608
  95.3 7.7 %slice-start.1 = ((s8[4718592]{0:T(1024)(128)(4,1)}), s8[524288]{0:T(1024)(128)(4,1)S(1)}, s32[]{:S(2)}) async-start(s8[4718592]{0:T(1024)(128)(4,1)} %bitcast.78), calls=%async_computation.2 | async-start | bytes 1048576
  108.3 1.2 collective-permute-start.3
  110.2 21.0 %all-to-all-start = ((f32[32,4,16]{2,1,0:T(4,128)}), f32[32,4,16]{2,1,0:T(4,128)S(1)}, u32[]{:S(2)}, u32[]{:S(2)}) async-start(f32[32,4,16]{2,1,0:T(4,128)} %broadcast_in_dim.2), calls=%async_computation | async-start | bytes 131072 | tf_op jit(solution)/shard_map/all_to_all | solution.py:231
  122.4 8.9 %collective-permute-start.4 = (f32[16,1280]{1,0:T(8,128)S(1)}, f32[16,1280]{1,0:T(8,128)S(1)}, u32[]{:S(2)}, u32[]{:S(2)}) collective-permute-start(f32[16,1280]{1,0:T(8,128)S(1)} %bitcast.83), channel_id=1, source_target_pairs={{0,4},{4,8},{8,12},{12,16},{16,20},{20,24},{24,28},{28,32},{32,36}... | collective-permute-start | bytes 245768 | tf_op jit(solution)/shard_map/ppermute | solution.py:223

commit v2 on v1

v2 whole, which is shorter than its diff:
```python
import functools
import math

import jax
import jax.numpy as jnp
from jax import lax
from jax.experimental import pallas as pl
from jax.experimental.pallas import tpu as pltpu
from jax.sharding import PartitionSpec as P

REACH = 5
STEPS = REACH + 1
UNIT = 0.025
LENGTH = 0.12
NUGGET = 0.5
W = 256
TAPER = REACH * UNIT
DECAY = math.sqrt(3.0) * TAPER / LENGTH
LOG2E = math.log2(math.e)
CHUNK = 16
HALF = W // 2
FLOOR_INV = 1e18


def split2(x):
    hi = x.astype(jnp.bfloat16)
    lo = (x - hi.astype(jnp.float32)).astype(jnp.bfloat16)
    return hi, lo


def split3(x):
    hi = x.astype(jnp.bfloat16)
    rest = x - hi.astype(jnp.float32)
    mid = rest.astype(jnp.bfloat16)
    lo = (rest - mid.astype(jnp.float32)).astype(jnp.bfloat16)
    return hi, mid, lo


def load_values(v_ref, src_ref, leaves, first):
    n = v_ref.shape[1] // 2
    for k in range(leaves):
        hi, lo = split2(src_ref[0:n, k * W : (k + 1) * W])
        v_ref[first + k] = jnp.concatenate([hi, lo], axis=0)


def prepare_kernel(
    pairs_ref, count_ref, base_ref, coords_hbm, order_hbm, b_hbm,
    listed_ref, pts_ref, cols_ref, v_ref, edge_ref, coords_ref, order_ref, b_ref, sems,
):
    copies = [
        pltpu.make_async_copy(coords_hbm, coords_ref, sems.at[0]),
        pltpu.make_async_copy(order_hbm, order_ref, sems.at[1]),
        pltpu.make_async_copy(b_hbm, b_ref, sems.at[2]),
    ]
    for copy in copies:
        copy.start()
    slots = pairs_ref.shape[1]
    row = pairs_ref[0:1, :]
    place = (row - base_ref[0]) * STEPS + pairs_ref[1:2, :] - row
    live = lax.broadcasted_iota(jnp.int32, (1, slots), 1) < count_ref[0]
    place = jnp.where(live, place, -1)
    hit = lax.broadcasted_iota(jnp.int32, (slots, slots), 0) == place
    found = jnp.sum(hit.astype(jnp.float32), axis=1, keepdims=True)
    listed_ref[...] = jnp.broadcast_to(found, (slots, HALF))
    for copy in copies:
        copy.wait()
    leaves = order_ref.shape[0]
    n = b_ref.shape[0]
    sub = lax.broadcasted_iota(jnp.int32, (W, W), 0)
    dot = functools.partial(jnp.dot, preferred_element_type=jnp.float32)
    for k in range(leaves):
        at = slice(k * W, (k + 1) * W)
        sel = (sub == order_ref[k : k + 1, :]).astype(jnp.float32).astype(jnp.bfloat16)
        hi, mid, lo = split3(coords_ref[:, at] * (1.0 / TAPER))
        zero = jnp.zeros((5, W), jnp.float32)
        parts = [dot(p, sel) for p in (hi, mid, lo)]
        got = parts[0] + parts[1] + parts[2]
        pts_ref[k, 0:3, :] = got
        stack = jnp.concatenate([z for p in parts for z in (p, zero)], axis=0)
        cols_ref[k] = jnp.transpose(stack).astype(jnp.bfloat16)
        if k < REACH:
            edge_ref[0:n, at] = b_ref[:, at]
            edge_ref[n : n + 3, at] = got
    load_values(v_ref, b_ref, leaves, 0)


def spread_rows(bc_ref, cols):
    r = lax.broadcasted_iota(jnp.int32, (24, 3 * HALF), 0)
    c = lax.broadcasted_iota(jnp.int32, (24, 3 * HALF), 1)
    sel = ((r & 7) == (c >> 7)).astype(jnp.float32).astype(jnp.bfloat16)
    bc_ref[...] = jnp.dot(cols, sel, preferred_element_type=jnp.float32)


def make_tile(t_ref, bc_ref, other, listed, same):
    f0 = jnp.broadcast_to(listed, (CHUNK, HALF))
    coef = {}
    for weight in (0.5, 1.0) if same else (1.0,):
        f = f0 * weight if weight != 1.0 else f0
        coef[weight] = (f, f * (4.0 + DECAY), f * (4.0 * DECAY))
    b = [
        [jnp.broadcast_to(other[c : c + 1, h * HALF : (h + 1) * HALF], (CHUNK, HALF)) for c in range(3)]
        for h in range(2)
    ]
    for k in range(W // CHUNK):
        rows = slice(k * CHUNK, (k + 1) * CHUNK)
        lower = k * CHUNK >= HALF
        for h in range(2):
            at = slice(h * HALF, (h + 1) * HALF)
            at_lo = slice(W + h * HALF, W + (h + 1) * HALF)
            if same and lower and h == 0:
                t_ref[rows, at] = jnp.zeros((CHUNK, HALF), jnp.bfloat16)
                t_ref[rows, at_lo] = jnp.zeros((CHUNK, HALF), jnp.bfloat16)
                continue
            g0, g1, g2 = coef[0.5 if same and lower == bool(h) else 1.0]
            u = None
            for c in range(3):
                d = bc_ref[rows, c * HALF : (c + 1) * HALF] - b[h][c]
                u = d * d if u is None else u + d * d
            u = jnp.minimum(u, 1.0)
            q = u * jnp.minimum(lax.rsqrt(u), FLOOR_INV)
            t = 1.0 - q
            t = t * t
            t = t * t
            e = jnp.exp2(q * (-DECAY * LOG2E))
            x = (q * g1 + g0 + u * g2) * (t * e)
            hi, lo = split2(x)
            t_ref[rows, at] = hi
            t_ref[rows, at_lo] = lo


def products(t_ref, vi, vj):
    hi = t_ref[:, 0:W]
    lo = t_ref[:, W : 2 * W]
    dot = functools.partial(lax.dot_general, preferred_element_type=jnp.float32)
    nt = (((1,), (1,)), ((), ()))
    nn = (((1,), (0,)), ((), ()))
    n = vi.shape[0] // 2
    p = dot(vj, hi, nt)
    to_row = p[:n] + p[n:] + dot(vj[:n], lo, nt)
    p = dot(vi, hi, nn)
    to_col = p[:n] + p[n:] + dot(vi[:n], lo, nn)
    return to_row, to_col


def evaluate_kernel(i0, i1, leaf_dev, listed_ref, pts_ref, cols_ref, v_ref, *rest):
    rest = list(rest)
    shift_by = 0
    if i1 + REACH > leaf_dev:
        edge_ref = rest.pop(0)
        prev_ref = rest.pop(0)
        tiles_ref, acc_ref, bc_ref, pts_all, v_all = rest
        n = v_ref.shape[1] // 2
        own = leaf_dev - i0
        pts_all[0:own] = pts_ref[i0:leaf_dev]
        v_all[0:own] = v_ref[i0:leaf_dev]
        for k in range(REACH):
            pts_all[own + k, 0:3, :] = edge_ref[n : n + 3, k * W : (k + 1) * W]
        load_values(v_all, edge_ref, REACH, own)
        pts_ref, v_ref = pts_all, v_all
        shift_by = i0
    else:
        if i0:
            prev_ref = rest.pop(0)
        tiles_ref, acc_ref, bc_ref = rest
    if i0:
        acc_ref[...] = prev_ref[...]
    else:
        acc_ref[...] = jnp.zeros_like(acc_ref)
    tiles_ref[0] = jnp.zeros_like(tiles_ref[0])

    def last_of(i):
        to_row, to_col = products(tiles_ref.at[(i - i0) * STEPS], v_ref[i - 1 - shift_by], v_ref[i - 1 + REACH - shift_by])
        acc_ref[i - 1] += to_row
        acc_ref[i - 1 + REACH] += to_col

    def one_leaf(i, _):
        slot = (i - i0) * STEPS
        spread_rows(bc_ref, cols_ref[i])
        vi = v_ref[i - shift_by]

        def make(d):
            j = i + d - shift_by
            listed = listed_ref[pl.ds(i * STEPS + d, 1), :]
            make_tile(tiles_ref.at[slot + (1 + d)], bc_ref, pts_ref.at[j], listed, d == 0)

        make(0)
        before = jnp.maximum(i - 1, i0)
        to_row, to_col = products(
            tiles_ref.at[slot], v_ref[before - shift_by], v_ref[before + REACH - shift_by]
        )
        acc_ref[before] += to_row
        acc_ref[before + REACH] += to_col
        total = None
        for d in range(REACH):
            make(d + 1)
            to_row, to_col = products(tiles_ref.at[slot + (1 + d)], vi, v_ref[i + d - shift_by])
            total = to_row if total is None else total + to_row
            acc_ref[i + d] += to_col
        acc_ref[i] += total
        return 0

    lax.fori_loop(i0, i1, one_leaf, 0)
    last_of(i1)


def apply_kernel(i0, i1, leaf_dev, tiles_ref, w_ref, *rest):
    rest = list(rest)
    if i1 + REACH > leaf_dev:
        far_ref = rest.pop(0)
    if i0:
        prev_ref = rest.pop(0)
    acc_ref, v_ref = rest
    load_values(v_ref, w_ref, leaf_dev, 0)
    if i1 + REACH > leaf_dev:
        load_values(v_ref, far_ref, REACH, leaf_dev)
    if i0:
        acc_ref[...] = prev_ref[...]
    else:
        acc_ref[...] = jnp.zeros_like(acc_ref)

    def one_leaf(i, _):
        slot = (i - i0) * STEPS
        vi = v_ref[i]
        total = None
        for d in range(STEPS):
            to_row, to_col = products(tiles_ref.at[slot + (1 + d)], vi, v_ref[i + d])
            total = to_row if total is None else total + to_row
            acc_ref[i + d] += to_col
        acc_ref[i] += total
        return 0

    lax.fori_loop(i0, i1, one_leaf, 0)


VM = pl.BlockSpec(memory_space=pltpu.VMEM)
SM = pl.BlockSpec(memory_space=pltpu.SMEM)
ANY = pl.BlockSpec(memory_space=pl.ANY)
PARAMS = pltpu.CompilerParams(vmem_limit_bytes=8 << 20)


def prepare_call(pairs, count, base, coords, order, b):
    leaves = order.shape[0]
    n = b.shape[0]
    return pl.pallas_call(
        prepare_kernel,
        out_shape=(
            jax.ShapeDtypeStruct((pairs.shape[1], HALF), jnp.float32),
            jax.ShapeDtypeStruct((leaves, 8, W), jnp.float32),
            jax.ShapeDtypeStruct((leaves, W, 24), jnp.bfloat16),
            jax.ShapeDtypeStruct((leaves, 2 * n, W), jnp.bfloat16),
            jax.ShapeDtypeStruct((n + 3, REACH * W), jnp.float32),
        ),
        in_specs=[VM, SM, SM, ANY, ANY, ANY],
        out_specs=(VM,) * 5,
        scratch_shapes=[
            pltpu.VMEM(coords.shape, jnp.float32),
            pltpu.VMEM(order.shape, jnp.int32),
            pltpu.VMEM(b.shape, jnp.float32),
            pltpu.SemaphoreType.DMA((3,)),
        ],
        compiler_params=PARAMS,
        name="prepare",
    )(pairs, count, base, coords, order, b)


def evaluate_call(i0, i1, leaf_dev, n, prepared, far, prev):
    extent = leaf_dev + REACH
    tiles = (i1 - i0) * STEPS
    ops = [*prepared, *far, *([] if prev is None else [prev])]
    scratch = [pltpu.VMEM((W, 3 * HALF), jnp.float32)]
    if far:
        held = leaf_dev - i0 + REACH
        scratch += [pltpu.VMEM((held, 8, W), jnp.float32), pltpu.VMEM((held, 2 * n, W), jnp.bfloat16)]
    return pl.pallas_call(
        functools.partial(evaluate_kernel, i0, i1, leaf_dev),
        out_shape=(
            jax.ShapeDtypeStruct((tiles + 1, W, 2 * W), jnp.bfloat16),
            jax.ShapeDtypeStruct((extent, n, W), jnp.float32),
        ),
        in_specs=[VM] * len(ops),
        out_specs=(VM, VM),
        scratch_shapes=scratch,
        compiler_params=PARAMS,
        cost_estimate=pl.CostEstimate(flops=tiles << 28, transcendentals=tiles << 17, bytes_accessed=tiles << 18),
        name=f"evaluate_{i0}",
    )(*ops)


def apply_call(i0, i1, leaf_dev, n, tiles, own, far, prev):
    extent = leaf_dev + REACH
    ops = [tiles, own, *far, *([] if prev is None else [prev])]
    return pl.pallas_call(
        functools.partial(apply_kernel, i0, i1, leaf_dev),
        out_shape=jax.ShapeDtypeStruct((extent, n, W), jnp.float32),
        in_specs=[VM] * len(ops),
        out_specs=VM,
        scratch_shapes=[pltpu.VMEM((extent, 2 * n, W), jnp.bfloat16)],
        compiler_params=PARAMS,
        cost_estimate=pl.CostEstimate(flops=tiles.shape[0] << 27, transcendentals=0, bytes_accessed=tiles.size * 2),
        name=f"apply_{i0}",
    )(*ops)


def shift(value, by):
    length = lax.axis_size("leaf")
    return lax.ppermute(value, "leaf", [(i, i + by) for i in range(length) if 0 <= i + by < length])


def sum_over_leaf(value):
    length = lax.axis_size("leaf")
    value = value + lax.ppermute(value, "leaf", [(i, i ^ 1) for i in range(length)])
    copies = jnp.broadcast_to(value, (length // 2, *value.shape))
    groups = [[i for i in range(length) if i % 2 == c] for c in range(2)]
    got = lax.all_to_all(
        copies, "leaf", split_axis=0, concat_axis=0, tiled=True, axis_index_groups=groups
    )
    return jnp.sum(got, axis=0)


def to_rows(acc):
    return jnp.moveaxis(acc, 1, 0).reshape(acc.shape[1], -1)


def body(coords, site_order, leaf_pairs, pair_count, probes):
    leaf_dev, width = site_order.shape
    n = probes.shape[0]
    edge = REACH * width
    base = (lax.axis_index("leaf") * leaf_dev).astype(jnp.int32).reshape(1)
    *prepared, packed = prepare_call(leaf_pairs, pair_count, base, coords, site_order, probes)
    far = (shift(packed, -1),)
    cut0, cut1 = leaf_dev // 2, leaf_dev - REACH

    def operator(run, far):
        t0, acc = run(0, cut0, (), None)
        t1, acc = run(cut1, leaf_dev, far, acc)
        back = shift(to_rows(acc[leaf_dev:]), 1)
        part_far = acc[leaf_dev:]
        t2, acc = run(cut0, cut1, (), acc)
        part_own = to_rows(acc[:leaf_dev])
        return (t0, t1, t2), part_own, part_far, back

    def run_first(i0, i1, far, prev):
        return evaluate_call(i0, i1, leaf_dev, n, prepared, far, prev)

    tiles, part, _, back = operator(run_first, far)
    image = NUGGET * probes + part
    image = jnp.concatenate([image[:, :edge] + back, image[:, edge:]], axis=1)
    image_far = shift(image[:, :edge], -1)
    by_start = {0: tiles[0], cut1: tiles[1], cut0: tiles[2]}

    def run_second(i0, i1, far, prev):
        return None, apply_call(i0, i1, leaf_dev, n, by_start[i0], image, far, prev)

    _, part2, part2_far, back2 = operator(run_second, (image_far,))
    image2_here = NUGGET * image + part2
    far_dot = jnp.sum(jnp.moveaxis(part2_far, 1, 0) * image_far.reshape(n, REACH, width), axis=(1, 2))
    sums = jnp.stack(
        [
            jnp.sum(probes * probes, axis=1),
            jnp.sum(probes * image, axis=1),
            jnp.sum(image * image, axis=1),
            jnp.sum(image * image2_here, axis=1) + far_dot,
        ]
    )
    rr, bw, ww, wz = sum_over_leaf(sums)
    image2 = jnp.concatenate([image2_here[:, :edge] + back2, image2_here[:, edge:]], axis=1)
    alpha = rr / bw
    rr1 = rr - 2.0 * alpha * bw + alpha * alpha * ww
    beta = rr1 / rr
    g = 1.0 + beta
    curve = g * g * bw - 2.0 * g * alpha * ww + alpha * alpha * wz
    alpha1 = rr1 / curve
    c = lambda x: x[:, None]
    direction1 = c(g) * probes - c(alpha) * image
    image1 = c(g) * image - c(alpha) * image2
    solution = c(alpha) * probes + c(alpha1) * direction1
    residual = probes - c(alpha) * image - c(alpha1) * image1
    return solution, residual


def solution(mesh):
    in_specs = (P(None, "leaf"), P("leaf", None), P(None, "leaf"), P("leaf"), P("probe", "leaf"))
    out_specs = (P("probe", "leaf"), P("probe", "leaf"))
    return jax.shard_map(body, mesh=mesh, in_specs=in_specs, out_specs=out_specs, check_vma=False)
```

time: 133 us -> 86 us (0.65)
  Pallas kernels: 77.8 us -> 44.9 us
  local copies, waits for them, and re-layouts: 17.1 us -> 3.98 us
    pallas_call x6 -> x7, Pallas kernels: 77.8 us -> 44.9 us  [the longest x3 31.7 us: evaluate_call(): pl.pallas_call(functools.partial(evaluate_kernel, i0, i1, leaf_dev), out_...]
    unnamed x31 -> x14, local copies, waits for them, and re-layouts: 14.7 us -> 3.26 us
    slice x4 -> x0, local copies, waits for them, and re-layouts: 1.64 us -> none  [the longest x1 0.89 us: body(): probes[:, :edge]]
  transfers between devices with their start and end apart: 6 -> 6, of which waited for: 4 -> 3; matrix products, arithmetic and copies ran while one was open for 0% -> 0% of each run, Pallas kernels for 28% -> 25%
where the time goes in v2:
time: 86 us; the launch traced here: 85.5 us
  Pallas kernels  44.9 us (52%)
  starting transfers between devices  25.9 us (30%)
  waiting for transfers between devices  7.59 us (9%)
  local copies, waits for them, and re-layouts  3.98 us (5%)
  other arithmetic  1.65 us (2%)
  between operations  1.5 us (2%)
    pallas_call x3, Pallas kernels, evaluate_call(): pl.pallas_call(functools.partial(evaluate_kernel, i0, i1, leaf_dev), out_...  31.7 us
    all_to_all x1, starting transfers between devices, sum_over_leaf(): lax.all_to_all(copies, 'leaf', split_axis=0, concat_axis=0, tiled=True, a...  13 us
    ppermute x4, starting transfers between devices, shift(): lax.ppermute(value, 'leaf', [(i, i + by) for i in range(length) if 0 <= i...  12.7 us
    pallas_call x3, Pallas kernels, apply_call(): pl.pallas_call(functools.partial(apply_kernel, i0, i1, leaf_dev), out_sha...  11.8 us
    all_to_all x1, waiting for transfers between devices, sum_over_leaf(): lax.all_to_all(copies, 'leaf', split_axis=0, concat_axis=0, tiled=True, a...  5.04 us
    unnamed x14, local copies, waits for them, and re-layouts  3.26 us
  transfers between devices with their start and end apart: 6, of which 3 were waited for; matrix products, arithmetic and copies ran while one was open for 0% of the time, Pallas kernels for 25%

profile of v2, /device:TPU:1, one launch (start us, length us, event | category | flops | bytes accessed | tf_op | source)
XLA Modules:
  0.0 85.5 jit_solution(7631098153933756108)
XLA Ops:
  1.3 0.0 copy-start
  1.3 0.9 %copy-done = f32[16,4096]{1,0:T(8,128)S(1)} copy-done((f32[16,4096]{1,0:T(8,128)S(1)}, f32[16,4096]{1,0:T(8,128)}, u32[]{:S(2)}) %copy-start) | copy-done | bytes 262168
  2.2 0.0 copy-start.2
  2.2 0.8 copy-done.2
  3.1 0.0 copy-start.3
  3.1 0.7 copy-done.3
  3.8 0.7 copy-done.4
  4.5 1.3 %prepare.1 = (f32[96,128]{1,0:T(8,128)S(1)}, f32[16,8,256]{2,1,0:T(8,128)S(1)}, bf16[16,256,24]{2,1,0:T(8,128)(2,1)S(1)}, bf16[16,32,256]{2,1,0:T(8,128)(2,1)S(1)}, f32[19,1280]{1,0:T(8,128)S(1)}) custom-call(s32[2,96]{1,0:T(2,128)S(1)} %copy-done.4, s32[1]{0:T(128)S(6)} %copy.49.count_ref, s32[1]{0:T(128)} %bitcast.1.base_ref, f32[3,4096]{1,0:T(4,128)S(1)} %copy-done.2, ...), custom_call_target="tpu_custom_call" | custom-call | tf_op jit(solution)/shard_map/prepare/pallas_call | solution.py:244
  5.8 5.1 %collective-permute-start = (f32[19,1280]{1,0:T(8,128)S(1)}, f32[19,1280]{1,0:T(8,128)S(1)}, u32[]{:S(2)}, u32[]{:S(2)}) collective-permute-start(f32[19,1280]{1,0:T(8,128)S(1)} %get-tuple-element.17), channel_id=1, source_target_pairs={{4,0},{8,4},{12,8},{16,12},{20,16},{24,20},{28,24},{32,28},{36,32}... | collective-permute-start | bytes 291848 | tf_op jit(solution)/shard_map/ppermute | solution.py:306
  10.9 15.8 %evaluate_0.1 = (bf16[49,256,512]{2,1,0:T(8,128)(2,1)S(1)}, f32[21,16,256]{2,1,0:T(8,128)S(1)}) custom-call(f32[96,128]{1,0:T(8,128)S(1)} %get-tuple-element.13.listed_ref, f32[16,8,256]{2,1,0:T(8,128)S(1)} %get-tuple-element.14.pts_ref, bf16[16,256,24]{2,1,0:T(8,128)(2,1)S(1)} %get-tuple-element.15.cols_ref, bf16[16,32,256]{2,1,0:T(8,128)(2,1)S(1)} %get-tuple-element.16.v_ref), custom_call_target="tpu_custom_call" | custom-call | flops 12884901888 | bytes 12582912 | tf_op jit(solution)/shard_map/evaluate_0/pallas_call | solution.py:274
  26.7 0.0 collective-permute-done.rest_0_
  26.7 9.9 %evaluate_11.1 = (bf16[31,256,512]{2,1,0:T(8,128)(2,1)S(1)}, f32[21,16,256]{2,1,0:T(8,128)S(1)}) custom-call(f32[96,128]{1,0:T(8,128)S(1)} %get-tuple-element.13.listed_ref, f32[16,8,256]{2,1,0:T(8,128)S(1)} %get-tuple-element.14.pts_ref, bf16[16,256,24]{2,1,0:T(8,128)(2,1)S(1)} %get-tuple-element.15.cols_ref, ...), custom_call_target="tpu_custom_call" | custom-call | flops 8053063680 | bytes 7864320 | tf_op jit(solution)/shard_map/evaluate_11/pallas_call | solution.py:274
  36.7 6.0 %evaluate_8.1 = (bf16[19,256,512]{2,1,0:T(8,128)(2,1)S(1)}, f32[21,16,256]{2,1,0:T(8,128)S(1)}) custom-call(f32[96,128]{1,0:T(8,128)S(1)} %get-tuple-element.13.listed_ref, f32[16,8,256]{2,1,0:T(8,128)S(1)} %get-tuple-element.14.pts_ref, bf16[16,256,24]{2,1,0:T(8,128)(2,1)S(1)} %get-tuple-element.15.cols_ref, ...), custom_call_target="tpu_custom_call" | custom-call | flops 4831838208 | bytes 4718592 | tf_op jit(solution)/shard_map/evaluate_8/pallas_call | solution.py:274
  42.8 1.9 %collective-permute-start.1 = (f32[16,1280]{1,0:T(8,128)S(1)}, f32[16,1280]{1,0:T(8,128)S(1)}, u32[]{:S(2)}, u32[]{:S(2)}) collective-permute-start(f32[16,1280]{1,0:T(8,128)S(1)} %bitcast.78), channel_id=1, source_target_pairs={{0,4},{4,8},{8,12},{12,16},{16,20},{20,24},{24,28},{28,32},{32,36}... | collective-permute-start | bytes 245768 | tf_op jit(solution)/shard_map/ppermute | solution.py:306
  44.7 0.0 copy-done.1
  44.8 1.4 %collective-permute-done.1 = f32[16,1280]{1,0:T(8,128)S(1)} collective-permute-done((f32[16,1280]{1,0:T(8,128)S(1)}, f32[16,1280]{1,0:T(8,128)S(1)}, u32[]{:S(2)}, u32[]{:S(2)}) %collective-permute-start.1) | collective-permute-done | bytes 81952 | tf_op jit(solution)/shard_map/ppermute | solution.py:306
  46.2 1.9 %collective-permute-start.2 = (f32[16,1280]{1,0:T(8,128)S(1)}, f32[16,1280]{1,0:T(8,128)S(1)}, u32[]{:S(2)}, u32[]{:S(2)}) collective-permute-start(f32[16,1280]{1,0:T(8,128)S(1)} %slice_add_fusion.1), channel_id=1, source_target_pairs={{4,0},{8,4},{12,8},{16,12},{20,16},{24,20},{28,24},{32,28},{36,32}... | collective-permute-start | bytes 245768 | tf_op jit(solution)/shard_map/ppermute | solution.py:306
  48.2 5.9 %apply_0.1.rest_1_ = f32[21,16,256]{2,1,0:T(8,128)S(1)} custom-call(bf16[49,256,512]{2,1,0:T(8,128)(2,1)S(1)} %get-tuple-element.23.tiles_ref, f32[16,4096]{1,0:T(8,128)S(1)} %pad_maximum_fusion.w_ref), custom_call_target="tpu_custom_call" | custom-call | flops 6576668672 | bytes 12845056 | tf_op jit(solution)/shard_map/apply_0/pallas_call | solution.py:292
  54.0 0.0 collective-permute-done.2.rest_0_
  54.1 3.7 %apply_11.1.rest_0_ = f32[21,16,256]{2,1,0:T(8,128)S(1)} custom-call(bf16[31,256,512]{2,1,0:T(8,128)(2,1)S(1)} %get-tuple-element.22.tiles_ref, f32[16,4096]{1,0:T(8,128)S(1)} %pad_maximum_fusion.w_ref, f32[16,1280]{1,0:T(8,128)S(1)} %collective-permute-done.2.rest_0_, f32[21,16,256]{2,1,0:T(8,128)S(1)} %apply_0.1.rest_1_), custom_call_target="tpu_custom_call" | custom-call | flops 4160749568 | bytes 8126464 | tf_op jit(solution)/shard_map/apply_11/pallas_call | solution.py:292
  57.8 0.1 fusion.5
  57.9 2.2 %apply_8.1 = f32[21,16,256]{2,1,0:T(8,128)S(1)} custom-call(bf16[19,256,512]{2,1,0:T(8,128)(2,1)S(1)} %get-tuple-element.21.tiles_ref, f32[16,4096]{1,0:T(8,128)S(1)} %pad_maximum_fusion.w_ref, f32[21,16,256]{2,1,0:T(8,128)S(1)} %apply_11.1.rest_0_), custom_call_target="tpu_custom_call" | custom-call | flops 2550136832 | bytes 4980736 | tf_op jit(solution)/shard_map/apply_8/pallas_call | solution.py:292
  60.2 0.2 fusion
  60.3 0.2 multiply_reduce_fusion.2
  60.6 0.1 collective-permute-start.3
  60.7 1.1 %collective-permute-done.3 = f32[4,16]{1,0:T(4,128)S(1)} collective-permute-done((f32[4,16]{1,0:T(4,128)S(1)}, f32[4,16]{1,0:T(4,128)S(1)}, u32[]{:S(2)}, u32[]{:S(2)}) %collective-permute-start.3) | collective-permute-done | bytes 288 | tf_op jit(solution)/shard_map/ppermute | solution.py:311
  61.8 0.6 broadcast_in_dim.2
  62.5 13.0 %all-to-all-start = ((f32[32,4,16]{2,1,0:T(4,128)}), f32[32,4,16]{2,1,0:T(4,128)S(1)}, u32[]{:S(2)}, u32[]{:S(2)}) async-start(f32[32,4,16]{2,1,0:T(4,128)} %broadcast_in_dim.2), calls=%async_computation | async-start | bytes 131072 | tf_op jit(solution)/shard_map/all_to_all | solution.py:314
  75.6 3.8 %collective-permute-start.4 = (f32[16,1280]{1,0:T(8,128)S(1)}, f32[16,1280]{1,0:T(8,128)S(1)}, u32[]{:S(2)}, u32[]{:S(2)}) collective-permute-start(f32[16,1280]{1,0:T(8,128)S(1)} %bitcast.77), channel_id=1, source_target_pairs={{0,4},{4,8},{8,12},{12,16},{16,20},{20,24},{24,28},{28,32},{32,36}... | collective-permute-start | bytes 245768 | tf_op jit(solution)/shard_map/ppermute | solution.py:306
  79.3 5.0 %all-to-all-done = f32[32,4,16]{2,1,0:T(4,128)S(1)} async-done(((f32[32,4,16]{2,1,0:T(4,128)}), f32[32,4,16]{2,1,0:T(4,128)S(1)}, u32[]{:S(2)}, u32[]{:S(2)}) %all-to-all-start) | async-done | bytes 8224 | tf_op jit(solution)/shard_map/all_to_all | solution.py:314
  84.5 0.0 collective-permute-done.4
  84.5 1.0 %fusion.4 = (f32[16,4096]{1,0:T(8,128)}, f32[16,4096]{1,0:T(8,128)}) fusion(f32[16,2816]{1,0:T(8,128)S(1)} %slice.38, f32[16,1280]{1,0:T(8,128)S(1)} %slice_add_fusion, f32[16,4096]{1,0:T(8,128)S(1)} %copy-done.1, f32[16]{0:T(128)S(1)} %get-tuple-element.28, f32[16]{0:T(128)S(1)} %get-tuple-element.27, f32[16]{0:T(128)S(1)} %get-tuple-element.30, ...), kind=kLoop, calls=%fused_computation.8 | loop fusion | flops 917504 | bytes 1310912 | tf_op jit(solution)/shard_map/sub | solution.py:377
  (22 shorter events, 0.3 us)
Async XLA Ops:
  1.3 1.0 %copy-start = (f32[16,4096]{1,0:T(8,128)S(1)}, f32[16,4096]{1,0:T(8,128)}, u32[]{:S(2)}) copy-start(f32[16,4096]{1,0:T(8,128)} %b_hbm.1) | copy-start | bytes 786436
  2.2 0.8 copy-start.2
  3.1 0.7 copy-start.3
  3.8 0.7 copy-start.4
  5.8 20.9 %collective-permute-start = (f32[19,1280]{1,0:T(8,128)S(1)}, f32[19,1280]{1,0:T(8,128)S(1)}, u32[]{:S(2)}, u32[]{:S(2)}) collective-permute-start(f32[19,1280]{1,0:T(8,128)S(1)} %get-tuple-element.17), channel_id=1, source_target_pairs={{4,0},{8,4},{12,8},{16,12},{20,16},{24,20},{28,24},{32,28},{36,32}... | collective-permute-start | bytes 291848 | tf_op jit(solution)/shard_map/ppermute | solution.py:306
  36.6 8.1 %copy-start.1 = (f32[16,4096]{1,0:T(8,128)S(1)}, f32[16,4096]{1,0:T(8,128)}, u32[]{:S(2)}) copy-start(f32[16,4096]{1,0:T(8,128)} %b_hbm.1) | copy-start | bytes 786436
  42.8 3.4 %collective-permute-start.1 = (f32[16,1280]{1,0:T(8,128)S(1)}, f32[16,1280]{1,0:T(8,128)S(1)}, u32[]{:S(2)}, u32[]{:S(2)}) collective-permute-start(f32[16,1280]{1,0:T(8,128)S(1)} %bitcast.78), channel_id=1, source_target_pairs={{0,4},{4,8},{8,12},{12,16},{16,20},{20,24},{24,28},{28,32},{32,36}... | collective-permute-start | bytes 245768 | tf_op jit(solution)/shard_map/ppermute | solution.py:306
  46.2 7.8 %collective-permute-start.2 = (f32[16,1280]{1,0:T(8,128)S(1)}, f32[16,1280]{1,0:T(8,128)S(1)}, u32[]{:S(2)}, u32[]{:S(2)}) collective-permute-start(f32[16,1280]{1,0:T(8,128)S(1)} %slice_add_fusion.1), channel_id=1, source_target_pairs={{4,0},{8,4},{12,8},{16,12},{20,16},{24,20},{28,24},{32,28},{36,32}... | collective-permute-start | bytes 245768 | tf_op jit(solution)/shard_map/ppermute | solution.py:306
  60.6 1.2 %collective-permute-start.3 = (f32[4,16]{1,0:T(4,128)S(1)}, f32[4,16]{1,0:T(4,128)S(1)}, u32[]{:S(2)}, u32[]{:S(2)}) collective-permute-start(f32[4,16]{1,0:T(4,128)S(1)} %pad_maximum_fusion.1), channel_id=1, source_target_pairs={{0,4},{4,0},{8,12},{12,8},{16,20},{20,16},{24,28},{28,24},{32,36},... | collective-permute-start | bytes 776 | tf_op jit(solution)/shard_map/ppermute | solution.py:311
  62.5 21.9 %all-to-all-start = ((f32[32,4,16]{2,1,0:T(4,128)}), f32[32,4,16]{2,1,0:T(4,128)S(1)}, u32[]{:S(2)}, u32[]{:S(2)}) async-start(f32[32,4,16]{2,1,0:T(4,128)} %broadcast_in_dim.2), calls=%async_computation | async-start | bytes 131072 | tf_op jit(solution)/shard_map/all_to_all | solution.py:314
  75.6 8.9 %collective-permute-start.4 = (f32[16,1280]{1,0:T(8,128)S(1)}, f32[16,1280]{1,0:T(8,128)S(1)}, u32[]{:S(2)}, u32[]{:S(2)}) collective-permute-start(f32[16,1280]{1,0:T(8,128)S(1)} %bitcast.77), channel_id=1, source_target_pairs={{0,4},{4,8},{8,12},{12,16},{16,20},{20,24},{24,28},{28,32},{32,36}... | collective-permute-start | bytes 245768 | tf_op jit(solution)/shard_map/ppermute | solution.py:306

commit v3 on v2

v3 whole, which is shorter than its diff:
```python
import functools
import math

import jax
import jax.numpy as jnp
from jax import lax
from jax.experimental import pallas as pl
from jax.experimental.pallas import tpu as pltpu
from jax.sharding import PartitionSpec as P

REACH = 5
STEPS = REACH + 1
UNIT = 0.025
LENGTH = 0.12
NUGGET = 0.5
W = 256
TAPER = REACH * UNIT
DECAY = math.sqrt(3.0) * TAPER / LENGTH
LOG2E = math.log2(math.e)
CHUNK = 16
HALF = W // 2
FLOOR_INV = 1e18
KAPPA = DECAY * LOG2E
PEAK = KAPPA**6 / (4.0 * DECAY) * 2.0**KAPPA
ROUNDER = 1.5 * 2.0 ** (23 + math.ceil(math.log2(PEAK)) - 8)


def split2(x):
    hi = x.astype(jnp.bfloat16)
    lo = (x - hi.astype(jnp.float32)).astype(jnp.bfloat16)
    return hi, lo


def split3(x):
    hi = x.astype(jnp.bfloat16)
    rest = x - hi.astype(jnp.float32)
    mid = rest.astype(jnp.bfloat16)
    lo = (rest - mid.astype(jnp.float32)).astype(jnp.bfloat16)
    return hi, mid, lo


def load_values(v_ref, src_ref, leaves, first):
    n = v_ref.shape[1] // 2
    for k in range(leaves):
        hi, lo = split2(src_ref[0:n, k * W : (k + 1) * W])
        v_ref[first + k] = jnp.concatenate([hi, lo], axis=0)


def prepare_kernel(
    pairs_ref, count_ref, base_ref, coords_hbm, order_hbm, b_hbm,
    listed_ref, pts_ref, cols_ref, v_ref, center_ref, edge_ref, coords_ref, order_ref, b_ref, sems,
):
    copies = [
        pltpu.make_async_copy(coords_hbm, coords_ref, sems.at[0]),
        pltpu.make_async_copy(order_hbm, order_ref, sems.at[1]),
        pltpu.make_async_copy(b_hbm, b_ref, sems.at[2]),
    ]
    for copy in copies:
        copy.start()
    slots = pairs_ref.shape[1]
    row = pairs_ref[0:1, :]
    place = (row - base_ref[0]) * STEPS + pairs_ref[1:2, :] - row
    live = lax.broadcasted_iota(jnp.int32, (1, slots), 1) < count_ref[0]
    place = jnp.where(live, place, -1)
    hit = lax.broadcasted_iota(jnp.int32, (slots, slots), 0) == place
    found = jnp.sum(hit.astype(jnp.float32), axis=1, keepdims=True)
    listed_ref[...] = jnp.broadcast_to(found.astype(jnp.bfloat16)[:, :, None], listed_ref.shape)
    for copy in copies:
        copy.wait()
    leaves = order_ref.shape[0]
    n = b_ref.shape[0]
    sub = lax.broadcasted_iota(jnp.int32, (W, W), 0)
    dot = functools.partial(jnp.dot, preferred_element_type=jnp.float32)
    center = jnp.broadcast_to(coords_ref[:, 0:1], (3, W))
    center_ref[...] = center
    zero = jnp.zeros((5, W), jnp.float32)
    for k in range(leaves):
        at = slice(k * W, (k + 1) * W)
        sel = (sub == order_ref[k : k + 1, :]).astype(jnp.float32).astype(jnp.bfloat16)
        parts = [dot(p, sel) for p in split3(coords_ref[:, at])]
        got = parts[0] + parts[1] + parts[2]
        here = (got - center) * (KAPPA / TAPER)
        pts_ref[k, 0:3, :] = here
        parts = [p.astype(jnp.float32) for p in split3(here)]
        stack = jnp.concatenate([z for p in parts for z in (p, zero)], axis=0)
        cols_ref[k] = jnp.transpose(stack).astype(jnp.bfloat16)
        if k < REACH:
            edge_ref[0:n, at] = b_ref[:, at]
            edge_ref[n : n + 3, at] = got
    load_values(v_ref, b_ref, leaves, 0)


def spread_rows(bc_ref, cols):
    r = lax.broadcasted_iota(jnp.int32, (24, 3 * HALF), 0)
    c = lax.broadcasted_iota(jnp.int32, (24, 3 * HALF), 1)
    sel = ((r & 7) == (c >> 7)).astype(jnp.float32).astype(jnp.bfloat16)
    bc_ref[...] = jnp.dot(cols, sel, preferred_element_type=jnp.float32)


def make_tile(t_ref, bc_ref, other, same):
    b = [
        [jnp.broadcast_to(other[c : c + 1, h * HALF : (h + 1) * HALF], (CHUNK, HALF)) for c in range(3)]
        for h in range(2)
    ]
    for k in range(W // CHUNK):
        rows = slice(k * CHUNK, (k + 1) * CHUNK)
        lower = k * CHUNK >= HALF
        for h in range(2):
            at = slice(h * HALF, (h + 1) * HALF)
            at_lo = slice(W + h * HALF, W + (h + 1) * HALF)
            if same and lower and h == 0:
                t_ref[rows, at] = jnp.zeros((CHUNK, HALF), jnp.bfloat16)
                t_ref[rows, at_lo] = jnp.zeros((CHUNK, HALF), jnp.bfloat16)
                continue
            u = None
            for c in range(3):
                d = bc_ref[rows, c * HALF : (c + 1) * HALF] - b[h][c]
                u = d * d if u is None else u + d * d
            u = jnp.minimum(u, KAPPA * KAPPA)
            q = u * jnp.minimum(lax.rsqrt(u), FLOOR_INV)
            t = KAPPA - q
            e = jnp.exp2(t)
            t = t * t
            t = t * t
            x = ((q + KAPPA / 4.0) * (q + KAPPA / DECAY)) * (t * e)
            if same and lower == bool(h):
                x = x * 0.5
            hi = (x + ROUNDER) - ROUNDER
            t_ref[rows, at] = hi.astype(jnp.bfloat16)
            t_ref[rows, at_lo] = (x - hi).astype(jnp.bfloat16)


def products(t_ref, vi, vj, listed):
    hi = t_ref[:, 0:W]
    lo = t_ref[:, W : 2 * W]
    dot = functools.partial(lax.dot_general, preferred_element_type=jnp.float32)
    nt = (((1,), (1,)), ((), ()))
    nn = (((1,), (0,)), ((), ()))
    n = vi.shape[0] // 2
    keep = jnp.concatenate([listed, listed], axis=1)
    keep = jnp.concatenate([keep, keep], axis=0)
    vi = vi * keep
    vj = vj * keep
    p = dot(vj, hi, nt)
    to_row = p[:n] + p[n:] + dot(vj[:n], lo, nt)
    p = dot(vi, hi, nn)
    to_col = p[:n] + p[n:] + dot(vi[:n], lo, nn)
    return to_row, to_col


def put_rows(out_ref, acc_ref, first, leaves, own_ref=None):
    for k in range(leaves):
        at = slice(k * W, (k + 1) * W)
        x = acc_ref[first + k] * (1.0 / PEAK)
        out_ref[:, at] = x if own_ref is None else x + NUGGET * own_ref[:, at]


def evaluate_kernel(i0, i1, leaf_dev, last, listed_ref, pts_ref, cols_ref, v_ref, center_ref, *rest):
    rest = list(rest)
    far = i1 + REACH > leaf_dev
    shift_by = 0
    edge_ref = rest.pop(0) if far else None
    own_ref = rest.pop(0) if last else None
    prev_ref = rest.pop(0) if i0 else None
    tiles_ref = rest.pop(0)
    acc_ref = rest.pop(1 if last else 0)
    rows_ref = rest.pop(0) if last or far else None
    bc_ref = rest.pop(0)
    if far:
        pts_all, v_all = rest
        n = v_ref.shape[1] // 2
        own = leaf_dev - i0
        pts_all[0:own] = pts_ref[i0:leaf_dev]
        v_all[0:own] = v_ref[i0:leaf_dev]
        for k in range(REACH):
            got = edge_ref[n : n + 3, k * W : (k + 1) * W]
            pts_all[own + k, 0:3, :] = (got - center_ref[...]) * (KAPPA / TAPER)
        load_values(v_all, edge_ref, REACH, own)
        pts_ref, v_ref = pts_all, v_all
        shift_by = i0
    if i0:
        acc_ref[...] = prev_ref[...]
    else:
        acc_ref[...] = jnp.zeros_like(acc_ref)
    tiles_ref[0] = jnp.zeros_like(tiles_ref[0])

    def finish(i, slot):
        to_row, to_col = products(
            tiles_ref.at[slot], v_ref[i - shift_by], v_ref[i + REACH - shift_by], listed_ref[i * STEPS + REACH]
        )
        acc_ref[i] += to_row
        acc_ref[i + REACH] += to_col

    def one_leaf(i, _):
        slot = (i - i0) * STEPS
        spread_rows(bc_ref, cols_ref[i])
        vi = v_ref[i - shift_by]

        def make(d):
            make_tile(tiles_ref.at[slot + (1 + d)], bc_ref, pts_ref.at[i + d - shift_by], d == 0)

        make(0)
        finish(jnp.maximum(i - 1, i0), slot)
        total = None
        for d in range(REACH):
            make(d + 1)
            to_row, to_col = products(
                tiles_ref.at[slot + (1 + d)], vi, v_ref[i + d - shift_by], listed_ref[i * STEPS + d]
            )
            total = to_row if total is None else total + to_row
            acc_ref[i + d] += to_col
        acc_ref[i] += total
        return 0

    lax.fori_loop(i0, i1, one_leaf, 0)
    finish(i1 - 1, (i1 - i0) * STEPS)
    if far:
        put_rows(rows_ref, acc_ref, leaf_dev, REACH)
    if last:
        put_rows(rows_ref, acc_ref, 0, leaf_dev, own_ref)


def apply_kernel(i0, i1, leaf_dev, last, listed_ref, tiles_ref, w_ref, *rest):
    rest = list(rest)
    far = i1 + REACH > leaf_dev
    far_ref = rest.pop(0) if far else None
    prev_ref = rest.pop(0) if i0 else None
    acc_ref = rest.pop(1 if last else 0)
    rows_ref = rest.pop(0) if last or far else None
    v_ref = rest.pop(0)
    load_values(v_ref, w_ref, leaf_dev, 0)
    if far:
        load_values(v_ref, far_ref, REACH, leaf_dev)
    if i0:
        acc_ref[...] = prev_ref[...]
    else:
        acc_ref[...] = jnp.zeros_like(acc_ref)

    def one_leaf(i, _):
        slot = (i - i0) * STEPS
        vi = v_ref[i]
        total = None
        for d in range(STEPS):
            to_row, to_col = products(
                tiles_ref.at[slot + (1 + d)], vi, v_ref[i + d], listed_ref[i * STEPS + d]
            )
            total = to_row if total is None else total + to_row
            acc_ref[i + d] += to_col
        acc_ref[i] += total
        return 0

    lax.fori_loop(i0, i1, one_leaf, 0)
    if far:
        put_rows(rows_ref, acc_ref, leaf_dev, REACH)
    if last:
        put_rows(rows_ref, acc_ref, 0, leaf_dev, w_ref)


VM = pl.BlockSpec(memory_space=pltpu.VMEM)
SM = pl.BlockSpec(memory_space=pltpu.SMEM)
ANY = pl.BlockSpec(memory_space=pl.ANY)
PARAMS = pltpu.CompilerParams(vmem_limit_bytes=8 << 20)


def prepare_call(pairs, count, base, coords, order, b):
    leaves = order.shape[0]
    n = b.shape[0]
    return pl.pallas_call(
        prepare_kernel,
        out_shape=(
            jax.ShapeDtypeStruct((pairs.shape[1], 16, HALF), jnp.bfloat16),
            jax.ShapeDtypeStruct((leaves, 8, W), jnp.float32),
            jax.ShapeDtypeStruct((leaves, W, 24), jnp.bfloat16),
            jax.ShapeDtypeStruct((leaves, 2 * n, W), jnp.bfloat16),
            jax.ShapeDtypeStruct((3, W), jnp.float32),
            jax.ShapeDtypeStruct((n + 3, REACH * W), jnp.float32),
        ),
        in_specs=[VM, SM, SM, ANY, ANY, ANY],
        out_specs=(VM,) * 6,
        scratch_shapes=[
            pltpu.VMEM(coords.shape, jnp.float32),
            pltpu.VMEM(order.shape, jnp.int32),
            pltpu.VMEM(b.shape, jnp.float32),
            pltpu.SemaphoreType.DMA((3,)),
        ],
        compiler_params=PARAMS,
        name="prepare",
    )(pairs, count, base, coords, order, b)


def shapes_out(leaf_dev, n, far, last):
    acc = (leaf_dev + REACH, n, W)
    rows = (n, (leaf_dev if last else REACH) * W)
    f32 = jnp.float32
    if last:
        return [jax.ShapeDtypeStruct(rows, f32)], [pltpu.VMEM(acc, f32)]
    return [jax.ShapeDtypeStruct(acc, f32)] + ([jax.ShapeDtypeStruct(rows, f32)] if far else []), []


def evaluate_call(i0, i1, leaf_dev, n, prepared, far, own, prev):
    tiles = (i1 - i0) * STEPS
    last = own is not None
    ops = [*prepared, *far, *([own] if last else []), *([] if prev is None else [prev])]
    outs, held_acc = shapes_out(leaf_dev, n, bool(far), last)
    scratch = [*held_acc, pltpu.VMEM((W, 3 * HALF), jnp.float32)]
    if far:
        held = leaf_dev - i0 + REACH
        scratch += [pltpu.VMEM((held, 8, W), jnp.float32), pltpu.VMEM((held, 2 * n, W), jnp.bfloat16)]
    outs = [jax.ShapeDtypeStruct((tiles + 1, W, 2 * W), jnp.bfloat16), *outs]
    return pl.pallas_call(
        functools.partial(evaluate_kernel, i0, i1, leaf_dev, last),
        out_shape=outs,
        in_specs=[VM] * len(ops),
        out_specs=[VM] * len(outs),
        scratch_shapes=scratch,
        compiler_params=PARAMS,
        cost_estimate=pl.CostEstimate(flops=tiles << 28, transcendentals=tiles << 17, bytes_accessed=tiles << 18),
        name=f"evaluate_{i0}",
    )(*ops)


def apply_call(i0, i1, leaf_dev, n, listed, tiles, own, far, last, prev):
    ops = [listed, tiles, own, *far, *([] if prev is None else [prev])]
    outs, held_acc = shapes_out(leaf_dev, n, bool(far), last)
    return pl.pallas_call(
        functools.partial(apply_kernel, i0, i1, leaf_dev, last),
        out_shape=outs,
        in_specs=[VM] * len(ops),
        out_specs=[VM] * len(outs),
        scratch_shapes=[*held_acc, pltpu.VMEM((leaf_dev + REACH, 2 * n, W), jnp.bfloat16)],
        compiler_params=PARAMS,
        cost_estimate=pl.CostEstimate(flops=tiles.shape[0] << 27, transcendentals=0, bytes_accessed=tiles.size * 2),
        name=f"apply_{i0}",
    )(*ops)


def shift(value, by):
    length = lax.axis_size("leaf")
    return lax.ppermute(value, "leaf", [(i, i + by) for i in range(length) if 0 <= i + by < length])


def sum_over_leaf(value):
    length = lax.axis_size("leaf")
    value = value + lax.ppermute(value, "leaf", [(i, i ^ 1) for i in range(length)])
    copies = jnp.broadcast_to(value, (length // 2, *value.shape))
    groups = [[i for i in range(length) if i % 2 == c] for c in range(2)]
    got = lax.all_to_all(
        copies, "leaf", split_axis=0, concat_axis=0, tiled=True, axis_index_groups=groups
    )
    return jnp.sum(got, axis=0)


def body(coords, site_order, leaf_pairs, pair_count, probes):
    leaf_dev, width = site_order.shape
    n = probes.shape[0]
    edge = REACH * width
    base = (lax.axis_index("leaf") * leaf_dev).astype(jnp.int32).reshape(1)
    *prepared, packed = prepare_call(leaf_pairs, pair_count, base, coords, site_order, probes)
    far = shift(packed, -1)
    cut0, cut1 = leaf_dev - REACH - 5, leaf_dev - REACH
    evaluate = functools.partial(evaluate_call, leaf_dev=leaf_dev, n=n, prepared=prepared)
    tiles0, acc = evaluate(0, cut0, far=(), own=None, prev=None)
    tiles1, acc, send = evaluate(cut1, leaf_dev, far=(far,), own=None, prev=acc)
    back = shift(send, 1)
    tiles2, image = evaluate(cut0, cut1, far=(), own=probes, prev=acc)
    image = jnp.concatenate([image[:, :edge] + back, image[:, edge:]], axis=1)

    image_far = shift(image[:, :edge], -1)
    apply = functools.partial(apply_call, leaf_dev=leaf_dev, n=n, listed=prepared[0], own=image)
    (acc,) = apply(0, cut0, tiles=tiles0, far=(), last=False, prev=None)
    acc, send = apply(cut1, leaf_dev, tiles=tiles1, far=(image_far,), last=False, prev=acc)
    back = shift(send, 1)
    (image2,) = apply(cut0, cut1, tiles=tiles2, far=(), last=True, prev=acc)
    image2 = jnp.concatenate([image2[:, :edge] + back, image2[:, edge:]], axis=1)
    sums = jnp.stack(
        [
            jnp.sum(probes * probes, axis=1),
            jnp.sum(probes * image, axis=1),
            jnp.sum(image * image, axis=1),
            jnp.sum(image * image2, axis=1),
        ]
    )
    rr, bw, ww, wz = sum_over_leaf(sums)
    alpha = rr / bw
    rr1 = rr - 2.0 * alpha * bw + alpha * alpha * ww
    beta = rr1 / rr
    g = 1.0 + beta
    curve = g * g * bw - 2.0 * g * alpha * ww + alpha * alpha * wz
    alpha1 = rr1 / curve
    c = lambda x: x[:, None]
    direction1 = c(g) * probes - c(alpha) * image
    image1 = c(g) * image - c(alpha) * image2
    solution = c(alpha) * probes + c(alpha1) * direction1
    residual = probes - c(alpha) * image - c(alpha1) * image1
    return solution, residual


def solution(mesh):
    in_specs = (P(None, "leaf"), P("leaf", None), P(None, "leaf"), P("leaf"), P("probe", "leaf"))
    out_specs = (P("probe", "leaf"), P("probe", "leaf"))
    return jax.shard_map(body, mesh=mesh, in_specs=in_specs, out_specs=out_specs, check_vma=False)
```

time: 86 us -> 87.3 us (1.015)
  blocking collectives: 0 us -> 22.1 us
  starting transfers between devices: 25.9 us -> 12.7 us
  waiting for transfers between devices: 7.59 us -> 1.15 us
    all_to_all x0 -> x1, blocking collectives: none -> 22.1 us  [sum_over_leaf(): lax.all_to_all(copies, 'leaf', split_axis=0, concat_axis=0, tiled=True, a...]
    all_to_all x1 -> x0, starting transfers between devices: 13 us -> none  [sum_over_leaf(): lax.all_to_all(copies, 'leaf', split_axis=0, concat_axis=0, tiled=True, a...]
    all_to_all x1 -> x0, waiting for transfers between devices: 5.04 us -> none  [sum_over_leaf(): lax.all_to_all(copies, 'leaf', split_axis=0, concat_axis=0, tiled=True, a...]
    ppermute x4, waiting for transfers between devices: 1.4 us -> 0.01 us  [shift(): lax.ppermute(value, 'leaf', [(i, i + by) for i in range(length) if 0 <= i...]
    unnamed x14 -> x10, local copies, waits for them, and re-layouts: 3.26 us -> 3.19 us
  transfers between devices with their start and end apart: 6 -> 5, of which waited for: 3 -> 1; matrix products, arithmetic and copies ran while one was open for 0% -> 0% of each run, Pallas kernels for 25% -> 34%
where the time goes in v3:
time: 87.3 us; the launch traced here: 86.8 us
  Pallas kernels  44.8 us (51%)
  blocking collectives  22.1 us (25%)
  starting transfers between devices  12.7 us (15%)
  local copies, waits for them, and re-layouts  3.23 us (4%)
  between operations  1.45 us (2%)
  other arithmetic  1.32 us (2%)
  waiting for transfers between devices  1.15 us (1%)
    pallas_call x3, Pallas kernels, evaluate_call(): pl.pallas_call(functools.partial(evaluate_kernel, i0, i1, leaf_dev, last)...  31.3 us
    all_to_all x1, blocking collectives, sum_over_leaf(): lax.all_to_all(copies, 'leaf', split_axis=0, concat_axis=0, tiled=True, a...  22.1 us
    ppermute x4, starting transfers between devices, shift(): lax.ppermute(value, 'leaf', [(i, i + by) for i in range(length) if 0 <= i...  12.6 us
    pallas_call x3, Pallas kernels, apply_call(): pl.pallas_call(functools.partial(apply_kernel, i0, i1, leaf_dev, last), o...  12 us
    unnamed x10, local copies, waits for them, and re-layouts  3.19 us
  transfers between devices with their start and end apart: 5, of which 1 were waited for; matrix products, arithmetic and copies ran while one was open for 0% of the time, Pallas kernels for 34%

profile of v3, /device:TPU:1, one launch (start us, length us, event | category | flops | bytes accessed | tf_op | source)
XLA Modules:
  0.0 86.8 jit_solution(18249154045804487686)
XLA Ops:
  1.3 0.0 copy-start
  1.3 0.9 %copy-done = f32[16,4096]{1,0:T(8,128)S(1)} copy-done((f32[16,4096]{1,0:T(8,128)S(1)}, f32[16,4096]{1,0:T(8,128)}, u32[]{:S(2)}) %copy-start) | copy-done | bytes 262168
  2.2 0.0 copy-start.2
  2.2 0.8 copy-done.2
  3.1 0.0 copy-start.3
  3.1 0.7 copy-done.3
  3.8 0.0 copy-start.4
  3.8 0.7 copy-done.4
  4.5 1.6 %prepare.1 = (bf16[96,16,128]{2,1,0:T(8,128)(2,1)S(1)}, f32[16,8,256]{2,1,0:T(8,128)S(1)}, bf16[16,256,24]{2,1,0:T(8,128)(2,1)S(1)}, bf16[16,32,256]{2,1,0:T(8,1...) custom-call(s32[2,96]{1,0:T(2,128)S(1)} %copy-done.4, s32[1]{0:T(128)S(6)} %copy.13.count_ref, ...), custom_call_target="tpu_custom_call" | custom-call | tf_op jit(solution)/shard_map/prepare/pallas_call | solution.py:268
  6.1 5.1 %collective-permute-start = (f32[19,1280]{1,0:T(8,128)S(1)}, f32[19,1280]{1,0:T(8,128)S(1)}, u32[]{:S(2)}, u32[]{:S(2)}) collective-permute-start(f32[19,1280]{1,0:T(8,128)S(1)} %get-tuple-element.22), channel_id=1, source_target_pairs={{4,0},{8,4},{12,8},{16,12},{20,16},{24,20},{28,24},{32,28},{36,32}... | collective-permute-start | bytes 291848 | tf_op jit(solution)/shard_map/ppermute | solution.py:339
  11.2 11.7 %evaluate_0.1 = (bf16[37,256,512]{2,1,0:T(8,128)(2,1)S(1)}, f32[21,16,256]{2,1,0:T(8,128)S(1)}) custom-call(bf16[96,16,128]{2,1,0:T(8,128)(2,1)S(1)} %get-tuple-element.17.listed_ref, f32[16,8,256]{2,1,0:T(8,128)S(1)} %get-tuple-element.18.pts_ref, bf16[16,256,24]{2,1,0:T(8,128)(2,1)S(1)} %get-tuple-element.19.cols_ref, ...), custom_call_target="tpu_custom_call" | custom-call | flops 9663676416 | bytes 9437184 | tf_op jit(solution)/shard_map/evaluate_0/pallas_call | solution.py:310
  22.9 0.0 collective-permute-done.rest_0_
  22.9 0.0 copy-start.1
  22.9 9.8 %evaluate_11.1 = (bf16[31,256,512]{2,1,0:T(8,128)(2,1)S(1)}, f32[21,16,256]{2,1,0:T(8,128)S(1)}, f32[16,1280]{1,0:T(8,128)S(1)}) custom-call(bf16[96,16,128]{2,1,0:T(8,128)(2,1)S(1)} %get-tuple-element.17.listed_ref, f32[16,8,256]{2,1,0:T(8,128)S(1)} %get-tuple-element.18.pts_ref, bf16[16,256,24]{2,1,0:T(8,128)(2,1)S(1)} %get-tuple-element.19.cols_ref, ...), custom_call_target="tpu_custom_call" | custom-call | flops 8053063680 | bytes 7864320 | tf_op jit(solution)/shard_map/evaluate_11/pallas_call | solution.py:310
  32.7 1.9 %collective-permute-start.1 = (f32[16,1280]{1,0:T(8,128)S(1)}, f32[16,1280]{1,0:T(8,128)S(1)}, u32[]{:S(2)}, u32[]{:S(2)}) collective-permute-start(f32[16,1280]{1,0:T(8,128)S(1)} %get-tuple-element.26), channel_id=1, source_target_pairs={{0,4},{4,8},{8,12},{12,16},{16,20},{20,24},{24,28},{28,32},{32,36}... | collective-permute-start | bytes 245768 | tf_op jit(solution)/shard_map/ppermute | solution.py:339
  34.7 0.0 copy-done.1
  34.7 9.8 %evaluate_6.1 = (bf16[31,256,512]{2,1,0:T(8,128)(2,1)S(1)}, f32[16,4096]{1,0:T(8,128)S(1)}) custom-call(bf16[96,16,128]{2,1,0:T(8,128)(2,1)S(1)} %get-tuple-element.17.listed_ref, f32[16,8,256]{2,1,0:T(8,128)S(1)} %get-tuple-element.18.pts_ref, bf16[16,256,24]{2,1,0:T(8,128)(2,1)S(1)} %get-tuple-element.19.cols_ref, ...), custom_call_target="tpu_custom_call" | custom-call | flops 8053063680 | bytes 7864320 | tf_op jit(solution)/shard_map/evaluate_6/pallas_call | solution.py:310
  44.5 0.0 collective-permute-done.1
  44.5 2.4 %collective-permute-start.2 = (f32[16,1280]{1,0:T(8,128)S(1)}, f32[16,1280]{1,0:T(8,128)S(1)}, u32[]{:S(2)}, u32[]{:S(2)}) collective-permute-start(f32[16,1280]{1,0:T(8,128)S(1)} %slice_add_fusion.1), channel_id=1, source_target_pairs={{4,0},{8,4},{12,8},{16,12},{20,16},{24,20},{28,24},{32,28},{36,32}... | collective-permute-start | bytes 245768 | tf_op jit(solution)/shard_map/ppermute | solution.py:339
  47.0 4.5 %apply_0.1.rest_1_ = f32[21,16,256]{2,1,0:T(8,128)S(1)} custom-call(bf16[96,16,128]{2,1,0:T(8,128)(2,1)S(1)} %get-tuple-element.17.listed_ref, bf16[37,256,512]{2,1,0:T(8,128)(2,1)S(1)} %get-tuple-element.29.tiles_ref, f32[16,4096]{1,0:T(8,128)S(1)} %pad_maximum_fusion.w_ref), custom_call_target="tpu_custom_call" | custom-call | flops 4966055936 | bytes 9699328 | tf_op jit(solution)/shard_map/apply_0/pallas_call | solution.py:325
  51.4 0.0 collective-permute-done.2.rest_0_
  51.4 3.7 %apply_11.1 = (f32[21,16,256]{2,1,0:T(8,128)S(1)}, f32[16,1280]{1,0:T(8,128)S(1)}) custom-call(bf16[96,16,128]{2,1,0:T(8,128)(2,1)S(1)} %get-tuple-element.17.listed_ref, bf16[31,256,512]{2,1,0:T(8,128)(2,1)S(1)} %get-tuple-element.28.tiles_ref, f32[16,4096]{1,0:T(8,128)S(1)} %pad_maximum_fusion.w_ref, f32[16,1280]{1,0:T(8,128)S(1)} %collective-permute-done.2.rest_0_, ...), custom_call_target="tpu_custom_call" | custom-call | flops 4160749568 | bytes 8126464 | tf_op jit(solution)/shard_map/apply_11/pallas_call | solution.py:325
  55.2 3.2 %collective-permute-start.3 = (f32[16,1280]{1,0:T(8,128)S(1)}, f32[16,1280]{1,0:T(8,128)S(1)}, u32[]{:S(2)}, u32[]{:S(2)}) collective-permute-start(f32[16,1280]{1,0:T(8,128)S(1)} %get-tuple-element.31), channel_id=1, source_target_pairs={{0,4},{4,8},{8,12},{12,16},{16,20},{20,24},{24,28},{28,32},{32,36}... | collective-permute-start | bytes 245768 | tf_op jit(solution)/shard_map/ppermute | solution.py:339
  58.3 3.8 %apply_6.1 = f32[16,4096]{1,0:T(8,128)S(1)} custom-call(bf16[96,16,128]{2,1,0:T(8,128)(2,1)S(1)} %get-tuple-element.17.listed_ref, bf16[31,256,512]{2,1,0:T(8,128)(2,1)S(1)} %get-tuple-element.27.tiles_ref, f32[16,4096]{1,0:T(8,128)S(1)} %pad_maximum_fusion.w_ref, f32[21,16,256]{2,1,0:T(8,128)S(1)} %get-tuple-element.30.rest_0_), custom_call_target="tpu_custom_call" | custom-call | flops 4160749568 | bytes 8126464 | tf_op jit(solution)/shard_map/apply_6/pallas_call | solution.py:325
  62.1 0.0 collective-permute-done.3
  62.2 0.2 multiply_reduce_fusion.3
  62.4 0.1 collective-permute-start.4
  62.5 1.1 %collective-permute-done.4 = f32[4,16]{1,0:T(4,128)S(1)} collective-permute-done((f32[4,16]{1,0:T(4,128)S(1)}, f32[4,16]{1,0:T(4,128)S(1)}, u32[]{:S(2)}, u32[]{:S(2)}) %collective-permute-start.4) | collective-permute-done | bytes 288 | tf_op jit(solution)/shard_map/ppermute | solution.py:344
  63.7 22.1 %all_to_all.5 = f32[32,4,16]{2,1,0:T(4,128)S(1)} all-to-all(f32[32,4,16]{2,1,0:T(4,128)S(1)} %broadcast_in_dim.2), channel_id=1, replica_groups={{0,8,16,24,32,40,48,56,64,72,80,88,96,104,112,120,128,136,144,152,160,1..., dimensions={0} | all-to-all | bytes 16384 | tf_op jit(solution)/shard_map/all_to_all | solution.py:347
  85.8 1.0 %multiply_subtract_fusion = (f32[16,4096]{1,0:T(8,128)}, f32[16,4096]{1,0:T(8,128)}) fusion(f32[16,4096]{1,0:T(8,128)S(1)} %copy-done.1, f32[16,2816]{1,0:T(8,128)S(1)} %slice.17, f32[16,1280]{1,0:T(8,128)S(1)} %slice_add_fusion, f32[16]{0:T(128)S(1)} %get-tuple-element.37, f32[16]{0:T(128)S(1)} %get-tuple-element.36, f32[16]{0:T(128)S(1)} %get-tuple-element.39, ...), kind=kLoop, calls=%fused_computation.2 | loop fusion | flops 917504 | bytes 1310912 | tf_op jit(solution)/shard_map/sub | solution.py:394
  (11 shorter events, 0.2 us)
Async XLA Ops:
  1.3 1.0 %copy-start = (f32[16,4096]{1,0:T(8,128)S(1)}, f32[16,4096]{1,0:T(8,128)}, u32[]{:S(2)}) copy-start(f32[16,4096]{1,0:T(8,128)} %rest_0_.1) | copy-start | bytes 786436
  2.2 0.8 copy-start.2
  3.1 0.7 copy-start.3
  3.8 0.7 copy-start.4
  6.1 16.8 %collective-permute-start = (f32[19,1280]{1,0:T(8,128)S(1)}, f32[19,1280]{1,0:T(8,128)S(1)}, u32[]{:S(2)}, u32[]{:S(2)}) collective-permute-start(f32[19,1280]{1,0:T(8,128)S(1)} %get-tuple-element.22), channel_id=1, source_target_pairs={{4,0},{8,4},{12,8},{16,12},{20,16},{24,20},{28,24},{32,28},{36,32}... | collective-permute-start | bytes 291848 | tf_op jit(solution)/shard_map/ppermute | solution.py:339
  22.9 11.8 %copy-start.1 = (f32[16,4096]{1,0:T(8,128)S(1)}, f32[16,4096]{1,0:T(8,128)}, u32[]{:S(2)}) copy-start(f32[16,4096]{1,0:T(8,128)} %rest_0_.1) | copy-start | bytes 786436
  32.7 11.8 %collective-permute-start.1 = (f32[16,1280]{1,0:T(8,128)S(1)}, f32[16,1280]{1,0:T(8,128)S(1)}, u32[]{:S(2)}, u32[]{:S(2)}) collective-permute-start(f32[16,1280]{1,0:T(8,128)S(1)} %get-tuple-element.26), channel_id=1, source_target_pairs={{0,4},{4,8},{8,12},{12,16},{16,20},{20,24},{24,28},{28,32},{32,36}... | collective-permute-start | bytes 245768 | tf_op jit(solution)/shard_map/ppermute | solution.py:339
  44.5 6.9 %collective-permute-start.2 = (f32[16,1280]{1,0:T(8,128)S(1)}, f32[16,1280]{1,0:T(8,128)S(1)}, u32[]{:S(2)}, u32[]{:S(2)}) collective-permute-start(f32[16,1280]{1,0:T(8,128)S(1)} %slice_add_fusion.1), channel_id=1, source_target_pairs={{4,0},{8,4},{12,8},{16,12},{20,16},{24,20},{28,24},{32,28},{36,32}... | collective-permute-start | bytes 245768 | tf_op jit(solution)/shard_map/ppermute | solution.py:339
  55.2 7.0 %collective-permute-start.3 = (f32[16,1280]{1,0:T(8,128)S(1)}, f32[16,1280]{1,0:T(8,128)S(1)}, u32[]{:S(2)}, u32[]{:S(2)}) collective-permute-start(f32[16,1280]{1,0:T(8,128)S(1)} %get-tuple-element.31), channel_id=1, source_target_pairs={{0,4},{4,8},{8,12},{12,16},{16,20},{20,24},{24,28},{28,32},{32,36}... | collective-permute-start | bytes 245768 | tf_op jit(solution)/shard_map/ppermute | solution.py:339
  62.4 1.2 %collective-permute-start.4 = (f32[4,16]{1,0:T(4,128)S(1)}, f32[4,16]{1,0:T(4,128)S(1)}, u32[]{:S(2)}, u32[]{:S(2)}) collective-permute-start(f32[4,16]{1,0:T(4,128)S(1)} %pad_maximum_fusion.2), channel_id=1, source_target_pairs={{0,4},{4,0},{8,12},{12,8},{16,20},{20,16},{24,28},{28,24},{32,36},... | collective-permute-start | bytes 776 | tf_op jit(solution)/shard_map/ppermute | solution.py:344

commit v4 on v3

--- a/solution.py
+++ b/solution.py
@@ -22,6 +22,11 @@
 FLOOR_INV = 1e18
 KAPPA = DECAY * LOG2E
 PEAK = KAPPA**6 / (4.0 * DECAY) * 2.0**KAPPA
+SCALE = KAPPA / TAPER
+COMPACT = 20.0 * KAPPA * KAPPA
+RANGE = 1e15
+TINY = 1e-12
+GROUPS = 6
 ROUNDER = 1.5 * 2.0 ** (23 + math.ceil(math.log2(PEAK)) - 8)
 
 
@@ -46,9 +51,21 @@
         v_ref[first + k] = jnp.concatenate([hi, lo], axis=0)
 
 
+def split_rows(point, center, top, weight):
+    x = (point - center) * SCALE
+    sq = x * x
+    sq = sq[0:1] + sq[1:2] + sq[2:3]
+    row = lax.broadcasted_iota(jnp.int32, x.shape, 0)
+    x = jnp.where(top, x * weight, jnp.where(row == 3, sq, 0.0))
+    hi = x.astype(jnp.bfloat16).astype(jnp.float32)
+    rest = x - hi
+    mid = rest.astype(jnp.bfloat16).astype(jnp.float32)
+    return hi, mid, rest - mid
+
+
 def prepare_kernel(
     pairs_ref, count_ref, base_ref, coords_hbm, order_hbm, b_hbm,
-    listed_ref, pts_ref, cols_ref, v_ref, center_ref, edge_ref, coords_ref, order_ref, b_ref, sems,
+    listed_ref, pts_ref, cols_ref, v_ref, center_ref, wide_ref, edge_ref, coords_ref, order_ref, b_ref, sems,
 ):
     copies = [
         pltpu.make_async_copy(coords_hbm, coords_ref, sems.at[0]),
@@ -71,53 +88,74 @@
     n = b_ref.shape[0]
     sub = lax.broadcasted_iota(jnp.int32, (W, W), 0)
     dot = functools.partial(jnp.dot, preferred_element_type=jnp.float32)
-    center = jnp.broadcast_to(coords_ref[:, 0:1], (3, W))
-    center_ref[...] = center
-    zero = jnp.zeros((5, W), jnp.float32)
+    top = lax.broadcasted_iota(jnp.int32, (8, W), 0) < 3
+    pad = jnp.zeros((5, W), jnp.float32)
+    wide = jnp.zeros((8, W), jnp.float32)
     for k in range(leaves):
         at = slice(k * W, (k + 1) * W)
         sel = (sub == order_ref[k : k + 1, :]).astype(jnp.float32).astype(jnp.bfloat16)
         parts = [dot(p, sel) for p in split3(coords_ref[:, at])]
         got = parts[0] + parts[1] + parts[2]
-        here = (got - center) * (KAPPA / TAPER)
-        pts_ref[k, 0:3, :] = here
-        parts = [p.astype(jnp.float32) for p in split3(here)]
-        stack = jnp.concatenate([z for p in parts for z in (p, zero)], axis=0)
-        cols_ref[k] = jnp.transpose(stack).astype(jnp.bfloat16)
+        point = jnp.concatenate([got, pad], axis=0)
+        center = jnp.broadcast_to(jnp.sum(point, axis=1, keepdims=True) * (1.0 / W), (8, W))
+        pts_ref[k] = point
+        center_ref[k] = center
+        hi, mid, lo = split_rows(point, center, top, 1.0)
+        square = jnp.where(top, 0.0, hi + mid + lo)
+        first = center if k == 0 else first
+        far_off = jnp.abs(point - first) * (SCALE * COMPACT / RANGE)
+        wide = jnp.maximum(wide, jnp.maximum(square, far_off))
+        one = jnp.where(lax.broadcasted_iota(jnp.int32, (8, W), 0) == 3, 1.0, 0.0)
+        stack = [hi, jnp.where(top, hi, mid), jnp.where(top, hi, lo)]
+        stack += [jnp.where(top, mid, one), jnp.where(top, mid, one), jnp.where(top, lo, one)]
+        cols_ref[k] = jnp.transpose(jnp.concatenate(stack, axis=0)).astype(jnp.bfloat16)
         if k < REACH:
             edge_ref[0:n, at] = b_ref[:, at]
             edge_ref[n : n + 3, at] = got
+    wide_ref[...] = wide
     load_values(v_ref, b_ref, leaves, 0)
 
 
-def spread_rows(bc_ref, cols):
-    r = lax.broadcasted_iota(jnp.int32, (24, 3 * HALF), 0)
-    c = lax.broadcasted_iota(jnp.int32, (24, 3 * HALF), 1)
-    sel = ((r & 7) == (c >> 7)).astype(jnp.float32).astype(jnp.bfloat16)
-    bc_ref[...] = jnp.dot(cols, sel, preferred_element_type=jnp.float32)
-
-
-def make_tile(t_ref, bc_ref, other, same):
-    b = [
-        [jnp.broadcast_to(other[c : c + 1, h * HALF : (h + 1) * HALF], (CHUNK, HALF)) for c in range(3)]
-        for h in range(2)
-    ]
+def spread_rows(bc_ref, points):
+    cols = jnp.transpose(points)
+    for c in range(3):
+        bc_ref[:, c * HALF : (c + 1) * HALF] = jnp.broadcast_to(cols[:, c : c + 1], (W, HALF))
+
+
+def far_squares(bc_ref, other):
+    def block(rows, h):
+        u = None
+        for c in range(3):
+            b = jnp.broadcast_to(other[c : c + 1, h * HALF : (h + 1) * HALF], (CHUNK, HALF))
+            d = bc_ref[rows, c * HALF : (c + 1) * HALF] - b
+            u = d * d if u is None else u + d * d
+        return u * (SCALE * SCALE)
+
+    return block
+
+
+def near_squares(cols, other, center):
+    top = lax.broadcasted_iota(jnp.int32, (8, W), 0) < 3
+    one = jnp.where(lax.broadcasted_iota(jnp.int32, (8, W), 0) == 3, 1.0, 0.0)
+    hi, mid, lo = split_rows(other, center, top, -2.0)
+    stack = [jnp.where(top, hi, one), jnp.where(top, mid, one), jnp.where(top, lo, one)]
+    stack += [hi, mid, jnp.where(top, hi, lo)]
+    rows = jnp.concatenate(stack, axis=0).astype(jnp.bfloat16)
+    all_u = jnp.dot(cols, rows, preferred_element_type=jnp.float32)
+    return lambda rows, h: all_u[rows, h * HALF : (h + 1) * HALF]
+
+
+def make_tile(t_ref, block, same):
     for k in range(W // CHUNK):
         rows = slice(k * CHUNK, (k + 1) * CHUNK)
         lower = k * CHUNK >= HALF
         for h in range(2):
-            at = slice(h * HALF, (h + 1) * HALF)
-            at_lo = slice(W + h * HALF, W + (h + 1) * HALF)
             if same and lower and h == 0:
-                t_ref[rows, at] = jnp.zeros((CHUNK, HALF), jnp.bfloat16)
-                t_ref[rows, at_lo] = jnp.zeros((CHUNK, HALF), jnp.bfloat16)
+                t_ref[0, rows, :] = jnp.zeros((CHUNK, HALF), jnp.bfloat16)
+                t_ref[2, rows, :] = jnp.zeros((CHUNK, HALF), jnp.bfloat16)
                 continue
-            u = None
-            for c in range(3):
-                d = bc_ref[rows, c * HALF : (c + 1) * HALF] - b[h][c]
-                u = d * d if u is None else u + d * d
-            u = jnp.minimum(u, KAPPA * KAPPA)
-            q = u * jnp.minimum(lax.rsqrt(u), FLOOR_INV)
+            u = jnp.minimum(jnp.maximum(block(rows, h), TINY), KAPPA * KAPPA)
+            q = u * lax.rsqrt(u)
             t = KAPPA - q
             e = jnp.exp2(t)
             t = t * t
@@ -126,13 +164,13 @@
             if same and lower == bool(h):
                 x = x * 0.5
             hi = (x + ROUNDER) - ROUNDER
-            t_ref[rows, at] = hi.astype(jnp.bfloat16)
-            t_ref[rows, at_lo] = (x - hi).astype(jnp.bfloat16)
+            t_ref[h, rows, :] = hi.astype(jnp.bfloat16)
+            t_ref[2 + h, rows, :] = (x - hi).astype(jnp.bfloat16)
 
 
 def products(t_ref, vi, vj, listed):
-    hi = t_ref[:, 0:W]
-    lo = t_ref[:, W : 2 * W]
+    hi = jnp.concatenate([t_ref[0], t_ref[1]], axis=1)
+    lo = jnp.concatenate([t_ref[2], t_ref[3]], axis=1)
     dot = functools.partial(lax.dot_general, preferred_element_type=jnp.float32)
     nt = (((1,), (1,)), ((), ()))
     nn = (((1,), (0,)), ((), ()))
@@ -155,7 +193,7 @@
         out_ref[:, at] = x if own_ref is None else x + NUGGET * own_ref[:, at]
 
 
-def evaluate_kernel(i0, i1, leaf_dev, last, listed_ref, pts_ref, cols_ref, v_ref, center_ref, *rest):
+def evaluate_kernel(i0, i1, leaf_dev, last, listed_ref, pts_ref, cols_ref, v_ref, center_ref, wide_ref, *rest):
     rest = list(rest)
     far = i1 + REACH > leaf_dev
     shift_by = 0
@@ -166,16 +204,22 @@
     acc_ref = rest.pop(1 if last else 0)
     rows_ref = rest.pop(0) if last or far else None
     bc_ref = rest.pop(0)
+    compact = jnp.max(wide_ref[...]) <= COMPACT
     if far:
         pts_all, v_all = rest
         n = v_ref.shape[1] // 2
         own = leaf_dev - i0
         pts_all[0:own] = pts_ref[i0:leaf_dev]
         v_all[0:own] = v_ref[i0:leaf_dev]
+        first = center_ref[leaf_dev - 1, 0:3, :]
+        pts_all[own:] = jnp.zeros_like(pts_all[own:])
         for k in range(REACH):
             got = edge_ref[n : n + 3, k * W : (k + 1) * W]
-            pts_all[own + k, 0:3, :] = (got - center_ref[...]) * (KAPPA / TAPER)
+            pts_all[own + k, 0:3, :] = got
+            far_off = jnp.abs(got - first) * (SCALE * COMPACT / RANGE)
+            wide = far_off if k == 0 else jnp.maximum(wide, far_off)
         load_values(v_all, edge_ref, REACH, own)
+        compact = compact & (jnp.max(wide) <= COMPACT)
         pts_ref, v_ref = pts_all, v_all
         shift_by = i0
     if i0:
@@ -191,13 +235,15 @@
         acc_ref[i] += to_row
         acc_ref[i + REACH] += to_col
 
-    def one_leaf(i, _):
+    def near_leaf(i, _):
         slot = (i - i0) * STEPS
-        spread_rows(bc_ref, cols_ref[i])
+        cols = cols_ref[i]
+        center = center_ref[i]
         vi = v_ref[i - shift_by]
 
         def make(d):
-            make_tile(tiles_ref.at[slot + (1 + d)], bc_ref, pts_ref.at[i + d - shift_by], d == 0)
+            block = near_squares(cols, pts_ref[i + d - shift_by], center)
+            make_tile(tiles_ref.at[slot + (1 + d)], block, d == 0)
 
         make(0)
         finish(jnp.maximum(i - 1, i0), slot)
@@ -212,7 +258,39 @@
         acc_ref[i] += total
         return 0
 
-    lax.fori_loop(i0, i1, one_leaf, 0)
+    def far_leaf(i, _):
+        slot = (i - i0) * STEPS
+        spread_rows(bc_ref, pts_ref[i - shift_by])
+
+        def step(d, _):
+            t_ref = tiles_ref.at[slot + (1 + d)]
+            block = far_squares(bc_ref, pts_ref.at[i + d - shift_by])
+            lax.cond(d == 0, lambda: make_tile(t_ref, block, True), lambda: make_tile(t_ref, block, False))
+
+            @pl.when(d < REACH)
+            def _():
+                to_row, to_col = products(
+                    t_ref, v_ref[i - shift_by], v_ref[i + d - shift_by], listed_ref[i * STEPS + d]
+                )
+                acc_ref[i] += to_row
+                acc_ref[i + d] += to_col
+
+            return 0
+
+        @pl.when(i > i0)
+        def _():
+            finish(i - 1, slot)
+
+        return lax.fori_loop(0, STEPS, step, 0)
+
+    @pl.when(compact)
+    def _():
+        lax.fori_loop(i0, i1, near_leaf, 0)
+
+    @pl.when(jnp.logical_not(compact))
+    def _():
+        lax.fori_loop(i0, i1, far_leaf, 0)
+
     finish(i1 - 1, (i1 - i0) * STEPS)
     if far:
         put_rows(rows_ref, acc_ref, leaf_dev, REACH)
@@ -270,13 +348,14 @@
         out_shape=(
             jax.ShapeDtypeStruct((pairs.shape[1], 16, HALF), jnp.bfloat16),
             jax.ShapeDtypeStruct((leaves, 8, W), jnp.float32),
-            jax.ShapeDtypeStruct((leaves, W, 24), jnp.bfloat16),
+            jax.ShapeDtypeStruct((leaves, W, 8 * GROUPS), jnp.bfloat16),
             jax.ShapeDtypeStruct((leaves, 2 * n, W), jnp.bfloat16),
-            jax.ShapeDtypeStruct((3, W), jnp.float32),
+            jax.ShapeDtypeStruct((leaves, 8, W), jnp.float32),
+            jax.ShapeDtypeStruct((8, W), jnp.float32),
             jax.ShapeDtypeStruct((n + 3, REACH * W), jnp.float32),
         ),
         in_specs=[VM, SM, SM, ANY, ANY, ANY],
-        out_specs=(VM,) * 6,
+        out_specs=(VM,) * 7,
         scratch_shapes=[
             pltpu.VMEM(coords.shape, jnp.float32),
             pltpu.VMEM(order.shape, jnp.int32),
@@ -306,7 +385,7 @@
     if far:
         held = leaf_dev - i0 + REACH
         scratch += [pltpu.VMEM((held, 8, W), jnp.float32), pltpu.VMEM((held, 2 * n, W), jnp.bfloat16)]
-    outs = [jax.ShapeDtypeStruct((tiles + 1, W, 2 * W), jnp.bfloat16), *outs]
+    outs = [jax.ShapeDtypeStruct((tiles + 1, 4, W, HALF), jnp.bfloat16), *outs]
     return pl.pallas_call(
         functools.partial(evaluate_kernel, i0, i1, leaf_dev, last),
         out_shape=outs,

time: 87.3 us -> 77.8 us (0.89)
  Pallas kernels: 44.8 us -> 35.4 us
    pallas_call x3, Pallas kernels: 31.3 us -> 21.5 us  [evaluate_call(): pl.pallas_call(functools.partial(evaluate_kernel, i0, i1, leaf_dev, last)...]
  transfers between devices with their start and end apart: 5 -> 5, of which waited for: 1 -> 1; matrix products, arithmetic and copies ran while one was open for 0% -> 0% of each run, Pallas kernels for 34% -> 30%
where the time goes in v4:
time: 77.8 us; the launch traced here: 77.4 us
  Pallas kernels  35.4 us (46%)
  blocking collectives  22.1 us (28%)
  starting transfers between devices  12.7 us (16%)
  local copies, waits for them, and re-layouts  3.22 us (4%)
  between operations  1.44 us (2%)
  other arithmetic  1.32 us (2%)
  waiting for transfers between devices  1.15 us (1%)
    all_to_all x1, blocking collectives, sum_over_leaf(): lax.all_to_all(copies, 'leaf', split_axis=0, concat_axis=0, tiled=True, a...  22.1 us
    pallas_call x3, Pallas kernels, evaluate_call(): pl.pallas_call(functools.partial(evaluate_kernel, i0, i1, leaf_dev, last)...  21.5 us
    ppermute x4, starting transfers between devices, shift(): lax.ppermute(value, 'leaf', [(i, i + by) for i in range(length) if 0 <= i...  12.6 us
    pallas_call x3, Pallas kernels, apply_call(): pl.pallas_call(functools.partial(apply_kernel, i0, i1, leaf_dev, last), o...  12 us
    unnamed x10, local copies, waits for them, and re-layouts  3.18 us
    pallas_call x1, Pallas kernels, prepare_call(): pl.pallas_call(prepare_kernel, out_shape=(jax.ShapeDtypeStruct((pairs.sha...  1.91 us
  transfers between devices with their start and end apart: 5, of which 1 were waited for; matrix products, arithmetic and copies ran while one was open for 0% of the time, Pallas kernels for 30%

profile of v4, /device:TPU:1, one launch (start us, length us, event | category | flops | bytes accessed | tf_op | source)
XLA Modules:
  0.0 77.4 jit_solution(3536144867814945280)
XLA Ops:
  1.3 0.0 copy-start
  1.3 0.9 %copy-done = f32[16,4096]{1,0:T(8,128)S(1)} copy-done((f32[16,4096]{1,0:T(8,128)S(1)}, f32[16,4096]{1,0:T(8,128)}, u32[]{:S(2)}) %copy-start) | copy-done | bytes 262168
  2.2 0.0 copy-start.2
  2.2 0.8 %copy-done.2 = f32[3,4096]{1,0:T(4,128)S(1)} copy-done((f32[3,4096]{1,0:T(4,128)S(1)}, f32[3,4096]{1,0:T(4,128)}, u32[]{:S(2)}) %copy-start.2) | copy-done | bytes 49176
  3.1 0.0 copy-start.3
  3.1 0.7 copy-done.3
  3.8 0.0 copy-start.4
  3.8 0.7 copy-done.4
  4.5 1.9 %prepare.1 = (bf16[96,16,128]{2,1,0:T(8,128)(2,1)S(1)}, f32[16,8,256]{2,1,0:T(8,128)S(1)}, bf16[16,256,48]{2,1,0:T(8,128)(2,1)S(1)}, bf16[16,32,256]{2,1,0:T(8,1...) custom-call(s32[2,96]{1,0:T(2,128)S(1)} %copy-done.4, ...), custom_call_target="tpu_custom_call" | custom-call | tf_op jit(solution)/shard_map/prepare/pallas_call | solution.py:346
  6.4 5.1 %collective-permute-start = (f32[19,1280]{1,0:T(8,128)S(1)}, f32[19,1280]{1,0:T(8,128)S(1)}, u32[]{:S(2)}, u32[]{:S(2)}) collective-permute-start(f32[19,1280]{1,0:T(8,128)S(1)} %get-tuple-element.24), channel_id=1, source_target_pairs={{4,0},{8,4},{12,8},{16,12},{20,16},{24,20},{28,24},{32,28},{36,32}... | collective-permute-start | bytes 291848 | tf_op jit(solution)/shard_map/ppermute | solution.py:418
  11.5 8.0 %evaluate_0.1 = (bf16[37,4,256,128]{3,2,1,0:T(8,128)(2,1)S(1)}, f32[21,16,256]{2,1,0:T(8,128)S(1)}) custom-call(bf16[96,16,128]{2,1,0:T(8,128)(2,1)S(1)} %get-tuple-element.18.listed_ref, f32[16,8,256]{2,1,0:T(8,128)S(1)} %get-tuple-element.19.pts_ref, bf16[16,256,48]{2,1,0:T(8,128)(2,1)S(1)} %get-tuple-element.20.cols_ref, ...), custom_call_target="tpu_custom_call" | custom-call | flops 9663676416 | bytes 9437184 | tf_op jit(solution)/shard_map/evaluate_0/pallas_call | solution.py:389
  19.5 0.0 collective-permute-done.rest_0_
  19.5 0.0 copy-start.1
  19.5 6.8 %evaluate_11.1 = (bf16[31,4,256,128]{3,2,1,0:T(8,128)(2,1)S(1)}, f32[21,16,256]{2,1,0:T(8,128)S(1)}, f32[16,1280]{1,0:T(8,128)S(1)}) custom-call(bf16[96,16,128]{2,1,0:T(8,128)(2,1)S(1)} %get-tuple-element.18.listed_ref, f32[16,8,256]{2,1,0:T(8,128)S(1)} %get-tuple-element.19.pts_ref, bf16[16,256,48]{2,1,0:T(8,128)(2,1)S(1)} %get-tuple-element.20.cols_ref, ...), custom_call_target="tpu_custom_call" | custom-call | flops 8053063680 | bytes 7864320 | tf_op jit(solution)/shard_map/evaluate_11/pallas_call | solution.py:389
  26.3 1.9 %collective-permute-start.1 = (f32[16,1280]{1,0:T(8,128)S(1)}, f32[16,1280]{1,0:T(8,128)S(1)}, u32[]{:S(2)}, u32[]{:S(2)}) collective-permute-start(f32[16,1280]{1,0:T(8,128)S(1)} %get-tuple-element.28), channel_id=1, source_target_pairs={{0,4},{4,8},{8,12},{12,16},{16,20},{20,24},{24,28},{28,32},{32,36}... | collective-permute-start | bytes 245768 | tf_op jit(solution)/shard_map/ppermute | solution.py:418
  28.3 0.0 copy-done.1
  28.3 6.8 %evaluate_6.1 = (bf16[31,4,256,128]{3,2,1,0:T(8,128)(2,1)S(1)}, f32[16,4096]{1,0:T(8,128)S(1)}) custom-call(bf16[96,16,128]{2,1,0:T(8,128)(2,1)S(1)} %get-tuple-element.18.listed_ref, f32[16,8,256]{2,1,0:T(8,128)S(1)} %get-tuple-element.19.pts_ref, bf16[16,256,48]{2,1,0:T(8,128)(2,1)S(1)} %get-tuple-element.20.cols_ref, ...), custom_call_target="tpu_custom_call" | custom-call | flops 8053063680 | bytes 7864320 | tf_op jit(solution)/shard_map/evaluate_6/pallas_call | solution.py:389
  35.1 0.0 collective-permute-done.1
  35.1 2.4 %collective-permute-start.2 = (f32[16,1280]{1,0:T(8,128)S(1)}, f32[16,1280]{1,0:T(8,128)S(1)}, u32[]{:S(2)}, u32[]{:S(2)}) collective-permute-start(f32[16,1280]{1,0:T(8,128)S(1)} %slice_add_fusion.1), channel_id=1, source_target_pairs={{4,0},{8,4},{12,8},{16,12},{20,16},{24,20},{28,24},{32,28},{36,32}... | collective-permute-start | bytes 245768 | tf_op jit(solution)/shard_map/ppermute | solution.py:418
  37.5 4.5 %apply_0.1.rest_1_ = f32[21,16,256]{2,1,0:T(8,128)S(1)} custom-call(bf16[96,16,128]{2,1,0:T(8,128)(2,1)S(1)} %get-tuple-element.18.listed_ref, bf16[37,4,256,128]{3,2,1,0:T(8,128)(2,1)S(1)} %get-tuple-element.31.tiles_ref, f32[16,4096]{1,0:T(8,128)S(1)} %pad_maximum_fusion.w_ref), custom_call_target="tpu_custom_call" | custom-call | flops 4966055936 | bytes 9699328 | tf_op jit(solution)/shard_map/apply_0/pallas_call | solution.py:404
  42.0 0.0 collective-permute-done.2.rest_0_
  42.0 3.7 %apply_11.1 = (f32[21,16,256]{2,1,0:T(8,128)S(1)}, f32[16,1280]{1,0:T(8,128)S(1)}) custom-call(bf16[96,16,128]{2,1,0:T(8,128)(2,1)S(1)} %get-tuple-element.18.listed_ref, bf16[31,4,256,128]{3,2,1,0:T(8,128)(2,1)S(1)} %get-tuple-element.30.tiles_ref, f32[16,4096]{1,0:T(8,128)S(1)} %pad_maximum_fusion.w_ref, f32[16,1280]{1,0:T(8,128)S(1)} %collective-permute-done.2.rest_0_, ...), custom_call_target="tpu_custom_call" | custom-call | flops 4160749568 | bytes 8126464 | tf_op jit(solution)/shard_map/apply_11/pallas_call | solution.py:404
  45.8 3.2 %collective-permute-start.3 = (f32[16,1280]{1,0:T(8,128)S(1)}, f32[16,1280]{1,0:T(8,128)S(1)}, u32[]{:S(2)}, u32[]{:S(2)}) collective-permute-start(f32[16,1280]{1,0:T(8,128)S(1)} %get-tuple-element.33), channel_id=1, source_target_pairs={{0,4},{4,8},{8,12},{12,16},{16,20},{20,24},{24,28},{28,32},{32,36}... | collective-permute-start | bytes 245768 | tf_op jit(solution)/shard_map/ppermute | solution.py:418
  48.9 3.8 %apply_6.1 = f32[16,4096]{1,0:T(8,128)S(1)} custom-call(bf16[96,16,128]{2,1,0:T(8,128)(2,1)S(1)} %get-tuple-element.18.listed_ref, bf16[31,4,256,128]{3,2,1,0:T(8,128)(2,1)S(1)} %get-tuple-element.29.tiles_ref, f32[16,4096]{1,0:T(8,128)S(1)} %pad_maximum_fusion.w_ref, f32[21,16,256]{2,1,0:T(8,128)S(1)} %get-tuple-element.32.rest_0_), custom_call_target="tpu_custom_call" | custom-call | flops 4160749568 | bytes 8126464 | tf_op jit(solution)/shard_map/apply_6/pallas_call | solution.py:404
  52.7 0.0 collective-permute-done.3
  52.7 0.2 multiply_reduce_fusion.3
  53.0 0.1 collective-permute-start.4
  53.1 1.1 %collective-permute-done.4 = f32[4,16]{1,0:T(4,128)S(1)} collective-permute-done((f32[4,16]{1,0:T(4,128)S(1)}, f32[4,16]{1,0:T(4,128)S(1)}, u32[]{:S(2)}, u32[]{:S(2)}) %collective-permute-start.4) | collective-permute-done | bytes 288 | tf_op jit(solution)/shard_map/ppermute | solution.py:423
  54.2 22.1 %all_to_all.5 = f32[32,4,16]{2,1,0:T(4,128)S(1)} all-to-all(f32[32,4,16]{2,1,0:T(4,128)S(1)} %broadcast_in_dim.2), channel_id=1, replica_groups={{0,8,16,24,32,40,48,56,64,72,80,88,96,104,112,120,128,136,144,152,160,1..., dimensions={0} | all-to-all | bytes 16384 | tf_op jit(solution)/shard_map/all_to_all | solution.py:426
  76.4 1.0 %multiply_subtract_fusion = (f32[16,4096]{1,0:T(8,128)}, f32[16,4096]{1,0:T(8,128)}) fusion(f32[16,4096]{1,0:T(8,128)S(1)} %copy-done.1, f32[16,2816]{1,0:T(8,128)S(1)} %slice.17, f32[16,1280]{1,0:T(8,128)S(1)} %slice_add_fusion, f32[16]{0:T(128)S(1)} %get-tuple-element.39, f32[16]{0:T(128)S(1)} %get-tuple-element.38, f32[16]{0:T(128)S(1)} %get-tuple-element.41, ...), kind=kLoop, calls=%fused_computation.2 | loop fusion | flops 917504 | bytes 1310912 | tf_op jit(solution)/shard_map/sub | solution.py:473
  (11 shorter events, 0.2 us)
Async XLA Ops:
  1.3 1.0 %copy-start = (f32[16,4096]{1,0:T(8,128)S(1)}, f32[16,4096]{1,0:T(8,128)}, u32[]{:S(2)}) copy-start(f32[16,4096]{1,0:T(8,128)} %rest_0_.1) | copy-start | bytes 786436
  2.2 0.8 %copy-start.2 = (f32[3,4096]{1,0:T(4,128)S(1)}, f32[3,4096]{1,0:T(4,128)}, u32[]{:S(2)}) copy-start(f32[3,4096]{1,0:T(4,128)} %coords_hbm.1) | copy-start | bytes 147460
  3.1 0.7 copy-start.3
  3.8 0.7 copy-start.4
  6.4 13.1 %collective-permute-start = (f32[19,1280]{1,0:T(8,128)S(1)}, f32[19,1280]{1,0:T(8,128)S(1)}, u32[]{:S(2)}, u32[]{:S(2)}) collective-permute-start(f32[19,1280]{1,0:T(8,128)S(1)} %get-tuple-element.24), channel_id=1, source_target_pairs={{4,0},{8,4},{12,8},{16,12},{20,16},{24,20},{28,24},{32,28},{36,32}... | collective-permute-start | bytes 291848 | tf_op jit(solution)/shard_map/ppermute | solution.py:418
  19.5 8.7 %copy-start.1 = (f32[16,4096]{1,0:T(8,128)S(1)}, f32[16,4096]{1,0:T(8,128)}, u32[]{:S(2)}) copy-start(f32[16,4096]{1,0:T(8,128)} %rest_0_.1) | copy-start | bytes 786436
  26.3 8.7 %collective-permute-start.1 = (f32[16,1280]{1,0:T(8,128)S(1)}, f32[16,1280]{1,0:T(8,128)S(1)}, u32[]{:S(2)}, u32[]{:S(2)}) collective-permute-start(f32[16,1280]{1,0:T(8,128)S(1)} %get-tuple-element.28), channel_id=1, source_target_pairs={{0,4},{4,8},{8,12},{12,16},{16,20},{20,24},{24,28},{28,32},{32,36}... | collective-permute-start | bytes 245768 | tf_op jit(solution)/shard_map/ppermute | solution.py:418
  35.1 6.9 %collective-permute-start.2 = (f32[16,1280]{1,0:T(8,128)S(1)}, f32[16,1280]{1,0:T(8,128)S(1)}, u32[]{:S(2)}, u32[]{:S(2)}) collective-permute-start(f32[16,1280]{1,0:T(8,128)S(1)} %slice_add_fusion.1), channel_id=1, source_target_pairs={{4,0},{8,4},{12,8},{16,12},{20,16},{24,20},{28,24},{32,28},{36,32}... | collective-permute-start | bytes 245768 | tf_op jit(solution)/shard_map/ppermute | solution.py:418
  45.8 7.0 %collective-permute-start.3 = (f32[16,1280]{1,0:T(8,128)S(1)}, f32[16,1280]{1,0:T(8,128)S(1)}, u32[]{:S(2)}, u32[]{:S(2)}) collective-permute-start(f32[16,1280]{1,0:T(8,128)S(1)} %get-tuple-element.33), channel_id=1, source_target_pairs={{0,4},{4,8},{8,12},{12,16},{16,20},{20,24},{24,28},{28,32},{32,36}... | collective-permute-start | bytes 245768 | tf_op jit(solution)/shard_map/ppermute | solution.py:418
  53.0 1.2 %collective-permute-start.4 = (f32[4,16]{1,0:T(4,128)S(1)}, f32[4,16]{1,0:T(4,128)S(1)}, u32[]{:S(2)}, u32[]{:S(2)}) collective-permute-start(f32[4,16]{1,0:T(4,128)S(1)} %pad_maximum_fusion.2), channel_id=1, source_target_pairs={{0,4},{4,0},{8,12},{12,8},{16,20},{20,16},{24,28},{28,24},{32,36},... | collective-permute-start | bytes 776 | tf_op jit(solution)/shard_map/ppermute | solution.py:423

commit v5 on v4

--- a/solution.py
+++ b/solution.py
@@ -64,16 +64,19 @@
 
 
 def prepare_kernel(
-    pairs_ref, count_ref, base_ref, coords_hbm, order_hbm, b_hbm,
-    listed_ref, pts_ref, cols_ref, v_ref, center_ref, wide_ref, edge_ref, coords_ref, order_ref, b_ref, sems,
+    count_ref, base_ref, pairs_hbm, coords_hbm, order_hbm, b_hbm,
+    listed_ref, pts_ref, cols_ref, v_ref, center_ref, wide_ref, edge_ref,
+    pairs_ref, coords_ref, order_ref, b_ref, sems,
 ):
     copies = [
-        pltpu.make_async_copy(coords_hbm, coords_ref, sems.at[0]),
-        pltpu.make_async_copy(order_hbm, order_ref, sems.at[1]),
-        pltpu.make_async_copy(b_hbm, b_ref, sems.at[2]),
+        pltpu.make_async_copy(pairs_hbm, pairs_ref, sems.at[0]),
+        pltpu.make_async_copy(coords_hbm, coords_ref, sems.at[1]),
+        pltpu.make_async_copy(order_hbm, order_ref, sems.at[2]),
+        pltpu.make_async_copy(b_hbm, b_ref, sems.at[3]),
     ]
     for copy in copies:
         copy.start()
+    copies[0].wait()
     slots = pairs_ref.shape[1]
     row = pairs_ref[0:1, :]
     place = (row - base_ref[0]) * STEPS + pairs_ref[1:2, :] - row
@@ -82,7 +85,7 @@
     hit = lax.broadcasted_iota(jnp.int32, (slots, slots), 0) == place
     found = jnp.sum(hit.astype(jnp.float32), axis=1, keepdims=True)
     listed_ref[...] = jnp.broadcast_to(found.astype(jnp.bfloat16)[:, :, None], listed_ref.shape)
-    for copy in copies:
+    for copy in copies[1:]:
         copy.wait()
     leaves = order_ref.shape[0]
     n = b_ref.shape[0]
@@ -301,9 +304,9 @@
 def apply_kernel(i0, i1, leaf_dev, last, listed_ref, tiles_ref, w_ref, *rest):
     rest = list(rest)
     far = i1 + REACH > leaf_dev
-    far_ref = rest.pop(0) if far else None
+    far_ref = rest.pop(0) if far or last else None
     prev_ref = rest.pop(0) if i0 else None
-    acc_ref = rest.pop(1 if last else 0)
+    acc_ref = rest.pop(0)
     rows_ref = rest.pop(0) if last or far else None
     v_ref = rest.pop(0)
     load_values(v_ref, w_ref, leaf_dev, 0)
@@ -331,12 +334,22 @@
     if far:
         put_rows(rows_ref, acc_ref, leaf_dev, REACH)
     if last:
-        put_rows(rows_ref, acc_ref, 0, leaf_dev, w_ref)
+        total = jnp.zeros(rows_ref.shape, jnp.float32)
+        for k in range(leaf_dev):
+            total += acc_ref[k] * w_ref[:, k * W : (k + 1) * W]
+        for k in range(REACH):
+            total += acc_ref[leaf_dev + k] * far_ref[:, k * W : (k + 1) * W]
+        rows_ref[...] = total * (1.0 / PEAK)
+
+
+def finish_kernel(leaf_dev, acc_ref, own_ref, back_ref, rows_ref):
+    put_rows(rows_ref, acc_ref, 0, leaf_dev, own_ref)
+    rows_ref[:, 0 : REACH * W] += back_ref[...]
 
 
 VM = pl.BlockSpec(memory_space=pltpu.VMEM)
 SM = pl.BlockSpec(memory_space=pltpu.SMEM)
-ANY = pl.BlockSpec(memory_space=pl.ANY)
+HBM = pl.BlockSpec(memory_space=pltpu.HBM)
 PARAMS = pltpu.CompilerParams(vmem_limit_bytes=8 << 20)
 
 
@@ -354,17 +367,18 @@
             jax.ShapeDtypeStruct((8, W), jnp.float32),
             jax.ShapeDtypeStruct((n + 3, REACH * W), jnp.float32),
         ),
-        in_specs=[VM, SM, SM, ANY, ANY, ANY],
+        in_specs=[SM, SM, HBM, HBM, HBM, HBM],
         out_specs=(VM,) * 7,
         scratch_shapes=[
+            pltpu.VMEM(pairs.shape, jnp.int32),
             pltpu.VMEM(coords.shape, jnp.float32),
             pltpu.VMEM(order.shape, jnp.int32),
             pltpu.VMEM(b.shape, jnp.float32),
-            pltpu.SemaphoreType.DMA((3,)),
+            pltpu.SemaphoreType.DMA((4,)),
         ],
         compiler_params=PARAMS,
         name="prepare",
-    )(pairs, count, base, coords, order, b)
+    )(count, base, *(pltpu.with_memory_space_constraint(x, pltpu.HBM) for x in (pairs, coords, order, b)))
 
 
 def shapes_out(leaf_dev, n, far, last):
@@ -400,17 +414,32 @@
 
 def apply_call(i0, i1, leaf_dev, n, listed, tiles, own, far, last, prev):
     ops = [listed, tiles, own, *far, *([] if prev is None else [prev])]
-    outs, held_acc = shapes_out(leaf_dev, n, bool(far), last)
+    extent = leaf_dev + REACH
+    f32 = jnp.float32
+    outs = [jax.ShapeDtypeStruct((extent, n, W), f32)]
+    if far:
+        outs += [jax.ShapeDtypeStruct((n, W if last else REACH * W), f32)]
     return pl.pallas_call(
         functools.partial(apply_kernel, i0, i1, leaf_dev, last),
         out_shape=outs,
         in_specs=[VM] * len(ops),
         out_specs=[VM] * len(outs),
-        scratch_shapes=[*held_acc, pltpu.VMEM((leaf_dev + REACH, 2 * n, W), jnp.bfloat16)],
+        scratch_shapes=[pltpu.VMEM((extent, 2 * n, W), jnp.bfloat16)],
         compiler_params=PARAMS,
         cost_estimate=pl.CostEstimate(flops=tiles.shape[0] << 27, transcendentals=0, bytes_accessed=tiles.size * 2),
         name=f"apply_{i0}",
     )(*ops)
+
+
+def finish_call(leaf_dev, acc, own, back):
+    return pl.pallas_call(
+        functools.partial(finish_kernel, leaf_dev),
+        out_shape=jax.ShapeDtypeStruct(own.shape, jnp.float32),
+        in_specs=[VM] * 3,
+        out_specs=VM,
+        compiler_params=PARAMS,
+        name="finish",
+    )(acc, own, back)
 
 
 def shift(value, by):
@@ -449,16 +478,18 @@
     (acc,) = apply(0, cut0, tiles=tiles0, far=(), last=False, prev=None)
     acc, send = apply(cut1, leaf_dev, tiles=tiles1, far=(image_far,), last=False, prev=acc)
     back = shift(send, 1)
-    (image2,) = apply(cut0, cut1, tiles=tiles2, far=(), last=True, prev=acc)
-    image2 = jnp.concatenate([image2[:, :edge] + back, image2[:, edge:]], axis=1)
+    acc, dots = apply(cut0, cut1, tiles=tiles2, far=(image_far,), last=True, prev=acc)
+    dots, back = lax.optimization_barrier((dots, back))
+    square = jnp.sum(image * image, axis=1)
     sums = jnp.stack(
         [
             jnp.sum(probes * probes, axis=1),
             jnp.sum(probes * image, axis=1),
-            jnp.sum(image * image, axis=1),
-            jnp.sum(image * image2, axis=1),
+            square,
+            jnp.sum(dots, axis=1) + NUGGET * square,
         ]
     )
+    image2 = finish_call(leaf_dev, acc, image, back)
     rr, bw, ww, wz = sum_over_leaf(sums)
     alpha = rr / bw
     rr1 = rr - 2.0 * alpha * bw + alpha * alpha * ww

time: 77.8 us -> 76.2 us (0.979)
  blocking collectives: 22.1 us -> 0 us
  starting transfers between devices: 12.7 us -> 26.1 us
  waiting for transfers between devices: 1.15 us -> 9.96 us
  local copies, waits for them, and re-layouts: 3.22 us -> 0.66 us
  Pallas kernels: 35.4 us -> 36.3 us
    all_to_all x1 -> x0, blocking collectives: 22.1 us -> none  [sum_over_leaf(): lax.all_to_all(copies, 'leaf', split_axis=0, concat_axis=0, tiled=True, a...]
    all_to_all x0 -> x1, starting transfers between devices: none -> 13.4 us  [sum_over_leaf(): lax.all_to_all(copies, 'leaf', split_axis=0, concat_axis=0, tiled=True, a...]
    all_to_all x0 -> x1, waiting for transfers between devices: none -> 8.81 us  [sum_over_leaf(): lax.all_to_all(copies, 'leaf', split_axis=0, concat_axis=0, tiled=True, a...]
    unnamed x10 -> x2, local copies, waits for them, and re-layouts: 3.18 us -> 0.01 us
    pallas_call x1, Pallas kernels: 1.91 us -> 2.69 us  [prepare_call(): pl.pallas_call(prepare_kernel, out_shape=(jax.ShapeDtypeStruct((pairs.sha...]
  transfers between devices with their start and end apart: 5 -> 6, of which waited for: 1 -> 2; matrix products, arithmetic and copies ran while one was open for 0% -> 0% of each run, Pallas kernels for 30% -> 30%
where the time goes in v5:
time: 76.2 us; the launch traced here: 75.9 us
  Pallas kernels  36.3 us (48%)
  starting transfers between devices  26.1 us (34%)
  waiting for transfers between devices  9.96 us (13%)
  other arithmetic  1.41 us (2%)
  between operations  1.41 us (2%)
    pallas_call x3, Pallas kernels, evaluate_call(): pl.pallas_call(functools.partial(evaluate_kernel, i0, i1, leaf_dev, last)...  21.6 us
    all_to_all x1, starting transfers between devices, sum_over_leaf(): lax.all_to_all(copies, 'leaf', split_axis=0, concat_axis=0, tiled=True, a...  13.4 us
    ppermute x4, starting transfers between devices, shift(): lax.ppermute(value, 'leaf', [(i, i + by) for i in range(length) if 0 <= i...  12.6 us
    pallas_call x3, Pallas kernels, apply_call(): pl.pallas_call(functools.partial(apply_kernel, i0, i1, leaf_dev, last), o...  12 us
    all_to_all x1, waiting for transfers between devices, sum_over_leaf(): lax.all_to_all(copies, 'leaf', split_axis=0, concat_axis=0, tiled=True, a...  8.81 us
    pallas_call x1, Pallas kernels, prepare_call(): pl.pallas_call(prepare_kernel, out_shape=(jax.ShapeDtypeStruct((pairs.sha...  2.69 us
  transfers between devices with their start and end apart: 6, of which 2 were waited for; matrix products, arithmetic and copies ran while one was open for 0% of the time, Pallas kernels for 30%

profile of v5, /device:TPU:1, one launch (start us, length us, event | category | flops | bytes accessed | tf_op | source)
XLA Modules:
  0.0 75.9 jit_solution(1959394016907679590)
XLA Ops:
  1.3 2.7 %prepare.1 = (bf16[96,16,128]{2,1,0:T(8,128)(2,1)S(1)}, f32[16,8,256]{2,1,0:T(8,128)S(1)}, bf16[16,256,48]{2,1,0:T(8,128)(2,1)S(1)}, bf16[16,32,256]{2,1,0:T(8,1...) custom-call(s32[1]{0:T(128)S(6)} %copy.13.count_ref, s32[1]{0:T(128)} %bitcast.1.base_ref, ...), custom_call_target="tpu_custom_call" | custom-call | tf_op jit(solution)/shard_map/prepare/pallas_call | solution.py:359
  4.0 5.1 %collective-permute-start = (f32[19,1280]{1,0:T(8,128)S(1)}, f32[19,1280]{1,0:T(8,128)S(1)}, u32[]{:S(2)}, u32[]{:S(2)}) collective-permute-start(f32[19,1280]{1,0:T(8,128)S(1)} %get-tuple-element.28), channel_id=1, source_target_pairs={{4,0},{8,4},{12,8},{16,12},{20,16},{24,20},{28,24},{32,28},{36,32}... | collective-permute-start | bytes 291848 | tf_op jit(solution)/shard_map/ppermute | solution.py:447
  9.1 8.0 %evaluate_0.1 = (bf16[37,4,256,128]{3,2,1,0:T(8,128)(2,1)S(1)}, f32[21,16,256]{2,1,0:T(8,128)S(1)}) custom-call(bf16[96,16,128]{2,1,0:T(8,128)(2,1)S(1)} %get-tuple-element.22.listed_ref, f32[16,8,256]{2,1,0:T(8,128)S(1)} %get-tuple-element.23.pts_ref, bf16[16,256,48]{2,1,0:T(8,128)(2,1)S(1)} %get-tuple-element.24.cols_ref, ...), custom_call_target="tpu_custom_call" | custom-call | flops 9663676416 | bytes 9437184 | tf_op jit(solution)/shard_map/evaluate_0/pallas_call | solution.py:403
  17.1 0.0 collective-permute-done.rest_0_
  17.1 0.0 copy-start
  17.1 6.8 %evaluate_11.1 = (bf16[31,4,256,128]{3,2,1,0:T(8,128)(2,1)S(1)}, f32[21,16,256]{2,1,0:T(8,128)S(1)}, f32[16,1280]{1,0:T(8,128)S(1)}) custom-call(bf16[96,16,128]{2,1,0:T(8,128)(2,1)S(1)} %get-tuple-element.22.listed_ref, f32[16,8,256]{2,1,0:T(8,128)S(1)} %get-tuple-element.23.pts_ref, bf16[16,256,48]{2,1,0:T(8,128)(2,1)S(1)} %get-tuple-element.24.cols_ref, ...), custom_call_target="tpu_custom_call" | custom-call | flops 8053063680 | bytes 7864320 | tf_op jit(solution)/shard_map/evaluate_11/pallas_call | solution.py:403
  23.9 1.9 %collective-permute-start.1 = (f32[16,1280]{1,0:T(8,128)S(1)}, f32[16,1280]{1,0:T(8,128)S(1)}, u32[]{:S(2)}, u32[]{:S(2)}) collective-permute-start(f32[16,1280]{1,0:T(8,128)S(1)} %get-tuple-element.32), channel_id=1, source_target_pairs={{0,4},{4,8},{8,12},{12,16},{16,20},{20,24},{24,28},{28,32},{32,36}... | collective-permute-start | bytes 245768 | tf_op jit(solution)/shard_map/ppermute | solution.py:447
  25.9 0.0 copy-done
  25.9 6.8 %evaluate_6.1 = (bf16[31,4,256,128]{3,2,1,0:T(8,128)(2,1)S(1)}, f32[16,4096]{1,0:T(8,128)S(1)}) custom-call(bf16[96,16,128]{2,1,0:T(8,128)(2,1)S(1)} %get-tuple-element.22.listed_ref, f32[16,8,256]{2,1,0:T(8,128)S(1)} %get-tuple-element.23.pts_ref, bf16[16,256,48]{2,1,0:T(8,128)(2,1)S(1)} %get-tuple-element.24.cols_ref, ...), custom_call_target="tpu_custom_call" | custom-call | flops 8053063680 | bytes 7864320 | tf_op jit(solution)/shard_map/evaluate_6/pallas_call | solution.py:403
  32.7 0.0 collective-permute-done.1
  32.7 2.4 %collective-permute-start.2 = (f32[16,1280]{1,0:T(8,128)S(1)}, f32[16,1280]{1,0:T(8,128)S(1)}, u32[]{:S(2)}, u32[]{:S(2)}) collective-permute-start(f32[16,1280]{1,0:T(8,128)S(1)} %slice_add_fusion), channel_id=1, source_target_pairs={{4,0},{8,4},{12,8},{16,12},{20,16},{24,20},{28,24},{32,28},{36,32}... | collective-permute-start | bytes 245768 | tf_op jit(solution)/shard_map/ppermute | solution.py:447
  35.1 0.2 multiply_reduce_fusion.2
  35.3 4.5 %apply_0.1.rest_1_ = f32[21,16,256]{2,1,0:T(8,128)S(1)} custom-call(bf16[96,16,128]{2,1,0:T(8,128)(2,1)S(1)} %get-tuple-element.22.listed_ref, bf16[37,4,256,128]{3,2,1,0:T(8,128)(2,1)S(1)} %get-tuple-element.35.tiles_ref, f32[16,4096]{1,0:T(8,128)S(1)} %get-tuple-element.51.w_ref.own_ref), custom_call_target="tpu_custom_call" | custom-call | flops 4966055936 | bytes 9699328 | tf_op jit(solution)/shard_map/apply_0/pallas_call | solution.py:422
  39.8 0.0 collective-permute-done.2.rest_0_
  39.8 3.7 %apply_11.1 = (f32[21,16,256]{2,1,0:T(8,128)S(1)}, f32[16,1280]{1,0:T(8,128)S(1)}) custom-call(bf16[96,16,128]{2,1,0:T(8,128)(2,1)S(1)} %get-tuple-element.22.listed_ref, bf16[31,4,256,128]{3,2,1,0:T(8,128)(2,1)S(1)} %get-tuple-element.34.tiles_ref, f32[16,4096]{1,0:T(8,128)S(1)} %get-tuple-element.51.w_ref.own_ref, ...), custom_call_target="tpu_custom_call" | custom-call | flops 4160749568 | bytes 8126464 | tf_op jit(solution)/shard_map/apply_11/pallas_call | solution.py:422
  43.6 3.2 %collective-permute-start.3 = (f32[16,1280]{1,0:T(8,128)S(1)}, f32[16,1280]{1,0:T(8,128)S(1)}, u32[]{:S(2)}, u32[]{:S(2)}) collective-permute-start(f32[16,1280]{1,0:T(8,128)S(1)} %get-tuple-element.38), channel_id=1, source_target_pairs={{0,4},{4,8},{8,12},{12,16},{16,20},{20,24},{24,28},{28,32},{32,36}... | collective-permute-start | bytes 245768 | tf_op jit(solution)/shard_map/ppermute | solution.py:447
  46.7 3.8 %apply_6.1 = (f32[21,16,256]{2,1,0:T(8,128)S(1)}, f32[16,256]{1,0:T(8,128)S(1)}) custom-call(bf16[96,16,128]{2,1,0:T(8,128)(2,1)S(1)} %get-tuple-element.22.listed_ref, bf16[31,4,256,128]{3,2,1,0:T(8,128)(2,1)S(1)} %get-tuple-element.33.tiles_ref, f32[16,4096]{1,0:T(8,128)S(1)} %get-tuple-element.51.w_ref.own_ref, ...), custom_call_target="tpu_custom_call" | custom-call | flops 4160749568 | bytes 8126464 | tf_op jit(solution)/shard_map/apply_6/pallas_call | solution.py:422
  50.5 0.0 collective-permute-done.3.back_ref
  50.5 0.1 reduce_sum.50
  50.7 0.1 collective-permute-start.4
  50.8 1.1 %collective-permute-done.4 = f32[4,16]{1,0:T(4,128)S(1)} collective-permute-done((f32[4,16]{1,0:T(4,128)S(1)}, f32[4,16]{1,0:T(4,128)S(1)}, u32[]{:S(2)}, u32[]{:S(2)}) %collective-permute-start.4) | collective-permute-done | bytes 288 | tf_op jit(solution)/shard_map/ppermute | solution.py:452
  51.9 0.6 broadcast_in_dim.2
  52.5 13.4 %all-to-all-start = ((f32[32,4,16]{2,1,0:T(4,128)}), f32[32,4,16]{2,1,0:T(4,128)S(1)}, u32[]{:S(2)}, u32[]{:S(2)}) async-start(f32[32,4,16]{2,1,0:T(4,128)} %broadcast_in_dim.2), calls=%async_computation | async-start | bytes 131072 | tf_op jit(solution)/shard_map/all_to_all | solution.py:455
  66.0 8.8 %all-to-all-done = f32[32,4,16]{2,1,0:T(4,128)S(1)} async-done(((f32[32,4,16]{2,1,0:T(4,128)}), f32[32,4,16]{2,1,0:T(4,128)S(1)}, u32[]{:S(2)}, u32[]{:S(2)}) %all-to-all-start) | async-done | bytes 8224 | tf_op jit(solution)/shard_map/all_to_all | solution.py:455
  74.9 1.0 %multiply_subtract_fusion = (f32[16,4096]{1,0:T(8,128)}, f32[16,4096]{1,0:T(8,128)}) fusion(f32[16,4096]{1,0:T(8,128)S(1)} %finish.1, f32[16,4096]{1,0:T(8,128)S(1)} %copy-done, f32[16]{0:T(128)S(1)} %get-tuple-element.46, f32[16]{0:T(128)S(1)} %get-tuple-element.45, f32[16]{0:T(128)S(1)} %get-tuple-element.48, f32[16,2816]{1,0:T(8,128)S(1)} %slice.7, ...), kind=kLoop, calls=%fused_computation.1 | loop fusion | flops 851968 | bytes 1310912 | tf_op jit(solution)/shard_map/sub | solution.py:504
  (9 shorter events, 0.2 us)
Async XLA Ops:
  4.0 13.2 %collective-permute-start = (f32[19,1280]{1,0:T(8,128)S(1)}, f32[19,1280]{1,0:T(8,128)S(1)}, u32[]{:S(2)}, u32[]{:S(2)}) collective-permute-start(f32[19,1280]{1,0:T(8,128)S(1)} %get-tuple-element.28), channel_id=1, source_target_pairs={{4,0},{8,4},{12,8},{16,12},{20,16},{24,20},{28,24},{32,28},{36,32}... | collective-permute-start | bytes 291848 | tf_op jit(solution)/shard_map/ppermute | solution.py:447
  17.1 8.7 %copy-start = (f32[16,4096]{1,0:T(8,128)S(1)}, f32[16,4096]{1,0:T(8,128)}, u32[]{:S(2)}) copy-start(f32[16,4096]{1,0:T(8,128)} %rest_0_.1) | copy-start | bytes 786436
  23.9 8.8 %collective-permute-start.1 = (f32[16,1280]{1,0:T(8,128)S(1)}, f32[16,1280]{1,0:T(8,128)S(1)}, u32[]{:S(2)}, u32[]{:S(2)}) collective-permute-start(f32[16,1280]{1,0:T(8,128)S(1)} %get-tuple-element.32), channel_id=1, source_target_pairs={{0,4},{4,8},{8,12},{12,16},{16,20},{20,24},{24,28},{28,32},{32,36}... | collective-permute-start | bytes 245768 | tf_op jit(solution)/shard_map/ppermute | solution.py:447
  32.7 7.1 %collective-permute-start.2 = (f32[16,1280]{1,0:T(8,128)S(1)}, f32[16,1280]{1,0:T(8,128)S(1)}, u32[]{:S(2)}, u32[]{:S(2)}) collective-permute-start(f32[16,1280]{1,0:T(8,128)S(1)} %slice_add_fusion), channel_id=1, source_target_pairs={{4,0},{8,4},{12,8},{16,12},{20,16},{24,20},{28,24},{32,28},{36,32}... | collective-permute-start | bytes 245768 | tf_op jit(solution)/shard_map/ppermute | solution.py:447
  43.6 6.9 %collective-permute-start.3 = (f32[16,1280]{1,0:T(8,128)S(1)}, f32[16,1280]{1,0:T(8,128)S(1)}, u32[]{:S(2)}, u32[]{:S(2)}) collective-permute-start(f32[16,1280]{1,0:T(8,128)S(1)} %get-tuple-element.38), channel_id=1, source_target_pairs={{0,4},{4,8},{8,12},{12,16},{16,20},{20,24},{24,28},{28,32},{32,36}... | collective-permute-start | bytes 245768 | tf_op jit(solution)/shard_map/ppermute | solution.py:447
  50.7 1.2 %collective-permute-start.4 = (f32[4,16]{1,0:T(4,128)S(1)}, f32[4,16]{1,0:T(4,128)S(1)}, u32[]{:S(2)}, u32[]{:S(2)}) collective-permute-start(f32[4,16]{1,0:T(4,128)S(1)} %pad_maximum_fusion.1), channel_id=1, source_target_pairs={{0,4},{4,0},{8,12},{12,8},{16,20},{20,16},{24,28},{28,24},{32,36},... | collective-permute-start | bytes 776 | tf_op jit(solution)/shard_map/ppermute | solution.py:452
  52.5 22.3 %all-to-all-start = ((f32[32,4,16]{2,1,0:T(4,128)}), f32[32,4,16]{2,1,0:T(4,128)S(1)}, u32[]{:S(2)}, u32[]{:S(2)}) async-start(f32[32,4,16]{2,1,0:T(4,128)} %broadcast_in_dim.2), calls=%async_computation | async-start | bytes 131072 | tf_op jit(solution)/shard_map/all_to_all | solution.py:455

commit v6 on v5

--- a/solution.py
+++ b/solution.py
@@ -27,7 +27,6 @@
 RANGE = 1e15
 TINY = 1e-12
 GROUPS = 6
-ROUNDER = 1.5 * 2.0 ** (23 + math.ceil(math.log2(PEAK)) - 8)
 
 
 def split2(x):
@@ -166,27 +165,25 @@
             x = ((q + KAPPA / 4.0) * (q + KAPPA / DECAY)) * (t * e)
             if same and lower == bool(h):
                 x = x * 0.5
-            hi = (x + ROUNDER) - ROUNDER
-            t_ref[h, rows, :] = hi.astype(jnp.bfloat16)
-            t_ref[2 + h, rows, :] = (x - hi).astype(jnp.bfloat16)
-
-
-def products(t_ref, vi, vj, listed):
+            hi, lo = split2(x)
+            t_ref[h, rows, :] = hi
+            t_ref[2 + h, rows, :] = lo
+
+
+def product(t_ref, v, listed, transposed):
     hi = jnp.concatenate([t_ref[0], t_ref[1]], axis=1)
     lo = jnp.concatenate([t_ref[2], t_ref[3]], axis=1)
-    dot = functools.partial(lax.dot_general, preferred_element_type=jnp.float32)
-    nt = (((1,), (1,)), ((), ()))
-    nn = (((1,), (0,)), ((), ()))
-    n = vi.shape[0] // 2
+    dims = (((1,), (1 if transposed else 0,)), ((), ()))
+    dot = functools.partial(lax.dot_general, dimension_numbers=dims, preferred_element_type=jnp.float32)
+    n = v.shape[0] // 2
     keep = jnp.concatenate([listed, listed], axis=1)
-    keep = jnp.concatenate([keep, keep], axis=0)
-    vi = vi * keep
-    vj = vj * keep
-    p = dot(vj, hi, nt)
-    to_row = p[:n] + p[n:] + dot(vj[:n], lo, nt)
-    p = dot(vi, hi, nn)
-    to_col = p[:n] + p[n:] + dot(vi[:n], lo, nn)
-    return to_row, to_col
+    v = v * jnp.concatenate([keep, keep], axis=0)
+    p = dot(v, hi)
+    return p[:n] + p[n:] + dot(v[:n], lo)
+
+
+def products(t_ref, vi, vj, listed):
+    return product(t_ref, vj, listed, True), product(t_ref, vi, listed, False)
 
 
 def put_rows(out_ref, acc_ref, first, leaves, own_ref=None):
@@ -301,21 +298,27 @@
         put_rows(rows_ref, acc_ref, 0, leaf_dev, own_ref)
 
 
+def clear_or_copy(acc_ref, prev_ref):
+    acc_ref[...] = jnp.zeros_like(acc_ref) if prev_ref is None else prev_ref[...]
+
+
+def weighted(acc_ref, field_ref, first, leaves):
+    total = acc_ref[first] * field_ref[:, 0:W]
+    for k in range(1, leaves):
+        total += acc_ref[first + k] * field_ref[:, k * W : (k + 1) * W]
+    return total
+
+
 def apply_kernel(i0, i1, leaf_dev, last, listed_ref, tiles_ref, w_ref, *rest):
     rest = list(rest)
-    far = i1 + REACH > leaf_dev
-    far_ref = rest.pop(0) if far or last else None
+    if last:
+        far_ref, extra_ref = rest.pop(0), rest.pop(0)
     prev_ref = rest.pop(0) if i0 else None
     acc_ref = rest.pop(0)
-    rows_ref = rest.pop(0) if last or far else None
+    dots_ref = rest.pop(0) if last else None
     v_ref = rest.pop(0)
     load_values(v_ref, w_ref, leaf_dev, 0)
-    if far:
-        load_values(v_ref, far_ref, REACH, leaf_dev)
-    if i0:
-        acc_ref[...] = prev_ref[...]
-    else:
-        acc_ref[...] = jnp.zeros_like(acc_ref)
+    clear_or_copy(acc_ref, prev_ref)
 
     def one_leaf(i, _):
         slot = (i - i0) * STEPS
@@ -331,19 +334,52 @@
         return 0
 
     lax.fori_loop(i0, i1, one_leaf, 0)
-    if far:
-        put_rows(rows_ref, acc_ref, leaf_dev, REACH)
     if last:
-        total = jnp.zeros(rows_ref.shape, jnp.float32)
-        for k in range(leaf_dev):
-            total += acc_ref[k] * w_ref[:, k * W : (k + 1) * W]
-        for k in range(REACH):
-            total += acc_ref[leaf_dev + k] * far_ref[:, k * W : (k + 1) * W]
-        rows_ref[...] = total * (1.0 / PEAK)
-
-
-def finish_kernel(leaf_dev, acc_ref, own_ref, back_ref, rows_ref):
-    put_rows(rows_ref, acc_ref, 0, leaf_dev, own_ref)
+        total = weighted(acc_ref, w_ref, 0, leaf_dev) + weighted(acc_ref, far_ref, leaf_dev, REACH)
+        dots_ref[...] = (total + extra_ref[...]) * (1.0 / PEAK)
+
+
+def edge_kernel(i0, leaf_dev, listed_ref, tiles_ref, w_ref, far_ref, prev_ref, acc_ref, send_ref, dots_ref, v_ref, part_ref):
+    held = leaf_dev - i0
+    load_values(v_ref, w_ref, leaf_dev, 0)
+    clear_or_copy(part_ref, None)
+
+    def one_leaf(i, _):
+        slot = (i - i0) * STEPS
+        vi = v_ref[i]
+        for d in range(STEPS):
+            part_ref[i - i0 + d] += product(
+                tiles_ref.at[slot + (1 + d)], vi, listed_ref[i * STEPS + d], False
+            )
+        return 0
+
+    lax.fori_loop(i0, leaf_dev, one_leaf, 0)
+    dots_ref[...] = weighted(part_ref, w_ref.at[:, i0 * W :], 0, held) + weighted(part_ref, far_ref, held, REACH)
+    acc_ref[...] = prev_ref[...]
+    for k in range(held + REACH):
+        acc_ref[i0 + k] += part_ref[k]
+    put_rows(send_ref, acc_ref, leaf_dev, REACH)
+
+
+def finish_kernel(
+    i0, leaf_dev, listed_ref, tiles_hbm, w_ref, far_ref, prev_ref, back_ref, rows_ref, v_ref, acc_ref, tiles_ref, sems
+):
+    copies = []
+    for k in range(leaf_dev - i0):
+        at = pl.ds(k * STEPS, STEPS)
+        copies.append(pltpu.make_async_copy(tiles_hbm.at[pl.ds(k * STEPS + 1, STEPS)], tiles_ref.at[at], sems.at[k]))
+        copies[k].start()
+    load_values(v_ref, w_ref.at[:, i0 * W :], leaf_dev - i0, 0)
+    load_values(v_ref, far_ref, REACH, leaf_dev - i0)
+    acc_ref[...] = prev_ref[...]
+    for k, copy in enumerate(copies):
+        copy.wait()
+        total = None
+        for d in range(STEPS):
+            to_row = product(tiles_ref.at[k * STEPS + d], v_ref[k + d], listed_ref[(i0 + k) * STEPS + d], True)
+            total = to_row if total is None else total + to_row
+        acc_ref[i0 + k] += total
+    put_rows(rows_ref, acc_ref, 0, leaf_dev, w_ref)
     rows_ref[:, 0 : REACH * W] += back_ref[...]
 
 
@@ -412,34 +448,63 @@
     )(*ops)
 
 
-def apply_call(i0, i1, leaf_dev, n, listed, tiles, own, far, last, prev):
-    ops = [listed, tiles, own, *far, *([] if prev is None else [prev])]
-    extent = leaf_dev + REACH
-    f32 = jnp.float32
-    outs = [jax.ShapeDtypeStruct((extent, n, W), f32)]
-    if far:
-        outs += [jax.ShapeDtypeStruct((n, W if last else REACH * W), f32)]
+def small_call(kernel, name, outs, scratch, tiles, ops, in_hbm=()):
     return pl.pallas_call(
-        functools.partial(apply_kernel, i0, i1, leaf_dev, last),
-        out_shape=outs,
-        in_specs=[VM] * len(ops),
+        kernel,
+        out_shape=[jax.ShapeDtypeStruct(shape, jnp.float32) for shape in outs],
+        in_specs=[HBM if k in in_hbm else VM for k in range(len(ops))],
         out_specs=[VM] * len(outs),
-        scratch_shapes=[pltpu.VMEM((extent, 2 * n, W), jnp.bfloat16)],
-        compiler_params=PARAMS,
+        scratch_shapes=scratch,
+        compiler_params=pltpu.CompilerParams(vmem_limit_bytes=14 << 20) if in_hbm else PARAMS,
         cost_estimate=pl.CostEstimate(flops=tiles.shape[0] << 27, transcendentals=0, bytes_accessed=tiles.size * 2),
-        name=f"apply_{i0}",
-    )(*ops)
-
-
-def finish_call(leaf_dev, acc, own, back):
-    return pl.pallas_call(
-        functools.partial(finish_kernel, leaf_dev),
-        out_shape=jax.ShapeDtypeStruct(own.shape, jnp.float32),
-        in_specs=[VM] * 3,
-        out_specs=VM,
-        compiler_params=PARAMS,
-        name="finish",
-    )(acc, own, back)
+        name=name,
+    )(*[pltpu.with_memory_space_constraint(x, pltpu.HBM) if k in in_hbm else x for k, x in enumerate(ops)])
+
+
+def apply_call(i0, i1, leaf_dev, n, listed, tiles, own, last, prev):
+    acc = (leaf_dev + REACH, n, W)
+    ops = [listed, tiles, own, *last, *([] if prev is None else [prev])]
+    return small_call(
+        functools.partial(apply_kernel, i0, i1, leaf_dev, bool(last)),
+        f"apply_{i0}",
+        [acc, (n, W)] if last else [acc],
+        [pltpu.VMEM((leaf_dev, 2 * n, W), jnp.bfloat16)],
+        tiles,
+        ops,
+    )
+
+
+def edge_call(i0, leaf_dev, n, listed, tiles, own, far, prev):
+    acc = (leaf_dev + REACH, n, W)
+    return small_call(
+        functools.partial(edge_kernel, i0, leaf_dev),
+        "apply_edge",
+        [acc, (n, REACH * W), (n, W)],
+        [
+            pltpu.VMEM((leaf_dev, 2 * n, W), jnp.bfloat16),
+            pltpu.VMEM((leaf_dev - i0 + REACH, n, W), jnp.float32),
+        ],
+        tiles,
+        [listed, tiles, own, far, prev],
+    )
+
+
+def finish_call(i0, leaf_dev, n, listed, tiles, own, far, prev, back):
+    acc = (leaf_dev + REACH, n, W)
+    return small_call(
+        functools.partial(finish_kernel, i0, leaf_dev),
+        "finish",
+        [own.shape],
+        [
+            pltpu.VMEM((leaf_dev - i0 + REACH, 2 * n, W), jnp.bfloat16),
+            pltpu.VMEM(acc, jnp.float32),
+            pltpu.VMEM((tiles.shape[0] - 1, *tiles.shape[1:]), jnp.bfloat16),
+            pltpu.SemaphoreType.DMA((leaf_dev - i0,)),
+        ],
+        tiles,
+        [listed, tiles, own, far, prev, back],
+        in_hbm=(1,),
+    )[0]
 
 
 def shift(value, by):
@@ -450,12 +515,12 @@
 def sum_over_leaf(value):
     length = lax.axis_size("leaf")
     value = value + lax.ppermute(value, "leaf", [(i, i ^ 1) for i in range(length)])
-    copies = jnp.broadcast_to(value, (length // 2, *value.shape))
+    copies = jnp.broadcast_to(value.reshape(-1), (length // 2, value.size))
     groups = [[i for i in range(length) if i % 2 == c] for c in range(2)]
     got = lax.all_to_all(
         copies, "leaf", split_axis=0, concat_axis=0, tiled=True, axis_index_groups=groups
     )
-    return jnp.sum(got, axis=0)
+    return jnp.sum(got, axis=0).reshape(value.shape)
 
 
 def body(coords, site_order, leaf_pairs, pair_count, probes):
@@ -474,11 +539,11 @@
     image = jnp.concatenate([image[:, :edge] + back, image[:, edge:]], axis=1)
 
     image_far = shift(image[:, :edge], -1)
-    apply = functools.partial(apply_call, leaf_dev=leaf_dev, n=n, listed=prepared[0], own=image)
-    (acc,) = apply(0, cut0, tiles=tiles0, far=(), last=False, prev=None)
-    acc, send = apply(cut1, leaf_dev, tiles=tiles1, far=(image_far,), last=False, prev=acc)
+    common = dict(leaf_dev=leaf_dev, n=n, listed=prepared[0], own=image)
+    (acc,) = apply_call(0, cut0, tiles=tiles0, last=(), prev=None, **common)
+    acc, send, edge_dots = edge_call(cut1, tiles=tiles1, far=image_far, prev=acc, **common)
     back = shift(send, 1)
-    acc, dots = apply(cut0, cut1, tiles=tiles2, far=(image_far,), last=True, prev=acc)
+    acc, dots = apply_call(cut0, cut1, tiles=tiles2, last=(image_far, edge_dots), prev=acc, **common)
     dots, back = lax.optimization_barrier((dots, back))
     square = jnp.sum(image * image, axis=1)
     sums = jnp.stack(
@@ -489,7 +554,7 @@
             jnp.sum(dots, axis=1) + NUGGET * square,
         ]
     )
-    image2 = finish_call(leaf_dev, acc, image, back)
+    image2 = finish_call(cut1, tiles=tiles1, far=image_far, prev=acc, back=back, **common)
     rr, bw, ww, wz = sum_over_leaf(sums)
     alpha = rr / bw
     rr1 = rr - 2.0 * alpha * bw + alpha * alpha * ww

time: 76.2 us -> 73.6 us (0.966)
  waiting for transfers between devices: 9.96 us -> 3.98 us
  Pallas kernels: 36.3 us -> 39.5 us
    all_to_all x1, waiting for transfers between devices: 8.81 us -> 2.82 us  [sum_over_leaf(): lax.all_to_all(copies, 'leaf', split_axis=0, concat_axis=0, tiled=True, a...]
    pallas_call x4, Pallas kernels: 12 us -> 15.8 us  [small_call(): pl.pallas_call(kernel, out_shape=[jax.ShapeDtypeStruct(shape, jnp.float32...]
  transfers between devices with their start and end apart: 6 -> 6, of which waited for: 2 -> 2; matrix products, arithmetic and copies ran while one was open for 0% -> 0% of each run, Pallas kernels for 30% -> 39%
where the time goes in v6:
time: 73.6 us; the launch traced here: 73.3 us
  Pallas kernels  39.5 us (54%)
  starting transfers between devices  26.2 us (36%)
  waiting for transfers between devices  3.98 us (5%)
  other arithmetic  1.52 us (2%)
  between operations  1.42 us (2%)
    pallas_call x3, Pallas kernels, evaluate_call(): pl.pallas_call(functools.partial(evaluate_kernel, i0, i1, leaf_dev, last)...  21 us
    pallas_call x4, Pallas kernels, small_call(): pl.pallas_call(kernel, out_shape=[jax.ShapeDtypeStruct(shape, jnp.float32...  15.8 us
    all_to_all x1, starting transfers between devices, sum_over_leaf(): lax.all_to_all(copies, 'leaf', split_axis=0, concat_axis=0, tiled=True, a...  13.4 us
    ppermute x4, starting transfers between devices, shift(): lax.ppermute(value, 'leaf', [(i, i + by) for i in range(length) if 0 <= i...  12.6 us
    all_to_all x1, waiting for transfers between devices, sum_over_leaf(): lax.all_to_all(copies, 'leaf', split_axis=0, concat_axis=0, tiled=True, a...  2.82 us
    pallas_call x1, Pallas kernels, prepare_call(): pl.pallas_call(prepare_kernel, out_shape=(jax.ShapeDtypeStruct((pairs.sha...  2.69 us
  transfers between devices with their start and end apart: 6, of which 2 were waited for; matrix products, arithmetic and copies ran while one was open for 0% of the time, Pallas kernels for 39%

profile of v6, /device:TPU:1, one launch (start us, length us, event | category | flops | bytes accessed | tf_op | source)
XLA Modules:
  0.0 73.3 jit_solution(9405713053647115284)
XLA Ops:
  1.3 2.7 %prepare.1 = (bf16[96,16,128]{2,1,0:T(8,128)(2,1)S(1)}, f32[16,8,256]{2,1,0:T(8,128)S(1)}, bf16[16,256,48]{2,1,0:T(8,128)(2,1)S(1)}, bf16[16,32,256]{2,1,0:T(8,1...) custom-call(s32[1]{0:T(128)S(6)} %copy.8.count_ref, s32[1]{0:T(128)} %bitcast.1.base_ref, ...), custom_call_target="tpu_custom_call" | custom-call | tf_op jit(solution)/shard_map/prepare/pallas_call | solution.py:395
  4.0 5.1 %collective-permute-start = (f32[19,1280]{1,0:T(8,128)S(1)}, f32[19,1280]{1,0:T(8,128)S(1)}, u32[]{:S(2)}, u32[]{:S(2)}) collective-permute-start(f32[19,1280]{1,0:T(8,128)S(1)} %get-tuple-element.29), channel_id=1, source_target_pairs={{4,0},{8,4},{12,8},{16,12},{20,16},{24,20},{28,24},{32,28},{36,32}... | collective-permute-start | bytes 291848 | tf_op jit(solution)/shard_map/ppermute | solution.py:512
  9.1 7.8 %evaluate_0.1 = (bf16[37,4,256,128]{3,2,1,0:T(8,128)(2,1)S(1)}, f32[21,16,256]{2,1,0:T(8,128)S(1)}) custom-call(bf16[96,16,128]{2,1,0:T(8,128)(2,1)S(1)} %get-tuple-element.23.listed_ref, f32[16,8,256]{2,1,0:T(8,128)S(1)} %get-tuple-element.24.pts_ref, bf16[16,256,48]{2,1,0:T(8,128)(2,1)S(1)} %get-tuple-element.25.cols_ref, ...), custom_call_target="tpu_custom_call" | custom-call | flops 9663676416 | bytes 9437184 | tf_op jit(solution)/shard_map/evaluate_0/pallas_call | solution.py:439
  16.9 0.0 collective-permute-done.rest_0_
  16.9 0.0 copy-start
  16.9 6.6 %evaluate_11.1 = (bf16[31,4,256,128]{3,2,1,0:T(8,128)(2,1)S(1)}, f32[21,16,256]{2,1,0:T(8,128)S(1)}, f32[16,1280]{1,0:T(8,128)S(1)}) custom-call(bf16[96,16,128]{2,1,0:T(8,128)(2,1)S(1)} %get-tuple-element.23.listed_ref, f32[16,8,256]{2,1,0:T(8,128)S(1)} %get-tuple-element.24.pts_ref, bf16[16,256,48]{2,1,0:T(8,128)(2,1)S(1)} %get-tuple-element.25.cols_ref, ...), custom_call_target="tpu_custom_call" | custom-call | flops 8053063680 | bytes 7864320 | tf_op jit(solution)/shard_map/evaluate_11/pallas_call | solution.py:439
  23.5 0.0 copy-start.1
  23.5 1.9 %collective-permute-start.1 = (f32[16,1280]{1,0:T(8,128)S(1)}, f32[16,1280]{1,0:T(8,128)S(1)}, u32[]{:S(2)}, u32[]{:S(2)}) collective-permute-start(f32[16,1280]{1,0:T(8,128)S(1)} %get-tuple-element.33), channel_id=1, source_target_pairs={{0,4},{4,8},{8,12},{12,16},{16,20},{20,24},{24,28},{28,32},{32,36}... | collective-permute-start | bytes 245768 | tf_op jit(solution)/shard_map/ppermute | solution.py:512
  25.5 0.0 copy-done
  25.5 6.6 %evaluate_6.1 = (bf16[31,4,256,128]{3,2,1,0:T(8,128)(2,1)S(1)}, f32[16,4096]{1,0:T(8,128)S(1)}) custom-call(bf16[96,16,128]{2,1,0:T(8,128)(2,1)S(1)} %get-tuple-element.23.listed_ref, f32[16,8,256]{2,1,0:T(8,128)S(1)} %get-tuple-element.24.pts_ref, bf16[16,256,48]{2,1,0:T(8,128)(2,1)S(1)} %get-tuple-element.25.cols_ref, ...), custom_call_target="tpu_custom_call" | custom-call | flops 8053063680 | bytes 7864320 | tf_op jit(solution)/shard_map/evaluate_6/pallas_call | solution.py:439
  32.1 0.0 collective-permute-done.1
  32.1 2.4 %collective-permute-start.2 = (f32[16,1280]{1,0:T(8,128)S(1)}, f32[16,1280]{1,0:T(8,128)S(1)}, u32[]{:S(2)}, u32[]{:S(2)}) collective-permute-start(f32[16,1280]{1,0:T(8,128)S(1)} %slice_add_fusion), channel_id=1, source_target_pairs={{4,0},{8,4},{12,8},{16,12},{20,16},{24,20},{28,24},{32,28},{36,32}... | collective-permute-start | bytes 245768 | tf_op jit(solution)/shard_map/ppermute | solution.py:512
  34.5 0.2 multiply_reduce_fusion.2
  34.7 4.5 %apply_0.1.prev_ref = f32[21,16,256]{2,1,0:T(8,128)S(1)} custom-call(bf16[96,16,128]{2,1,0:T(8,128)(2,1)S(1)} %get-tuple-element.23.listed_ref, bf16[37,4,256,128]{3,2,1,0:T(8,128)(2,1)S(1)} %get-tuple-element.36.tiles_ref, f32[16,4096]{1,0:T(8,128)S(1)} %get-tuple-element.53.w_ref), custom_call_target="tpu_custom_call" | custom-call | flops 4966055936 | bytes 9699328 | tf_op jit(solution)/shard_map/apply_0/pallas_call | solution.py:452
  39.2 0.0 collective-permute-done.2.far_ref.rest_0_
  39.2 0.0 copy-done.1
  39.2 1.8 %apply_edge.1 = (f32[21,16,256]{2,1,0:T(8,128)S(1)}, f32[16,1280]{1,0:T(8,128)S(1)}, f32[16,256]{1,0:T(8,128)S(1)}) custom-call(bf16[96,16,128]{2,1,0:T(8,128)(2,1)S(1)} %get-tuple-element.23.listed_ref, bf16[31,4,256,128]{3,2,1,0:T(8,128)(2,1)S(1)} %get-tuple-element.35.tiles_ref.tiles_hbm, f32[16,4096]{1,0:T(8,128)S(1)} %get-tuple-element.53.w_ref, ...), custom_call_target="tpu_custom_call" | custom-call | flops 4160749568 | bytes 8126464 | tf_op jit(solution)/shard_map/apply_edge/pallas_call | solution.py:452
  41.1 3.2 %collective-permute-start.3 = (f32[16,1280]{1,0:T(8,128)S(1)}, f32[16,1280]{1,0:T(8,128)S(1)}, u32[]{:S(2)}, u32[]{:S(2)}) collective-permute-start(f32[16,1280]{1,0:T(8,128)S(1)} %get-tuple-element.40), channel_id=1, source_target_pairs={{0,4},{4,8},{8,12},{12,16},{16,20},{20,24},{24,28},{28,32},{32,36}... | collective-permute-start | bytes 245768 | tf_op jit(solution)/shard_map/ppermute | solution.py:512
  44.2 3.8 %apply_6.1 = (f32[21,16,256]{2,1,0:T(8,128)S(1)}, f32[16,256]{1,0:T(8,128)S(1)}) custom-call(bf16[96,16,128]{2,1,0:T(8,128)(2,1)S(1)} %get-tuple-element.23.listed_ref, bf16[31,4,256,128]{3,2,1,0:T(8,128)(2,1)S(1)} %get-tuple-element.34.tiles_ref, f32[16,4096]{1,0:T(8,128)S(1)} %get-tuple-element.53.w_ref, ...), custom_call_target="tpu_custom_call" | custom-call | flops 4160749568 | bytes 8126464 | tf_op jit(solution)/shard_map/apply_6/pallas_call | solution.py:452
  48.0 0.0 collective-permute-done.3.back_ref
  48.0 0.1 reduce_sum.50
  48.1 0.1 collective-permute-start.4
  48.2 1.1 %collective-permute-done.4 = f32[4,16]{1,0:T(4,128)S(1)} collective-permute-done((f32[4,16]{1,0:T(4,128)S(1)}, f32[4,16]{1,0:T(4,128)S(1)}, u32[]{:S(2)}, u32[]{:S(2)}) %collective-permute-start.4) | collective-permute-done | bytes 288 | tf_op jit(solution)/shard_map/ppermute | solution.py:517
  49.4 0.1 broadcast_in_dim.4
  49.5 0.6 broadcast_in_dim.5
  50.1 13.4 %all-to-all-start = ((f32[32,1,64]{2,1,0:T(1,128)}), f32[32,1,64]{2,1,0:T(1,128)S(1)}, u32[]{:S(2)}, u32[]{:S(2)}) async-start(f32[32,1,64]{2,1,0:T(1,128)} %broadcast_in_dim.5), calls=%async_computation | async-start | bytes 32768 | tf_op jit(solution)/shard_map/all_to_all | solution.py:520
  63.5 5.7 %finish.1 = f32[16,4096]{1,0:T(8,128)S(1)} custom-call(bf16[96,16,128]{2,1,0:T(8,128)(2,1)S(1)} %get-tuple-element.23.listed_ref, bf16[31,4,256,128]{3,2,1,0:T(8,128)(2,1)} %copy-done.1, f32[16,4096]{1,0:T(8,128)S(1)} %get-tuple-element.53.w_ref, f32[16,1280]{1,0:T(8,128)S(1)} %collective-permute-done.2.far_ref.rest_0_, ...), custom_call_target="tpu_custom_call" | custom-call | flops 4160749568 | bytes 8126464 | tf_op jit(solution)/shard_map/finish/pallas_call | solution.py:452
  69.3 2.8 %all-to-all-done = f32[32,1,64]{2,1,0:T(1,128)S(1)} async-done(((f32[32,1,64]{2,1,0:T(1,128)}), f32[32,1,64]{2,1,0:T(1,128)S(1)}, u32[]{:S(2)}, u32[]{:S(2)}) %all-to-all-start) | async-done | bytes 8224 | tf_op jit(solution)/shard_map/all_to_all | solution.py:520
  72.1 0.1 multiply_add_fusion.1
  72.2 0.1 add_divide_fusion
  72.3 1.0 %multiply_subtract_fusion = (f32[16,4096]{1,0:T(8,128)}, f32[16,4096]{1,0:T(8,128)}) fusion(f32[16,4096]{1,0:T(8,128)S(1)} %finish.1, f32[16,4096]{1,0:T(8,128)S(1)} %copy-done, f32[16]{0:T(128)S(1)} %get-tuple-element.48, f32[16]{0:T(128)S(1)} %get-tuple-element.47, f32[16]{0:T(128)S(1)} %get-tuple-element.50, f32[16,2816]{1,0:T(8,128)S(1)} %slice.11, ...), kind=kLoop, calls=%fused_computation.1 | loop fusion | flops 851968 | bytes 1310912 | tf_op jit(solution)/shard_map/sub | solution.py:569
  (6 shorter events, 0.1 us)
Async XLA Ops:
  4.0 12.9 %collective-permute-start = (f32[19,1280]{1,0:T(8,128)S(1)}, f32[19,1280]{1,0:T(8,128)S(1)}, u32[]{:S(2)}, u32[]{:S(2)}) collective-permute-start(f32[19,1280]{1,0:T(8,128)S(1)} %get-tuple-element.29), channel_id=1, source_target_pairs={{4,0},{8,4},{12,8},{16,12},{20,16},{24,20},{28,24},{32,28},{36,32}... | collective-permute-start | bytes 291848 | tf_op jit(solution)/shard_map/ppermute | solution.py:512
  16.9 8.6 %copy-start = (f32[16,4096]{1,0:T(8,128)S(1)}, f32[16,4096]{1,0:T(8,128)}, u32[]{:S(2)}) copy-start(f32[16,4096]{1,0:T(8,128)} %rest_0_.1) | copy-start | bytes 786436
  23.5 15.7 %copy-start.1 = (bf16[31,4,256,128]{3,2,1,0:T(8,128)(2,1)}, bf16[31,4,256,128]{3,2,1,0:T(8,128)(2,1)S(1)}, u32[]{:S(2)}) copy-start(bf16[31,4,256,128]{3,2,1,0:T(8,128)(2,1)S(1)} %get-tuple-element.35.tiles_ref.tiles_hbm) | copy-start | bytes 24379396
  23.5 8.6 %collective-permute-start.1 = (f32[16,1280]{1,0:T(8,128)S(1)}, f32[16,1280]{1,0:T(8,128)S(1)}, u32[]{:S(2)}, u32[]{:S(2)}) collective-permute-start(f32[16,1280]{1,0:T(8,128)S(1)} %get-tuple-element.33), channel_id=1, source_target_pairs={{0,4},{4,8},{8,12},{12,16},{16,20},{20,24},{24,28},{28,32},{32,36}... | collective-permute-start | bytes 245768 | tf_op jit(solution)/shard_map/ppermute | solution.py:512
  32.1 7.1 %collective-permute-start.2 = (f32[16,1280]{1,0:T(8,128)S(1)}, f32[16,1280]{1,0:T(8,128)S(1)}, u32[]{:S(2)}, u32[]{:S(2)}) collective-permute-start(f32[16,1280]{1,0:T(8,128)S(1)} %slice_add_fusion), channel_id=1, source_target_pairs={{4,0},{8,4},{12,8},{16,12},{20,16},{24,20},{28,24},{32,28},{36,32}... | collective-permute-start | bytes 245768 | tf_op jit(solution)/shard_map/ppermute | solution.py:512
  41.1 6.9 %collective-permute-start.3 = (f32[16,1280]{1,0:T(8,128)S(1)}, f32[16,1280]{1,0:T(8,128)S(1)}, u32[]{:S(2)}, u32[]{:S(2)}) collective-permute-start(f32[16,1280]{1,0:T(8,128)S(1)} %get-tuple-element.40), channel_id=1, source_target_pairs={{0,4},{4,8},{8,12},{12,16},{16,20},{20,24},{24,28},{28,32},{32,36}... | collective-permute-start | bytes 245768 | tf_op jit(solution)/shard_map/ppermute | solution.py:512
  48.1 1.2 %collective-permute-start.4 = (f32[4,16]{1,0:T(4,128)S(1)}, f32[4,16]{1,0:T(4,128)S(1)}, u32[]{:S(2)}, u32[]{:S(2)}) collective-permute-start(f32[4,16]{1,0:T(4,128)S(1)} %pad_maximum_fusion.1), channel_id=1, source_target_pairs={{0,4},{4,0},{8,12},{12,8},{16,20},{20,16},{24,28},{28,24},{32,36},... | collective-permute-start | bytes 776 | tf_op jit(solution)/shard_map/ppermute | solution.py:517
  50.1 22.0 %all-to-all-start = ((f32[32,1,64]{2,1,0:T(1,128)}), f32[32,1,64]{2,1,0:T(1,128)S(1)}, u32[]{:S(2)}, u32[]{:S(2)}) async-start(f32[32,1,64]{2,1,0:T(1,128)} %broadcast_in_dim.5), calls=%async_computation | async-start | bytes 32768 | tf_op jit(solution)/shard_map/all_to_all | solution.py:520

commit v7 on v6

--- a/solution.py
+++ b/solution.py
@@ -88,17 +88,20 @@
         copy.wait()
     leaves = order_ref.shape[0]
     n = b_ref.shape[0]
-    sub = lax.broadcasted_iota(jnp.int32, (W, W), 0)
+    sub = lax.broadcasted_iota(jnp.int32, (W, W), 0).astype(jnp.float32).astype(jnp.bfloat16)
+    one, zero = jnp.ones((W, W), jnp.bfloat16), jnp.zeros((W, W), jnp.bfloat16)
     dot = functools.partial(jnp.dot, preferred_element_type=jnp.float32)
     top = lax.broadcasted_iota(jnp.int32, (8, W), 0) < 3
     pad = jnp.zeros((5, W), jnp.float32)
     wide = jnp.zeros((8, W), jnp.float32)
     for k in range(leaves):
         at = slice(k * W, (k + 1) * W)
-        sel = (sub == order_ref[k : k + 1, :]).astype(jnp.float32).astype(jnp.bfloat16)
-        parts = [dot(p, sel) for p in split3(coords_ref[:, at])]
-        got = parts[0] + parts[1] + parts[2]
-        point = jnp.concatenate([got, pad], axis=0)
+        order = order_ref[k : k + 1, :].astype(jnp.float32).astype(jnp.bfloat16)
+        sel = jnp.where(sub == jnp.broadcast_to(order, (W, W)), one, zero)
+        raw = jnp.concatenate([coords_ref[:, at], pad], axis=0)
+        parts = dot(jnp.concatenate(split3(raw), axis=0), sel)
+        point = parts[0:8] + parts[8:16] + parts[16:24]
+        got = point[0:3]
         center = jnp.broadcast_to(jnp.sum(point, axis=1, keepdims=True) * (1.0 / W), (8, W))
         pts_ref[k] = point
         center_ref[k] = center
@@ -107,9 +110,9 @@
         first = center if k == 0 else first
         far_off = jnp.abs(point - first) * (SCALE * COMPACT / RANGE)
         wide = jnp.maximum(wide, jnp.maximum(square, far_off))
-        one = jnp.where(lax.broadcasted_iota(jnp.int32, (8, W), 0) == 3, 1.0, 0.0)
+        unit = jnp.where(lax.broadcasted_iota(jnp.int32, (8, W), 0) == 3, 1.0, 0.0)
         stack = [hi, jnp.where(top, hi, mid), jnp.where(top, hi, lo)]
-        stack += [jnp.where(top, mid, one), jnp.where(top, mid, one), jnp.where(top, lo, one)]
+        stack += [jnp.where(top, mid, unit), jnp.where(top, mid, unit), jnp.where(top, lo, unit)]
         cols_ref[k] = jnp.transpose(jnp.concatenate(stack, axis=0)).astype(jnp.bfloat16)
         if k < REACH:
             edge_ref[0:n, at] = b_ref[:, at]
@@ -368,12 +371,15 @@
     for k in range(leaf_dev - i0):
         at = pl.ds(k * STEPS, STEPS)
         copies.append(pltpu.make_async_copy(tiles_hbm.at[pl.ds(k * STEPS + 1, STEPS)], tiles_ref.at[at], sems.at[k]))
-        copies[k].start()
+    copies[0].start()
     load_values(v_ref, w_ref.at[:, i0 * W :], leaf_dev - i0, 0)
     load_values(v_ref, far_ref, REACH, leaf_dev - i0)
     acc_ref[...] = prev_ref[...]
+    copies[1].start()
     for k, copy in enumerate(copies):
         copy.wait()
+        if k + 2 < len(copies):
+            copies[k + 2].start()
         total = None
         for d in range(STEPS):
             to_row = product(tiles_ref.at[k * STEPS + d], v_ref[k + d], listed_ref[(i0 + k) * STEPS + d], True)

time: 73.6 us -> 73 us (level)
  no operation moved by 1% of the time
where the time goes in v7:
time: 73 us; the launch traced here: 72.7 us
  Pallas kernels  38.9 us (53%)
  starting transfers between devices  26.2 us (36%)
  waiting for transfers between devices  3.92 us (5%)
  other arithmetic  1.52 us (2%)
  between operations  1.42 us (2%)
  local copies, waits for them, and re-layouts  0.73 us (1%)
    pallas_call x3, Pallas kernels, evaluate_call(): pl.pallas_call(functools.partial(evaluate_kernel, i0, i1, leaf_dev, last)...  21 us
    pallas_call x4, Pallas kernels, small_call(): pl.pallas_call(kernel, out_shape=[jax.ShapeDtypeStruct(shape, jnp.float32...  15.8 us
    all_to_all x1, starting transfers between devices, sum_over_leaf(): lax.all_to_all(copies, 'leaf', split_axis=0, concat_axis=0, tiled=True, a...  13.4 us
    ppermute x4, starting transfers between devices, shift(): lax.ppermute(value, 'leaf', [(i, i + by) for i in range(length) if 0 <= i...  12.6 us
    all_to_all x1, waiting for transfers between devices, sum_over_leaf(): lax.all_to_all(copies, 'leaf', split_axis=0, concat_axis=0, tiled=True, a...  2.76 us
    pallas_call x1, Pallas kernels, prepare_call(): pl.pallas_call(prepare_kernel, out_shape=(jax.ShapeDtypeStruct((pairs.sha...  2.09 us
  transfers between devices with their start and end apart: 6, of which 2 were waited for; matrix products, arithmetic and copies ran while one was open for 0% of the time, Pallas kernels for 39%

profile of v7, /device:TPU:1, one launch (start us, length us, event | category | flops | bytes accessed | tf_op | source)
XLA Modules:
  0.0 72.7 jit_solution(9870138425361388837)
XLA Ops:
  1.3 2.1 %prepare.1 = (bf16[96,16,128]{2,1,0:T(8,128)(2,1)S(1)}, f32[16,8,256]{2,1,0:T(8,128)S(1)}, bf16[16,256,48]{2,1,0:T(8,128)(2,1)S(1)}, bf16[16,32,256]{2,1,0:T(8,1...) custom-call(s32[1]{0:T(128)S(6)} %copy.8.count_ref, s32[1]{0:T(128)} %bitcast.1.base_ref, ...), custom_call_target="tpu_custom_call" | custom-call | tf_op jit(solution)/shard_map/prepare/pallas_call | solution.py:401
  3.4 5.2 %collective-permute-start = (f32[19,1280]{1,0:T(8,128)S(1)}, f32[19,1280]{1,0:T(8,128)S(1)}, u32[]{:S(2)}, u32[]{:S(2)}) collective-permute-start(f32[19,1280]{1,0:T(8,128)S(1)} %get-tuple-element.29), channel_id=1, source_target_pairs={{4,0},{8,4},{12,8},{16,12},{20,16},{24,20},{28,24},{32,28},{36,32}... | collective-permute-start | bytes 291848 | tf_op jit(solution)/shard_map/ppermute | solution.py:518
  8.5 7.8 %evaluate_0.1 = (bf16[37,4,256,128]{3,2,1,0:T(8,128)(2,1)S(1)}, f32[21,16,256]{2,1,0:T(8,128)S(1)}) custom-call(bf16[96,16,128]{2,1,0:T(8,128)(2,1)S(1)} %get-tuple-element.23.listed_ref, f32[16,8,256]{2,1,0:T(8,128)S(1)} %get-tuple-element.24.pts_ref, bf16[16,256,48]{2,1,0:T(8,128)(2,1)S(1)} %get-tuple-element.25.cols_ref, ...), custom_call_target="tpu_custom_call" | custom-call | flops 9663676416 | bytes 9437184 | tf_op jit(solution)/shard_map/evaluate_0/pallas_call | solution.py:445
  16.3 0.0 collective-permute-done.rest_0_
  16.3 0.0 copy-start
  16.3 6.6 %evaluate_11.1 = (bf16[31,4,256,128]{3,2,1,0:T(8,128)(2,1)S(1)}, f32[21,16,256]{2,1,0:T(8,128)S(1)}, f32[16,1280]{1,0:T(8,128)S(1)}) custom-call(bf16[96,16,128]{2,1,0:T(8,128)(2,1)S(1)} %get-tuple-element.23.listed_ref, f32[16,8,256]{2,1,0:T(8,128)S(1)} %get-tuple-element.24.pts_ref, bf16[16,256,48]{2,1,0:T(8,128)(2,1)S(1)} %get-tuple-element.25.cols_ref, ...), custom_call_target="tpu_custom_call" | custom-call | flops 8053063680 | bytes 7864320 | tf_op jit(solution)/shard_map/evaluate_11/pallas_call | solution.py:445
  22.9 0.0 copy-start.1
  22.9 1.9 %collective-permute-start.1 = (f32[16,1280]{1,0:T(8,128)S(1)}, f32[16,1280]{1,0:T(8,128)S(1)}, u32[]{:S(2)}, u32[]{:S(2)}) collective-permute-start(f32[16,1280]{1,0:T(8,128)S(1)} %get-tuple-element.33), channel_id=1, source_target_pairs={{0,4},{4,8},{8,12},{12,16},{16,20},{20,24},{24,28},{28,32},{32,36}... | collective-permute-start | bytes 245768 | tf_op jit(solution)/shard_map/ppermute | solution.py:518
  24.9 0.0 copy-done
  24.9 6.6 %evaluate_6.1 = (bf16[31,4,256,128]{3,2,1,0:T(8,128)(2,1)S(1)}, f32[16,4096]{1,0:T(8,128)S(1)}) custom-call(bf16[96,16,128]{2,1,0:T(8,128)(2,1)S(1)} %get-tuple-element.23.listed_ref, f32[16,8,256]{2,1,0:T(8,128)S(1)} %get-tuple-element.24.pts_ref, bf16[16,256,48]{2,1,0:T(8,128)(2,1)S(1)} %get-tuple-element.25.cols_ref, ...), custom_call_target="tpu_custom_call" | custom-call | flops 8053063680 | bytes 7864320 | tf_op jit(solution)/shard_map/evaluate_6/pallas_call | solution.py:445
  31.5 0.0 collective-permute-done.1
  31.5 2.4 %collective-permute-start.2 = (f32[16,1280]{1,0:T(8,128)S(1)}, f32[16,1280]{1,0:T(8,128)S(1)}, u32[]{:S(2)}, u32[]{:S(2)}) collective-permute-start(f32[16,1280]{1,0:T(8,128)S(1)} %slice_add_fusion), channel_id=1, source_target_pairs={{4,0},{8,4},{12,8},{16,12},{20,16},{24,20},{28,24},{32,28},{36,32}... | collective-permute-start | bytes 245768 | tf_op jit(solution)/shard_map/ppermute | solution.py:518
  34.0 0.2 multiply_reduce_fusion.2
  34.2 4.5 %apply_0.1.prev_ref = f32[21,16,256]{2,1,0:T(8,128)S(1)} custom-call(bf16[96,16,128]{2,1,0:T(8,128)(2,1)S(1)} %get-tuple-element.23.listed_ref, bf16[37,4,256,128]{3,2,1,0:T(8,128)(2,1)S(1)} %get-tuple-element.36.tiles_ref, f32[16,4096]{1,0:T(8,128)S(1)} %get-tuple-element.53.w_ref), custom_call_target="tpu_custom_call" | custom-call | flops 4966055936 | bytes 9699328 | tf_op jit(solution)/shard_map/apply_0/pallas_call | solution.py:458
  38.6 0.0 collective-permute-done.2.far_ref.rest_0_
  38.6 0.0 copy-done.1
  38.6 1.8 %apply_edge.1 = (f32[21,16,256]{2,1,0:T(8,128)S(1)}, f32[16,1280]{1,0:T(8,128)S(1)}, f32[16,256]{1,0:T(8,128)S(1)}) custom-call(bf16[96,16,128]{2,1,0:T(8,128)(2,1)S(1)} %get-tuple-element.23.listed_ref, bf16[31,4,256,128]{3,2,1,0:T(8,128)(2,1)S(1)} %get-tuple-element.35.tiles_ref.tiles_hbm, f32[16,4096]{1,0:T(8,128)S(1)} %get-tuple-element.53.w_ref, ...), custom_call_target="tpu_custom_call" | custom-call | flops 4160749568 | bytes 8126464 | tf_op jit(solution)/shard_map/apply_edge/pallas_call | solution.py:458
  40.5 3.2 %collective-permute-start.3 = (f32[16,1280]{1,0:T(8,128)S(1)}, f32[16,1280]{1,0:T(8,128)S(1)}, u32[]{:S(2)}, u32[]{:S(2)}) collective-permute-start(f32[16,1280]{1,0:T(8,128)S(1)} %get-tuple-element.40), channel_id=1, source_target_pairs={{0,4},{4,8},{8,12},{12,16},{16,20},{20,24},{24,28},{28,32},{32,36}... | collective-permute-start | bytes 245768 | tf_op jit(solution)/shard_map/ppermute | solution.py:518
  43.6 3.8 %apply_6.1 = (f32[21,16,256]{2,1,0:T(8,128)S(1)}, f32[16,256]{1,0:T(8,128)S(1)}) custom-call(bf16[96,16,128]{2,1,0:T(8,128)(2,1)S(1)} %get-tuple-element.23.listed_ref, bf16[31,4,256,128]{3,2,1,0:T(8,128)(2,1)S(1)} %get-tuple-element.34.tiles_ref, f32[16,4096]{1,0:T(8,128)S(1)} %get-tuple-element.53.w_ref, ...), custom_call_target="tpu_custom_call" | custom-call | flops 4160749568 | bytes 8126464 | tf_op jit(solution)/shard_map/apply_6/pallas_call | solution.py:458
  47.4 0.0 collective-permute-done.3.back_ref
  47.4 0.1 reduce_sum.50
  47.5 0.1 collective-permute-start.4
  47.7 1.1 %collective-permute-done.4 = f32[4,16]{1,0:T(4,128)S(1)} collective-permute-done((f32[4,16]{1,0:T(4,128)S(1)}, f32[4,16]{1,0:T(4,128)S(1)}, u32[]{:S(2)}, u32[]{:S(2)}) %collective-permute-start.4) | collective-permute-done | bytes 288 | tf_op jit(solution)/shard_map/ppermute | solution.py:523
  48.8 0.1 broadcast_in_dim.4
  48.9 0.6 broadcast_in_dim.5
  49.5 13.4 %all-to-all-start = ((f32[32,1,64]{2,1,0:T(1,128)}), f32[32,1,64]{2,1,0:T(1,128)S(1)}, u32[]{:S(2)}, u32[]{:S(2)}) async-start(f32[32,1,64]{2,1,0:T(1,128)} %broadcast_in_dim.5), calls=%async_computation | async-start | bytes 32768 | tf_op jit(solution)/shard_map/all_to_all | solution.py:526
  62.9 5.8 %finish.1 = f32[16,4096]{1,0:T(8,128)S(1)} custom-call(bf16[96,16,128]{2,1,0:T(8,128)(2,1)S(1)} %get-tuple-element.23.listed_ref, bf16[31,4,256,128]{3,2,1,0:T(8,128)(2,1)} %copy-done.1, f32[16,4096]{1,0:T(8,128)S(1)} %get-tuple-element.53.w_ref, f32[16,1280]{1,0:T(8,128)S(1)} %collective-permute-done.2.far_ref.rest_0_, ...), custom_call_target="tpu_custom_call" | custom-call | flops 4160749568 | bytes 8126464 | tf_op jit(solution)/shard_map/finish/pallas_call | solution.py:458
  68.7 2.8 %all-to-all-done = f32[32,1,64]{2,1,0:T(1,128)S(1)} async-done(((f32[32,1,64]{2,1,0:T(1,128)}), f32[32,1,64]{2,1,0:T(1,128)S(1)}, u32[]{:S(2)}, u32[]{:S(2)}) %all-to-all-start) | async-done | bytes 8224 | tf_op jit(solution)/shard_map/all_to_all | solution.py:526
  71.5 0.1 multiply_add_fusion.1
  71.6 0.1 add_divide_fusion
  71.7 1.0 %multiply_subtract_fusion = (f32[16,4096]{1,0:T(8,128)}, f32[16,4096]{1,0:T(8,128)}) fusion(f32[16,4096]{1,0:T(8,128)S(1)} %finish.1, f32[16,4096]{1,0:T(8,128)S(1)} %copy-done, f32[16]{0:T(128)S(1)} %get-tuple-element.48, f32[16]{0:T(128)S(1)} %get-tuple-element.47, f32[16]{0:T(128)S(1)} %get-tuple-element.50, f32[16,2816]{1,0:T(8,128)S(1)} %slice.11, ...), kind=kLoop, calls=%fused_computation.1 | loop fusion | flops 851968 | bytes 1310912 | tf_op jit(solution)/shard_map/sub | solution.py:575
  (6 shorter events, 0.1 us)
Async XLA Ops:
  3.4 12.9 %collective-permute-start = (f32[19,1280]{1,0:T(8,128)S(1)}, f32[19,1280]{1,0:T(8,128)S(1)}, u32[]{:S(2)}, u32[]{:S(2)}) collective-permute-start(f32[19,1280]{1,0:T(8,128)S(1)} %get-tuple-element.29), channel_id=1, source_target_pairs={{4,0},{8,4},{12,8},{16,12},{20,16},{24,20},{28,24},{32,28},{36,32}... | collective-permute-start | bytes 291848 | tf_op jit(solution)/shard_map/ppermute | solution.py:518
  16.3 8.6 %copy-start = (f32[16,4096]{1,0:T(8,128)S(1)}, f32[16,4096]{1,0:T(8,128)}, u32[]{:S(2)}) copy-start(f32[16,4096]{1,0:T(8,128)} %rest_0_.1) | copy-start | bytes 786436
  22.9 15.7 %copy-start.1 = (bf16[31,4,256,128]{3,2,1,0:T(8,128)(2,1)}, bf16[31,4,256,128]{3,2,1,0:T(8,128)(2,1)S(1)}, u32[]{:S(2)}) copy-start(bf16[31,4,256,128]{3,2,1,0:T(8,128)(2,1)S(1)} %get-tuple-element.35.tiles_ref.tiles_hbm) | copy-start | bytes 24379396
  22.9 8.6 %collective-permute-start.1 = (f32[16,1280]{1,0:T(8,128)S(1)}, f32[16,1280]{1,0:T(8,128)S(1)}, u32[]{:S(2)}, u32[]{:S(2)}) collective-permute-start(f32[16,1280]{1,0:T(8,128)S(1)} %get-tuple-element.33), channel_id=1, source_target_pairs={{0,4},{4,8},{8,12},{12,16},{16,20},{20,24},{24,28},{28,32},{32,36}... | collective-permute-start | bytes 245768 | tf_op jit(solution)/shard_map/ppermute | solution.py:518
  31.5 7.1 %collective-permute-start.2 = (f32[16,1280]{1,0:T(8,128)S(1)}, f32[16,1280]{1,0:T(8,128)S(1)}, u32[]{:S(2)}, u32[]{:S(2)}) collective-permute-start(f32[16,1280]{1,0:T(8,128)S(1)} %slice_add_fusion), channel_id=1, source_target_pairs={{4,0},{8,4},{12,8},{16,12},{20,16},{24,20},{28,24},{32,28},{36,32}... | collective-permute-start | bytes 245768 | tf_op jit(solution)/shard_map/ppermute | solution.py:518
  40.5 6.9 %collective-permute-start.3 = (f32[16,1280]{1,0:T(8,128)S(1)}, f32[16,1280]{1,0:T(8,128)S(1)}, u32[]{:S(2)}, u32[]{:S(2)}) collective-permute-start(f32[16,1280]{1,0:T(8,128)S(1)} %get-tuple-element.40), channel_id=1, source_target_pairs={{0,4},{4,8},{8,12},{12,16},{16,20},{20,24},{24,28},{28,32},{32,36}... | collective-permute-start | bytes 245768 | tf_op jit(solution)/shard_map/ppermute | solution.py:518
  47.5 1.2 %collective-permute-start.4 = (f32[4,16]{1,0:T(4,128)S(1)}, f32[4,16]{1,0:T(4,128)S(1)}, u32[]{:S(2)}, u32[]{:S(2)}) collective-permute-start(f32[4,16]{1,0:T(4,128)S(1)} %pad_maximum_fusion.1), channel_id=1, source_target_pairs={{0,4},{4,0},{8,12},{12,8},{16,20},{20,16},{24,28},{28,24},{32,36},... | collective-permute-start | bytes 776 | tf_op jit(solution)/shard_map/ppermute | solution.py:523
  49.5 22.0 %all-to-all-start = ((f32[32,1,64]{2,1,0:T(1,128)}), f32[32,1,64]{2,1,0:T(1,128)S(1)}, u32[]{:S(2)}, u32[]{:S(2)}) async-start(f32[32,1,64]{2,1,0:T(1,128)} %broadcast_in_dim.5), calls=%async_computation | async-start | bytes 32768 | tf_op jit(solution)/shard_map/all_to_all | solution.py:526

commit v8 on v7

--- a/solution.py
+++ b/solution.py
@@ -365,7 +365,7 @@
 
 
 def finish_kernel(
-    i0, leaf_dev, listed_ref, tiles_hbm, w_ref, far_ref, prev_ref, back_ref, rows_ref, v_ref, acc_ref, tiles_ref, sems
+    i0, leaf_dev, listed_ref, tiles_hbm, w_ref, far_ref, prev_ref, rows_ref, v_ref, acc_ref, tiles_ref, sems
 ):
     copies = []
     for k in range(leaf_dev - i0):
@@ -386,7 +386,6 @@
             total = to_row if total is None else total + to_row
         acc_ref[i0 + k] += total
     put_rows(rows_ref, acc_ref, 0, leaf_dev, w_ref)
-    rows_ref[:, 0 : REACH * W] += back_ref[...]
 
 
 VM = pl.BlockSpec(memory_space=pltpu.VMEM)
@@ -495,7 +494,7 @@
     )
 
 
-def finish_call(i0, leaf_dev, n, listed, tiles, own, far, prev, back):
+def finish_call(i0, leaf_dev, n, listed, tiles, own, far, prev):
     acc = (leaf_dev + REACH, n, W)
     return small_call(
         functools.partial(finish_kernel, i0, leaf_dev),
@@ -508,7 +507,7 @@
             pltpu.SemaphoreType.DMA((leaf_dev - i0,)),
         ],
         tiles,
-        [listed, tiles, own, far, prev, back],
+        [listed, tiles, own, far, prev],
         in_hbm=(1,),
     )[0]
 
@@ -550,7 +549,6 @@
     acc, send, edge_dots = edge_call(cut1, tiles=tiles1, far=image_far, prev=acc, **common)
     back = shift(send, 1)
     acc, dots = apply_call(cut0, cut1, tiles=tiles2, last=(image_far, edge_dots), prev=acc, **common)
-    dots, back = lax.optimization_barrier((dots, back))
     square = jnp.sum(image * image, axis=1)
     sums = jnp.stack(
         [
@@ -560,7 +558,8 @@
             jnp.sum(dots, axis=1) + NUGGET * square,
         ]
     )
-    image2 = finish_call(cut1, tiles=tiles1, far=image_far, prev=acc, back=back, **common)
+    image2 = finish_call(cut1, tiles=tiles1, far=image_far, prev=acc, **common)
+    image2 = jnp.concatenate([image2[:, :edge] + back, image2[:, edge:]], axis=1)
     rr, bw, ww, wz = sum_over_leaf(sums)
     alpha = rr / bw
     rr1 = rr - 2.0 * alpha * bw + alpha * alpha * ww

time: 73 us -> 71.8 us (0.984)
  waiting for transfers between devices: 3.92 us -> 2.76 us
    ppermute x1, waiting for transfers between devices: 1.14 us -> 0.01 us  [sum_over_leaf(): lax.ppermute(value, 'leaf', [(i, i ^ 1) for i in range(length)])]
  transfers between devices with their start and end apart: 6 -> 6, of which waited for: 2 -> 1; matrix products, arithmetic and copies ran while one was open for 0% -> 2% of each run, Pallas kernels for 39% -> 34%
where the time goes in v8:
time: 71.8 us; the launch traced here: 71.5 us
  Pallas kernels  38.9 us (54%)
  starting transfers between devices  26.2 us (36%)
  waiting for transfers between devices  2.76 us (4%)
  other arithmetic  1.53 us (2%)
  between operations  1.44 us (2%)
  local copies, waits for them, and re-layouts  0.74 us (1%)
    pallas_call x3, Pallas kernels, evaluate_call(): pl.pallas_call(functools.partial(evaluate_kernel, i0, i1, leaf_dev, last)...  21 us
    pallas_call x4, Pallas kernels, small_call(): pl.pallas_call(kernel, out_shape=[jax.ShapeDtypeStruct(shape, jnp.float32...  15.8 us
    all_to_all x1, starting transfers between devices, sum_over_leaf(): lax.all_to_all(copies, 'leaf', split_axis=0, concat_axis=0, tiled=True, a...  13.4 us
    ppermute x4, starting transfers between devices, shift(): lax.ppermute(value, 'leaf', [(i, i + by) for i in range(length) if 0 <= i...  12.7 us
    all_to_all x1, waiting for transfers between devices, sum_over_leaf(): lax.all_to_all(copies, 'leaf', split_axis=0, concat_axis=0, tiled=True, a...  2.75 us
    pallas_call x1, Pallas kernels, prepare_call(): pl.pallas_call(prepare_kernel, out_shape=(jax.ShapeDtypeStruct((pairs.sha...  2.09 us
  transfers between devices with their start and end apart: 6, of which 1 were waited for; matrix products, arithmetic and copies ran while one was open for 2% of the time, Pallas kernels for 34%

profile of v8, /device:TPU:1, one launch (start us, length us, event | category | flops | bytes accessed | tf_op | source)
XLA Modules:
  0.0 71.5 jit_solution(17071033642320018014)
XLA Ops:
  1.3 2.1 %prepare.1 = (bf16[96,16,128]{2,1,0:T(8,128)(2,1)S(1)}, f32[16,8,256]{2,1,0:T(8,128)S(1)}, bf16[16,256,48]{2,1,0:T(8,128)(2,1)S(1)}, bf16[16,32,256]{2,1,0:T(8,1...) custom-call(s32[1]{0:T(128)S(6)} %copy.8.count_ref, s32[1]{0:T(128)} %bitcast.1.base_ref, ...), custom_call_target="tpu_custom_call" | custom-call | tf_op jit(solution)/shard_map/prepare/pallas_call | solution.py:400
  3.4 5.2 %collective-permute-start = (f32[19,1280]{1,0:T(8,128)S(1)}, f32[19,1280]{1,0:T(8,128)S(1)}, u32[]{:S(2)}, u32[]{:S(2)}) collective-permute-start(f32[19,1280]{1,0:T(8,128)S(1)} %get-tuple-element.27), channel_id=1, source_target_pairs={{4,0},{8,4},{12,8},{16,12},{20,16},{24,20},{28,24},{32,28},{36,32}... | collective-permute-start | bytes 291848 | tf_op jit(solution)/shard_map/ppermute | solution.py:517
  8.5 7.8 %evaluate_0.1 = (bf16[37,4,256,128]{3,2,1,0:T(8,128)(2,1)S(1)}, f32[21,16,256]{2,1,0:T(8,128)S(1)}) custom-call(bf16[96,16,128]{2,1,0:T(8,128)(2,1)S(1)} %get-tuple-element.21.listed_ref, f32[16,8,256]{2,1,0:T(8,128)S(1)} %get-tuple-element.22.pts_ref, bf16[16,256,48]{2,1,0:T(8,128)(2,1)S(1)} %get-tuple-element.23.cols_ref, ...), custom_call_target="tpu_custom_call" | custom-call | flops 9663676416 | bytes 9437184 | tf_op jit(solution)/shard_map/evaluate_0/pallas_call | solution.py:444
  16.3 0.0 collective-permute-done.rest_0_
  16.3 0.0 copy-start
  16.3 6.6 %evaluate_11.1 = (bf16[31,4,256,128]{3,2,1,0:T(8,128)(2,1)S(1)}, f32[21,16,256]{2,1,0:T(8,128)S(1)}, f32[16,1280]{1,0:T(8,128)S(1)}) custom-call(bf16[96,16,128]{2,1,0:T(8,128)(2,1)S(1)} %get-tuple-element.21.listed_ref, f32[16,8,256]{2,1,0:T(8,128)S(1)} %get-tuple-element.22.pts_ref, bf16[16,256,48]{2,1,0:T(8,128)(2,1)S(1)} %get-tuple-element.23.cols_ref, ...), custom_call_target="tpu_custom_call" | custom-call | flops 8053063680 | bytes 7864320 | tf_op jit(solution)/shard_map/evaluate_11/pallas_call | solution.py:444
  22.9 0.0 copy-start.1
  22.9 1.9 %collective-permute-start.1 = (f32[16,1280]{1,0:T(8,128)S(1)}, f32[16,1280]{1,0:T(8,128)S(1)}, u32[]{:S(2)}, u32[]{:S(2)}) collective-permute-start(f32[16,1280]{1,0:T(8,128)S(1)} %get-tuple-element.31), channel_id=1, source_target_pairs={{0,4},{4,8},{8,12},{12,16},{16,20},{20,24},{24,28},{28,32},{32,36}... | collective-permute-start | bytes 245768 | tf_op jit(solution)/shard_map/ppermute | solution.py:517
  24.9 0.0 copy-done
  24.9 6.6 %evaluate_6.1 = (bf16[31,4,256,128]{3,2,1,0:T(8,128)(2,1)S(1)}, f32[16,4096]{1,0:T(8,128)S(1)}) custom-call(bf16[96,16,128]{2,1,0:T(8,128)(2,1)S(1)} %get-tuple-element.21.listed_ref, f32[16,8,256]{2,1,0:T(8,128)S(1)} %get-tuple-element.22.pts_ref, bf16[16,256,48]{2,1,0:T(8,128)(2,1)S(1)} %get-tuple-element.23.cols_ref, ...), custom_call_target="tpu_custom_call" | custom-call | flops 8053063680 | bytes 7864320 | tf_op jit(solution)/shard_map/evaluate_6/pallas_call | solution.py:444
  31.5 0.0 collective-permute-done.1
  31.5 2.4 %collective-permute-start.2 = (f32[16,1280]{1,0:T(8,128)S(1)}, f32[16,1280]{1,0:T(8,128)S(1)}, u32[]{:S(2)}, u32[]{:S(2)}) collective-permute-start(f32[16,1280]{1,0:T(8,128)S(1)} %slice_add_fusion.1), channel_id=1, source_target_pairs={{4,0},{8,4},{12,8},{16,12},{20,16},{24,20},{28,24},{32,28},{36,32}... | collective-permute-start | bytes 245768 | tf_op jit(solution)/shard_map/ppermute | solution.py:517
  34.0 0.2 multiply_reduce_fusion.2
  34.2 4.5 %apply_0.1.prev_ref = f32[21,16,256]{2,1,0:T(8,128)S(1)} custom-call(bf16[96,16,128]{2,1,0:T(8,128)(2,1)S(1)} %get-tuple-element.21.listed_ref, bf16[37,4,256,128]{3,2,1,0:T(8,128)(2,1)S(1)} %get-tuple-element.34.tiles_ref, f32[16,4096]{1,0:T(8,128)S(1)} %get-tuple-element.49.w_ref), custom_call_target="tpu_custom_call" | custom-call | flops 4966055936 | bytes 9699328 | tf_op jit(solution)/shard_map/apply_0/pallas_call | solution.py:457
  38.6 0.0 collective-permute-done.2.far_ref.rest_0_
  38.6 0.0 copy-done.1
  38.6 1.8 %apply_edge.1 = (f32[21,16,256]{2,1,0:T(8,128)S(1)}, f32[16,1280]{1,0:T(8,128)S(1)}, f32[16,256]{1,0:T(8,128)S(1)}) custom-call(bf16[96,16,128]{2,1,0:T(8,128)(2,1)S(1)} %get-tuple-element.21.listed_ref, bf16[31,4,256,128]{3,2,1,0:T(8,128)(2,1)S(1)} %get-tuple-element.33.tiles_ref.tiles_hbm, f32[16,4096]{1,0:T(8,128)S(1)} %get-tuple-element.49.w_ref, ...), custom_call_target="tpu_custom_call" | custom-call | flops 4160749568 | bytes 8126464 | tf_op jit(solution)/shard_map/apply_edge/pallas_call | solution.py:457
  40.5 3.8 %apply_6.1 = (f32[21,16,256]{2,1,0:T(8,128)S(1)}, f32[16,256]{1,0:T(8,128)S(1)}) custom-call(bf16[96,16,128]{2,1,0:T(8,128)(2,1)S(1)} %get-tuple-element.21.listed_ref, bf16[31,4,256,128]{3,2,1,0:T(8,128)(2,1)S(1)} %get-tuple-element.32.tiles_ref, f32[16,4096]{1,0:T(8,128)S(1)} %get-tuple-element.49.w_ref, ...), custom_call_target="tpu_custom_call" | custom-call | flops 4160749568 | bytes 8126464 | tf_op jit(solution)/shard_map/apply_6/pallas_call | solution.py:457
  44.2 0.1 reduce_sum.50
  44.4 0.1 collective-permute-start.3
  44.5 3.2 %collective-permute-start.4 = (f32[16,1280]{1,0:T(8,128)S(1)}, f32[16,1280]{1,0:T(8,128)S(1)}, u32[]{:S(2)}, u32[]{:S(2)}) collective-permute-start(f32[16,1280]{1,0:T(8,128)S(1)} %get-tuple-element.39), channel_id=1, source_target_pairs={{0,4},{4,8},{8,12},{12,16},{16,20},{20,24},{24,28},{28,32},{32,36}... | collective-permute-start | bytes 245768 | tf_op jit(solution)/shard_map/ppermute | solution.py:517
  47.7 0.0 collective-permute-done.3
  47.7 0.1 broadcast_in_dim.4
  47.8 0.6 broadcast_in_dim.5
  48.4 13.4 %all-to-all-start = ((f32[32,1,64]{2,1,0:T(1,128)}), f32[32,1,64]{2,1,0:T(1,128)S(1)}, u32[]{:S(2)}, u32[]{:S(2)}) async-start(f32[32,1,64]{2,1,0:T(1,128)} %broadcast_in_dim.5), calls=%async_computation | async-start | bytes 32768 | tf_op jit(solution)/shard_map/all_to_all | solution.py:525
  61.8 5.8 %finish.1 = f32[16,4096]{1,0:T(8,128)S(1)} custom-call(bf16[96,16,128]{2,1,0:T(8,128)(2,1)S(1)} %get-tuple-element.21.listed_ref, bf16[31,4,256,128]{3,2,1,0:T(8,128)(2,1)} %copy-done.1, f32[16,4096]{1,0:T(8,128)S(1)} %get-tuple-element.49.w_ref, f32[16,1280]{1,0:T(8,128)S(1)} %collective-permute-done.2.far_ref.rest_0_, ...), custom_call_target="tpu_custom_call" | custom-call | flops 4160749568 | bytes 8126464 | tf_op jit(solution)/shard_map/finish/pallas_call | solution.py:457
  67.6 2.8 %all-to-all-done = f32[32,1,64]{2,1,0:T(1,128)S(1)} async-done(((f32[32,1,64]{2,1,0:T(1,128)}), f32[32,1,64]{2,1,0:T(1,128)S(1)}, u32[]{:S(2)}, u32[]{:S(2)}) %all-to-all-start) | async-done | bytes 8224 | tf_op jit(solution)/shard_map/all_to_all | solution.py:525
  70.4 0.1 multiply_add_fusion.1
  70.5 0.1 add_divide_fusion
  70.5 0.0 collective-permute-done.4
  70.6 1.0 %fusion.2 = (f32[16,4096]{1,0:T(8,128)}, f32[16,4096]{1,0:T(8,128)}) fusion(f32[16,2816]{1,0:T(8,128)S(1)} %slice.21, f32[16,1280]{1,0:T(8,128)S(1)} %slice_add_fusion, f32[16,4096]{1,0:T(8,128)S(1)} %copy-done, f32[16]{0:T(128)S(1)} %get-tuple-element.44, f32[16]{0:T(128)S(1)} %get-tuple-element.43, f32[16]{0:T(128)S(1)} %get-tuple-element.46, ...), kind=kLoop, calls=%fused_computation.4 | loop fusion | flops 917504 | bytes 1310912 | tf_op jit(solution)/shard_map/sub | solution.py:574
  (8 shorter events, 0.1 us)
Async XLA Ops:
  3.4 12.9 %collective-permute-start = (f32[19,1280]{1,0:T(8,128)S(1)}, f32[19,1280]{1,0:T(8,128)S(1)}, u32[]{:S(2)}, u32[]{:S(2)}) collective-permute-start(f32[19,1280]{1,0:T(8,128)S(1)} %get-tuple-element.27), channel_id=1, source_target_pairs={{4,0},{8,4},{12,8},{16,12},{20,16},{24,20},{28,24},{32,28},{36,32}... | collective-permute-start | bytes 291848 | tf_op jit(solution)/shard_map/ppermute | solution.py:517
  16.3 8.6 %copy-start = (f32[16,4096]{1,0:T(8,128)S(1)}, f32[16,4096]{1,0:T(8,128)}, u32[]{:S(2)}) copy-start(f32[16,4096]{1,0:T(8,128)} %rest_0_.1) | copy-start | bytes 786436
  22.9 15.7 %copy-start.1 = (bf16[31,4,256,128]{3,2,1,0:T(8,128)(2,1)}, bf16[31,4,256,128]{3,2,1,0:T(8,128)(2,1)S(1)}, u32[]{:S(2)}) copy-start(bf16[31,4,256,128]{3,2,1,0:T(8,128)(2,1)S(1)} %get-tuple-element.33.tiles_ref.tiles_hbm) | copy-start | bytes 24379396
  22.9 8.6 %collective-permute-start.1 = (f32[16,1280]{1,0:T(8,128)S(1)}, f32[16,1280]{1,0:T(8,128)S(1)}, u32[]{:S(2)}, u32[]{:S(2)}) collective-permute-start(f32[16,1280]{1,0:T(8,128)S(1)} %get-tuple-element.31), channel_id=1, source_target_pairs={{0,4},{4,8},{8,12},{12,16},{16,20},{20,24},{24,28},{28,32},{32,36}... | collective-permute-start | bytes 245768 | tf_op jit(solution)/shard_map/ppermute | solution.py:517
  31.5 7.1 %collective-permute-start.2 = (f32[16,1280]{1,0:T(8,128)S(1)}, f32[16,1280]{1,0:T(8,128)S(1)}, u32[]{:S(2)}, u32[]{:S(2)}) collective-permute-start(f32[16,1280]{1,0:T(8,128)S(1)} %slice_add_fusion.1), channel_id=1, source_target_pairs={{4,0},{8,4},{12,8},{16,12},{20,16},{24,20},{28,24},{32,28},{36,32}... | collective-permute-start | bytes 245768 | tf_op jit(solution)/shard_map/ppermute | solution.py:517
  44.4 3.3 %collective-permute-start.3 = (f32[4,16]{1,0:T(4,128)S(1)}, f32[4,16]{1,0:T(4,128)S(1)}, u32[]{:S(2)}, u32[]{:S(2)}) collective-permute-start(f32[4,16]{1,0:T(4,128)S(1)} %pad_maximum_fusion.1), channel_id=1, source_target_pairs={{0,4},{4,0},{8,12},{12,8},{16,20},{20,16},{24,28},{28,24},{32,36},... | collective-permute-start | bytes 776 | tf_op jit(solution)/shard_map/ppermute | solution.py:522
  44.5 26.1 %collective-permute-start.4 = (f32[16,1280]{1,0:T(8,128)S(1)}, f32[16,1280]{1,0:T(8,128)S(1)}, u32[]{:S(2)}, u32[]{:S(2)}) collective-permute-start(f32[16,1280]{1,0:T(8,128)S(1)} %get-tuple-element.39), channel_id=1, source_target_pairs={{0,4},{4,8},{8,12},{12,16},{16,20},{20,24},{24,28},{28,32},{32,36}... | collective-permute-start | bytes 245768 | tf_op jit(solution)/shard_map/ppermute | solution.py:517
  48.4 21.9 %all-to-all-start = ((f32[32,1,64]{2,1,0:T(1,128)}), f32[32,1,64]{2,1,0:T(1,128)S(1)}, u32[]{:S(2)}, u32[]{:S(2)}) async-start(f32[32,1,64]{2,1,0:T(1,128)} %broadcast_in_dim.5), calls=%async_computation | async-start | bytes 32768 | tf_op jit(solution)/shard_map/all_to_all | solution.py:525

commit v9 on v8

--- a/solution.py
+++ b/solution.py
@@ -460,7 +460,7 @@
         in_specs=[HBM if k in in_hbm else VM for k in range(len(ops))],
         out_specs=[VM] * len(outs),
         scratch_shapes=scratch,
-        compiler_params=pltpu.CompilerParams(vmem_limit_bytes=14 << 20) if in_hbm else PARAMS,
+        compiler_params=pltpu.CompilerParams(vmem_limit_bytes=18 << 20) if in_hbm else PARAMS,
         cost_estimate=pl.CostEstimate(flops=tiles.shape[0] << 27, transcendentals=0, bytes_accessed=tiles.size * 2),
         name=name,
     )(*[pltpu.with_memory_space_constraint(x, pltpu.HBM) if k in in_hbm else x for k, x in enumerate(ops)])
@@ -535,7 +535,7 @@
     base = (lax.axis_index("leaf") * leaf_dev).astype(jnp.int32).reshape(1)
     *prepared, packed = prepare_call(leaf_pairs, pair_count, base, coords, site_order, probes)
     far = shift(packed, -1)
-    cut0, cut1 = leaf_dev - REACH - 5, leaf_dev - REACH
+    cut0, cut1 = leaf_dev - REACH - 5, leaf_dev - REACH - 2
     evaluate = functools.partial(evaluate_call, leaf_dev=leaf_dev, n=n, prepared=prepared)
     tiles0, acc = evaluate(0, cut0, far=(), own=None, prev=None)
     tiles1, acc, send = evaluate(cut1, leaf_dev, far=(far,), own=None, prev=acc)

time: 71.8 us -> 70.9 us (0.987)
  waiting for transfers between devices: 2.76 us -> 0.89 us
  Pallas kernels: 38.9 us -> 39.9 us
    all_to_all x1, waiting for transfers between devices: 2.75 us -> 0.88 us  [sum_over_leaf(): lax.all_to_all(copies, 'leaf', split_axis=0, concat_axis=0, tiled=True, a...]
    pallas_call x4, Pallas kernels: 15.8 us -> 16.9 us  [small_call(): pl.pallas_call(kernel, out_shape=[jax.ShapeDtypeStruct(shape, jnp.float32...]
where the time goes in v9:
time: 70.9 us; the launch traced here: 70.6 us
  Pallas kernels  39.9 us (56%)
  starting transfers between devices  26.2 us (37%)
  other arithmetic  1.53 us (2%)
  between operations  1.44 us (2%)
  waiting for transfers between devices  0.89 us (1%)
  local copies, waits for them, and re-layouts  0.74 us (1%)
    pallas_call x3, Pallas kernels, evaluate_call(): pl.pallas_call(functools.partial(evaluate_kernel, i0, i1, leaf_dev, last)...  20.9 us
    pallas_call x4, Pallas kernels, small_call(): pl.pallas_call(kernel, out_shape=[jax.ShapeDtypeStruct(shape, jnp.float32...  16.9 us
    all_to_all x1, starting transfers between devices, sum_over_leaf(): lax.all_to_all(copies, 'leaf', split_axis=0, concat_axis=0, tiled=True, a...  13.4 us
    ppermute x4, starting transfers between devices, shift(): lax.ppermute(value, 'leaf', [(i, i + by) for i in range(length) if 0 <= i...  12.7 us
    pallas_call x1, Pallas kernels, prepare_call(): pl.pallas_call(prepare_kernel, out_shape=(jax.ShapeDtypeStruct((pairs.sha...  2.09 us
  transfers between devices with their start and end apart: 6, of which 1 were waited for; matrix products, arithmetic and copies ran while one was open for 2% of the time, Pallas kernels for 34%

profile of v9, /device:TPU:1, one launch (start us, length us, event | category | flops | bytes accessed | tf_op | source)
XLA Modules:
  0.0 70.6 jit_solution(2554659124719961269)
XLA Ops:
  1.3 2.1 %prepare.1 = (bf16[96,16,128]{2,1,0:T(8,128)(2,1)S(1)}, f32[16,8,256]{2,1,0:T(8,128)S(1)}, bf16[16,256,48]{2,1,0:T(8,128)(2,1)S(1)}, bf16[16,32,256]{2,1,0:T(8,1...) custom-call(s32[1]{0:T(128)S(6)} %copy.8.count_ref, s32[1]{0:T(128)} %bitcast.1.base_ref, ...), custom_call_target="tpu_custom_call" | custom-call | tf_op jit(solution)/shard_map/prepare/pallas_call | solution.py:400
  3.4 5.2 %collective-permute-start = (f32[19,1280]{1,0:T(8,128)S(1)}, f32[19,1280]{1,0:T(8,128)S(1)}, u32[]{:S(2)}, u32[]{:S(2)}) collective-permute-start(f32[19,1280]{1,0:T(8,128)S(1)} %get-tuple-element.27), channel_id=1, source_target_pairs={{4,0},{8,4},{12,8},{16,12},{20,16},{24,20},{28,24},{32,28},{36,32}... | collective-permute-start | bytes 291848 | tf_op jit(solution)/shard_map/ppermute | solution.py:517
  8.5 7.8 %evaluate_0.1 = (bf16[37,4,256,128]{3,2,1,0:T(8,128)(2,1)S(1)}, f32[21,16,256]{2,1,0:T(8,128)S(1)}) custom-call(bf16[96,16,128]{2,1,0:T(8,128)(2,1)S(1)} %get-tuple-element.21.listed_ref, f32[16,8,256]{2,1,0:T(8,128)S(1)} %get-tuple-element.22.pts_ref, bf16[16,256,48]{2,1,0:T(8,128)(2,1)S(1)} %get-tuple-element.23.cols_ref, ...), custom_call_target="tpu_custom_call" | custom-call | flops 9663676416 | bytes 9437184 | tf_op jit(solution)/shard_map/evaluate_0/pallas_call | solution.py:444
  16.3 0.0 collective-permute-done.rest_0_
  16.3 0.0 copy-start
  16.3 9.0 %evaluate_9.1 = (bf16[43,4,256,128]{3,2,1,0:T(8,128)(2,1)S(1)}, f32[21,16,256]{2,1,0:T(8,128)S(1)}, f32[16,1280]{1,0:T(8,128)S(1)}) custom-call(bf16[96,16,128]{2,1,0:T(8,128)(2,1)S(1)} %get-tuple-element.21.listed_ref, f32[16,8,256]{2,1,0:T(8,128)S(1)} %get-tuple-element.22.pts_ref, bf16[16,256,48]{2,1,0:T(8,128)(2,1)S(1)} %get-tuple-element.23.cols_ref, ...), custom_call_target="tpu_custom_call" | custom-call | flops 11274289152 | bytes 11010048 | tf_op jit(solution)/shard_map/evaluate_9/pallas_call | solution.py:444
  25.4 0.0 copy-start.1
  25.4 1.9 %collective-permute-start.1 = (f32[16,1280]{1,0:T(8,128)S(1)}, f32[16,1280]{1,0:T(8,128)S(1)}, u32[]{:S(2)}, u32[]{:S(2)}) collective-permute-start(f32[16,1280]{1,0:T(8,128)S(1)} %get-tuple-element.31), channel_id=1, source_target_pairs={{0,4},{4,8},{8,12},{12,16},{16,20},{20,24},{24,28},{28,32},{32,36}... | collective-permute-start | bytes 245768 | tf_op jit(solution)/shard_map/ppermute | solution.py:517
  27.3 0.0 copy-done
  27.3 4.1 %evaluate_6.1 = (bf16[19,4,256,128]{3,2,1,0:T(8,128)(2,1)S(1)}, f32[16,4096]{1,0:T(8,128)S(1)}) custom-call(bf16[96,16,128]{2,1,0:T(8,128)(2,1)S(1)} %get-tuple-element.21.listed_ref, f32[16,8,256]{2,1,0:T(8,128)S(1)} %get-tuple-element.22.pts_ref, bf16[16,256,48]{2,1,0:T(8,128)(2,1)S(1)} %get-tuple-element.23.cols_ref, ...), custom_call_target="tpu_custom_call" | custom-call | flops 4831838208 | bytes 4718592 | tf_op jit(solution)/shard_map/evaluate_6/pallas_call | solution.py:444
  31.4 0.0 collective-permute-done.1
  31.5 2.4 %collective-permute-start.2 = (f32[16,1280]{1,0:T(8,128)S(1)}, f32[16,1280]{1,0:T(8,128)S(1)}, u32[]{:S(2)}, u32[]{:S(2)}) collective-permute-start(f32[16,1280]{1,0:T(8,128)S(1)} %slice_add_fusion.1), channel_id=1, source_target_pairs={{4,0},{8,4},{12,8},{16,12},{20,16},{24,20},{28,24},{32,28},{36,32}... | collective-permute-start | bytes 245768 | tf_op jit(solution)/shard_map/ppermute | solution.py:517
  33.9 0.2 multiply_reduce_fusion.2
  34.1 4.4 %apply_0.1.prev_ref = f32[21,16,256]{2,1,0:T(8,128)S(1)} custom-call(bf16[96,16,128]{2,1,0:T(8,128)(2,1)S(1)} %get-tuple-element.21.listed_ref, bf16[37,4,256,128]{3,2,1,0:T(8,128)(2,1)S(1)} %get-tuple-element.34.tiles_ref, f32[16,4096]{1,0:T(8,128)S(1)} %get-tuple-element.49.w_ref), custom_call_target="tpu_custom_call" | custom-call | flops 4966055936 | bytes 9699328 | tf_op jit(solution)/shard_map/apply_0/pallas_call | solution.py:457
  38.5 0.0 collective-permute-done.2.far_ref.rest_0_
  38.5 0.0 copy-done.1
  38.5 2.5 %apply_edge.1 = (f32[21,16,256]{2,1,0:T(8,128)S(1)}, f32[16,1280]{1,0:T(8,128)S(1)}, f32[16,256]{1,0:T(8,128)S(1)}) custom-call(bf16[96,16,128]{2,1,0:T(8,128)(2,1)S(1)} %get-tuple-element.21.listed_ref, bf16[43,4,256,128]{3,2,1,0:T(8,128)(2,1)S(1)} %get-tuple-element.33.tiles_ref.tiles_hbm, f32[16,4096]{1,0:T(8,128)S(1)} %get-tuple-element.49.w_ref, ...), custom_call_target="tpu_custom_call" | custom-call | flops 5771362304 | bytes 11272192 | tf_op jit(solution)/shard_map/apply_edge/pallas_call | solution.py:457
  41.0 2.3 %apply_6.1 = (f32[21,16,256]{2,1,0:T(8,128)S(1)}, f32[16,256]{1,0:T(8,128)S(1)}) custom-call(bf16[96,16,128]{2,1,0:T(8,128)(2,1)S(1)} %get-tuple-element.21.listed_ref, bf16[19,4,256,128]{3,2,1,0:T(8,128)(2,1)S(1)} %get-tuple-element.32.tiles_ref, f32[16,4096]{1,0:T(8,128)S(1)} %get-tuple-element.49.w_ref, ...), custom_call_target="tpu_custom_call" | custom-call | flops 2550136832 | bytes 4980736 | tf_op jit(solution)/shard_map/apply_6/pallas_call | solution.py:457
  43.3 0.1 reduce_sum.50
  43.5 0.1 collective-permute-start.3
  43.6 3.2 %collective-permute-start.4 = (f32[16,1280]{1,0:T(8,128)S(1)}, f32[16,1280]{1,0:T(8,128)S(1)}, u32[]{:S(2)}, u32[]{:S(2)}) collective-permute-start(f32[16,1280]{1,0:T(8,128)S(1)} %get-tuple-element.39), channel_id=1, source_target_pairs={{0,4},{4,8},{8,12},{12,16},{16,20},{20,24},{24,28},{28,32},{32,36}... | collective-permute-start | bytes 245768 | tf_op jit(solution)/shard_map/ppermute | solution.py:517
  46.8 0.0 collective-permute-done.3
  46.8 0.1 broadcast_in_dim.4
  46.9 0.6 broadcast_in_dim.5
  47.5 13.4 %all-to-all-start = ((f32[32,1,64]{2,1,0:T(1,128)}), f32[32,1,64]{2,1,0:T(1,128)S(1)}, u32[]{:S(2)}, u32[]{:S(2)}) async-start(f32[32,1,64]{2,1,0:T(1,128)} %broadcast_in_dim.5), calls=%async_computation | async-start | bytes 32768 | tf_op jit(solution)/shard_map/all_to_all | solution.py:525
  60.9 7.7 %finish.1 = f32[16,4096]{1,0:T(8,128)S(1)} custom-call(bf16[96,16,128]{2,1,0:T(8,128)(2,1)S(1)} %get-tuple-element.21.listed_ref, bf16[43,4,256,128]{3,2,1,0:T(8,128)(2,1)} %copy-done.1, f32[16,4096]{1,0:T(8,128)S(1)} %get-tuple-element.49.w_ref, f32[16,1280]{1,0:T(8,128)S(1)} %collective-permute-done.2.far_ref.rest_0_, ...), custom_call_target="tpu_custom_call" | custom-call | flops 5771362304 | bytes 11272192 | tf_op jit(solution)/shard_map/finish/pallas_call | solution.py:457
  68.6 0.9 %all-to-all-done = f32[32,1,64]{2,1,0:T(1,128)S(1)} async-done(((f32[32,1,64]{2,1,0:T(1,128)}), f32[32,1,64]{2,1,0:T(1,128)S(1)}, u32[]{:S(2)}, u32[]{:S(2)}) %all-to-all-start) | async-done | bytes 8224 | tf_op jit(solution)/shard_map/all_to_all | solution.py:525
  69.5 0.1 multiply_add_fusion.1
  69.5 0.1 add_divide_fusion
  69.6 0.0 collective-permute-done.4
  69.7 1.0 %fusion.2 = (f32[16,4096]{1,0:T(8,128)}, f32[16,4096]{1,0:T(8,128)}) fusion(f32[16,2816]{1,0:T(8,128)S(1)} %slice.21, f32[16,1280]{1,0:T(8,128)S(1)} %slice_add_fusion, f32[16,4096]{1,0:T(8,128)S(1)} %copy-done, f32[16]{0:T(128)S(1)} %get-tuple-element.44, f32[16]{0:T(128)S(1)} %get-tuple-element.43, f32[16]{0:T(128)S(1)} %get-tuple-element.46, ...), kind=kLoop, calls=%fused_computation.4 | loop fusion | flops 917504 | bytes 1310912 | tf_op jit(solution)/shard_map/sub | solution.py:574
  (8 shorter events, 0.1 us)
Async XLA Ops:
  3.4 12.9 %collective-permute-start = (f32[19,1280]{1,0:T(8,128)S(1)}, f32[19,1280]{1,0:T(8,128)S(1)}, u32[]{:S(2)}, u32[]{:S(2)}) collective-permute-start(f32[19,1280]{1,0:T(8,128)S(1)} %get-tuple-element.27), channel_id=1, source_target_pairs={{4,0},{8,4},{12,8},{16,12},{20,16},{24,20},{28,24},{32,28},{36,32}... | collective-permute-start | bytes 291848 | tf_op jit(solution)/shard_map/ppermute | solution.py:517
  16.3 11.0 %copy-start = (f32[16,4096]{1,0:T(8,128)S(1)}, f32[16,4096]{1,0:T(8,128)}, u32[]{:S(2)}) copy-start(f32[16,4096]{1,0:T(8,128)} %rest_0_.1) | copy-start | bytes 786436
  25.4 13.2 %copy-start.1 = (bf16[43,4,256,128]{3,2,1,0:T(8,128)(2,1)}, bf16[43,4,256,128]{3,2,1,0:T(8,128)(2,1)S(1)}, u32[]{:S(2)}) copy-start(bf16[43,4,256,128]{3,2,1,0:T(8,128)(2,1)S(1)} %get-tuple-element.33.tiles_ref.tiles_hbm) | copy-start | bytes 33816580
  25.4 6.1 %collective-permute-start.1 = (f32[16,1280]{1,0:T(8,128)S(1)}, f32[16,1280]{1,0:T(8,128)S(1)}, u32[]{:S(2)}, u32[]{:S(2)}) collective-permute-start(f32[16,1280]{1,0:T(8,128)S(1)} %get-tuple-element.31), channel_id=1, source_target_pairs={{0,4},{4,8},{8,12},{12,16},{16,20},{20,24},{24,28},{28,32},{32,36}... | collective-permute-start | bytes 245768 | tf_op jit(solution)/shard_map/ppermute | solution.py:517
  31.5 7.1 %collective-permute-start.2 = (f32[16,1280]{1,0:T(8,128)S(1)}, f32[16,1280]{1,0:T(8,128)S(1)}, u32[]{:S(2)}, u32[]{:S(2)}) collective-permute-start(f32[16,1280]{1,0:T(8,128)S(1)} %slice_add_fusion.1), channel_id=1, source_target_pairs={{4,0},{8,4},{12,8},{16,12},{20,16},{24,20},{28,24},{32,28},{36,32}... | collective-permute-start | bytes 245768 | tf_op jit(solution)/shard_map/ppermute | solution.py:517
  43.5 3.3 %collective-permute-start.3 = (f32[4,16]{1,0:T(4,128)S(1)}, f32[4,16]{1,0:T(4,128)S(1)}, u32[]{:S(2)}, u32[]{:S(2)}) collective-permute-start(f32[4,16]{1,0:T(4,128)S(1)} %pad_maximum_fusion.1), channel_id=1, source_target_pairs={{0,4},{4,0},{8,12},{12,8},{16,20},{20,16},{24,28},{28,24},{32,36},... | collective-permute-start | bytes 776 | tf_op jit(solution)/shard_map/ppermute | solution.py:522
  43.6 26.1 %collective-permute-start.4 = (f32[16,1280]{1,0:T(8,128)S(1)}, f32[16,1280]{1,0:T(8,128)S(1)}, u32[]{:S(2)}, u32[]{:S(2)}) collective-permute-start(f32[16,1280]{1,0:T(8,128)S(1)} %get-tuple-element.39), channel_id=1, source_target_pairs={{0,4},{4,8},{8,12},{12,16},{16,20},{20,24},{24,28},{28,32},{32,36}... | collective-permute-start | bytes 245768 | tf_op jit(solution)/shard_map/ppermute | solution.py:517
  47.5 21.9 %all-to-all-start = ((f32[32,1,64]{2,1,0:T(1,128)}), f32[32,1,64]{2,1,0:T(1,128)S(1)}, u32[]{:S(2)}, u32[]{:S(2)}) async-start(f32[32,1,64]{2,1,0:T(1,128)} %broadcast_in_dim.5), calls=%async_computation | async-start | bytes 32768 | tf_op jit(solution)/shard_map/all_to_all | solution.py:525

commit v10 on v9

--- a/solution.py
+++ b/solution.py
@@ -312,6 +312,11 @@
     return total
 
 
+def unrolled(start, stop, one):
+    for i in range(start, stop):
+        one(i, 0)
+
+
 def apply_kernel(i0, i1, leaf_dev, last, listed_ref, tiles_ref, w_ref, *rest):
     rest = list(rest)
     if last:
@@ -336,7 +341,7 @@
         acc_ref[i] += total
         return 0
 
-    lax.fori_loop(i0, i1, one_leaf, 0)
+    unrolled(i0, i1, one_leaf)
     if last:
         total = weighted(acc_ref, w_ref, 0, leaf_dev) + weighted(acc_ref, far_ref, leaf_dev, REACH)
         dots_ref[...] = (total + extra_ref[...]) * (1.0 / PEAK)
@@ -356,7 +361,7 @@
             )
         return 0
 
-    lax.fori_loop(i0, leaf_dev, one_leaf, 0)
+    unrolled(i0, leaf_dev, one_leaf)
     dots_ref[...] = weighted(part_ref, w_ref.at[:, i0 * W :], 0, held) + weighted(part_ref, far_ref, held, REACH)
     acc_ref[...] = prev_ref[...]
     for k in range(held + REACH):

time: 70.9 us -> 69.4 us (0.979)
  Pallas kernels: 39.9 us -> 38.2 us
    pallas_call x4, Pallas kernels: 16.9 us -> 15.2 us  [small_call(): pl.pallas_call(kernel, out_shape=[jax.ShapeDtypeStruct(shape, jnp.float32...]
where the time goes in v10:
time: 69.4 us; the launch traced here: 69.1 us
  Pallas kernels  38.2 us (55%)
  starting transfers between devices  26.3 us (38%)
  other arithmetic  1.53 us (2%)
  between operations  1.44 us (2%)
  waiting for transfers between devices  0.9 us (1%)
  local copies, waits for them, and re-layouts  0.74 us (1%)
    pallas_call x3, Pallas kernels, evaluate_call(): pl.pallas_call(functools.partial(evaluate_kernel, i0, i1, leaf_dev, last)...  20.9 us
    pallas_call x4, Pallas kernels, small_call(): pl.pallas_call(kernel, out_shape=[jax.ShapeDtypeStruct(shape, jnp.float32...  15.2 us
    all_to_all x1, starting transfers between devices, sum_over_leaf(): lax.all_to_all(copies, 'leaf', split_axis=0, concat_axis=0, tiled=True, a...  13.4 us
    ppermute x4, starting transfers between devices, shift(): lax.ppermute(value, 'leaf', [(i, i + by) for i in range(length) if 0 <= i...  12.9 us
    pallas_call x1, Pallas kernels, prepare_call(): pl.pallas_call(prepare_kernel, out_shape=(jax.ShapeDtypeStruct((pairs.sha...  2.09 us
  transfers between devices with their start and end apart: 6, of which 1 were waited for; matrix products, arithmetic and copies ran while one was open for 2% of the time, Pallas kernels for 34%

profile of v10, /device:TPU:1, one launch (start us, length us, event | category | flops | bytes accessed | tf_op | source)
XLA Modules:
  0.0 69.1 jit_solution(16082805686226228953)
XLA Ops:
  1.3 2.1 %prepare.1 = (bf16[96,16,128]{2,1,0:T(8,128)(2,1)S(1)}, f32[16,8,256]{2,1,0:T(8,128)S(1)}, bf16[16,256,48]{2,1,0:T(8,128)(2,1)S(1)}, bf16[16,32,256]{2,1,0:T(8,1...) custom-call(s32[1]{0:T(128)S(6)} %copy.8.count_ref, s32[1]{0:T(128)} %bitcast.1.base_ref, ...), custom_call_target="tpu_custom_call" | custom-call | tf_op jit(solution)/shard_map/prepare/pallas_call | solution.py:405
  3.4 5.2 %collective-permute-start = (f32[19,1280]{1,0:T(8,128)S(1)}, f32[19,1280]{1,0:T(8,128)S(1)}, u32[]{:S(2)}, u32[]{:S(2)}) collective-permute-start(f32[19,1280]{1,0:T(8,128)S(1)} %get-tuple-element.27), channel_id=1, source_target_pairs={{4,0},{8,4},{12,8},{16,12},{20,16},{24,20},{28,24},{32,28},{36,32}... | collective-permute-start | bytes 291848 | tf_op jit(solution)/shard_map/ppermute | solution.py:522
  8.5 7.8 %evaluate_0.1 = (bf16[37,4,256,128]{3,2,1,0:T(8,128)(2,1)S(1)}, f32[21,16,256]{2,1,0:T(8,128)S(1)}) custom-call(bf16[96,16,128]{2,1,0:T(8,128)(2,1)S(1)} %get-tuple-element.21.listed_ref, f32[16,8,256]{2,1,0:T(8,128)S(1)} %get-tuple-element.22.pts_ref, bf16[16,256,48]{2,1,0:T(8,128)(2,1)S(1)} %get-tuple-element.23.cols_ref, ...), custom_call_target="tpu_custom_call" | custom-call | flops 9663676416 | bytes 9437184 | tf_op jit(solution)/shard_map/evaluate_0/pallas_call | solution.py:449
  16.3 0.0 collective-permute-done.rest_0_
  16.3 0.0 copy-start
  16.3 9.0 %evaluate_9.1 = (bf16[43,4,256,128]{3,2,1,0:T(8,128)(2,1)S(1)}, f32[21,16,256]{2,1,0:T(8,128)S(1)}, f32[16,1280]{1,0:T(8,128)S(1)}) custom-call(bf16[96,16,128]{2,1,0:T(8,128)(2,1)S(1)} %get-tuple-element.21.listed_ref, f32[16,8,256]{2,1,0:T(8,128)S(1)} %get-tuple-element.22.pts_ref, bf16[16,256,48]{2,1,0:T(8,128)(2,1)S(1)} %get-tuple-element.23.cols_ref, ...), custom_call_target="tpu_custom_call" | custom-call | flops 11274289152 | bytes 11010048 | tf_op jit(solution)/shard_map/evaluate_9/pallas_call | solution.py:449
  25.4 0.0 copy-start.1
  25.4 1.9 %collective-permute-start.1 = (f32[16,1280]{1,0:T(8,128)S(1)}, f32[16,1280]{1,0:T(8,128)S(1)}, u32[]{:S(2)}, u32[]{:S(2)}) collective-permute-start(f32[16,1280]{1,0:T(8,128)S(1)} %get-tuple-element.31), channel_id=1, source_target_pairs={{0,4},{4,8},{8,12},{12,16},{16,20},{20,24},{24,28},{28,32},{32,36}... | collective-permute-start | bytes 245768 | tf_op jit(solution)/shard_map/ppermute | solution.py:522
  27.3 0.0 copy-done
  27.3 4.1 %evaluate_6.1 = (bf16[19,4,256,128]{3,2,1,0:T(8,128)(2,1)S(1)}, f32[16,4096]{1,0:T(8,128)S(1)}) custom-call(bf16[96,16,128]{2,1,0:T(8,128)(2,1)S(1)} %get-tuple-element.21.listed_ref, f32[16,8,256]{2,1,0:T(8,128)S(1)} %get-tuple-element.22.pts_ref, bf16[16,256,48]{2,1,0:T(8,128)(2,1)S(1)} %get-tuple-element.23.cols_ref, ...), custom_call_target="tpu_custom_call" | custom-call | flops 4831838208 | bytes 4718592 | tf_op jit(solution)/shard_map/evaluate_6/pallas_call | solution.py:449
  31.4 0.0 collective-permute-done.1
  31.5 2.6 %collective-permute-start.2 = (f32[16,1280]{1,0:T(8,128)S(1)}, f32[16,1280]{1,0:T(8,128)S(1)}, u32[]{:S(2)}, u32[]{:S(2)}) collective-permute-start(f32[16,1280]{1,0:T(8,128)S(1)} %slice_add_fusion.1), channel_id=1, source_target_pairs={{4,0},{8,4},{12,8},{16,12},{20,16},{24,20},{28,24},{32,28},{36,32}... | collective-permute-start | bytes 245768 | tf_op jit(solution)/shard_map/ppermute | solution.py:522
  34.0 0.2 multiply_reduce_fusion.2
  34.3 3.8 %apply_0.1.prev_ref = f32[21,16,256]{2,1,0:T(8,128)S(1)} custom-call(bf16[96,16,128]{2,1,0:T(8,128)(2,1)S(1)} %get-tuple-element.21.listed_ref, bf16[37,4,256,128]{3,2,1,0:T(8,128)(2,1)S(1)} %get-tuple-element.34.tiles_ref, f32[16,4096]{1,0:T(8,128)S(1)} %get-tuple-element.49.w_ref), custom_call_target="tpu_custom_call" | custom-call | flops 4966055936 | bytes 9699328 | tf_op jit(solution)/shard_map/apply_0/pallas_call | solution.py:462
  38.1 0.0 collective-permute-done.2.far_ref.rest_0_
  38.1 0.0 copy-done.1
  38.1 1.7 %apply_edge.1 = (f32[21,16,256]{2,1,0:T(8,128)S(1)}, f32[16,1280]{1,0:T(8,128)S(1)}, f32[16,256]{1,0:T(8,128)S(1)}) custom-call(bf16[96,16,128]{2,1,0:T(8,128)(2,1)S(1)} %get-tuple-element.21.listed_ref, bf16[43,4,256,128]{3,2,1,0:T(8,128)(2,1)S(1)} %get-tuple-element.33.tiles_ref.tiles_hbm, f32[16,4096]{1,0:T(8,128)S(1)} %get-tuple-element.49.w_ref, ...), custom_call_target="tpu_custom_call" | custom-call | flops 5771362304 | bytes 11272192 | tf_op jit(solution)/shard_map/apply_edge/pallas_call | solution.py:462
  39.8 2.0 %apply_6.1 = (f32[21,16,256]{2,1,0:T(8,128)S(1)}, f32[16,256]{1,0:T(8,128)S(1)}) custom-call(bf16[96,16,128]{2,1,0:T(8,128)(2,1)S(1)} %get-tuple-element.21.listed_ref, bf16[19,4,256,128]{3,2,1,0:T(8,128)(2,1)S(1)} %get-tuple-element.32.tiles_ref, f32[16,4096]{1,0:T(8,128)S(1)} %get-tuple-element.49.w_ref, ...), custom_call_target="tpu_custom_call" | custom-call | flops 2550136832 | bytes 4980736 | tf_op jit(solution)/shard_map/apply_6/pallas_call | solution.py:462
  41.8 0.1 reduce_sum.50
  42.0 0.1 collective-permute-start.3
  42.1 3.2 %collective-permute-start.4 = (f32[16,1280]{1,0:T(8,128)S(1)}, f32[16,1280]{1,0:T(8,128)S(1)}, u32[]{:S(2)}, u32[]{:S(2)}) collective-permute-start(f32[16,1280]{1,0:T(8,128)S(1)} %get-tuple-element.39), channel_id=1, source_target_pairs={{0,4},{4,8},{8,12},{12,16},{16,20},{20,24},{24,28},{28,32},{32,36}... | collective-permute-start | bytes 245768 | tf_op jit(solution)/shard_map/ppermute | solution.py:522
  45.3 0.0 collective-permute-done.3
  45.3 0.1 broadcast_in_dim.4
  45.4 0.6 broadcast_in_dim.5
  46.0 13.4 %all-to-all-start = ((f32[32,1,64]{2,1,0:T(1,128)}), f32[32,1,64]{2,1,0:T(1,128)S(1)}, u32[]{:S(2)}, u32[]{:S(2)}) async-start(f32[32,1,64]{2,1,0:T(1,128)} %broadcast_in_dim.5), calls=%async_computation | async-start | bytes 32768 | tf_op jit(solution)/shard_map/all_to_all | solution.py:530
  59.4 7.7 %finish.1 = f32[16,4096]{1,0:T(8,128)S(1)} custom-call(bf16[96,16,128]{2,1,0:T(8,128)(2,1)S(1)} %get-tuple-element.21.listed_ref, bf16[43,4,256,128]{3,2,1,0:T(8,128)(2,1)} %copy-done.1, f32[16,4096]{1,0:T(8,128)S(1)} %get-tuple-element.49.w_ref, f32[16,1280]{1,0:T(8,128)S(1)} %collective-permute-done.2.far_ref.rest_0_, ...), custom_call_target="tpu_custom_call" | custom-call | flops 5771362304 | bytes 11272192 | tf_op jit(solution)/shard_map/finish/pallas_call | solution.py:462
  67.1 0.9 %all-to-all-done = f32[32,1,64]{2,1,0:T(1,128)S(1)} async-done(((f32[32,1,64]{2,1,0:T(1,128)}), f32[32,1,64]{2,1,0:T(1,128)S(1)}, u32[]{:S(2)}, u32[]{:S(2)}) %all-to-all-start) | async-done | bytes 8224 | tf_op jit(solution)/shard_map/all_to_all | solution.py:530
  68.0 0.1 multiply_add_fusion.1
  68.0 0.1 add_divide_fusion
  68.1 0.0 collective-permute-done.4
  68.1 1.0 %fusion.2 = (f32[16,4096]{1,0:T(8,128)}, f32[16,4096]{1,0:T(8,128)}) fusion(f32[16,2816]{1,0:T(8,128)S(1)} %slice.21, f32[16,1280]{1,0:T(8,128)S(1)} %slice_add_fusion, f32[16,4096]{1,0:T(8,128)S(1)} %copy-done, f32[16]{0:T(128)S(1)} %get-tuple-element.44, f32[16]{0:T(128)S(1)} %get-tuple-element.43, f32[16]{0:T(128)S(1)} %get-tuple-element.46, ...), kind=kLoop, calls=%fused_computation.4 | loop fusion | flops 917504 | bytes 1310912 | tf_op jit(solution)/shard_map/sub | solution.py:579
  (8 shorter events, 0.1 us)
Async XLA Ops:
  3.4 12.9 %collective-permute-start = (f32[19,1280]{1,0:T(8,128)S(1)}, f32[19,1280]{1,0:T(8,128)S(1)}, u32[]{:S(2)}, u32[]{:S(2)}) collective-permute-start(f32[19,1280]{1,0:T(8,128)S(1)} %get-tuple-element.27), channel_id=1, source_target_pairs={{4,0},{8,4},{12,8},{16,12},{20,16},{24,20},{28,24},{32,28},{36,32}... | collective-permute-start | bytes 291848 | tf_op jit(solution)/shard_map/ppermute | solution.py:522
  16.3 11.0 %copy-start = (f32[16,4096]{1,0:T(8,128)S(1)}, f32[16,4096]{1,0:T(8,128)}, u32[]{:S(2)}) copy-start(f32[16,4096]{1,0:T(8,128)} %rest_0_.1) | copy-start | bytes 786436
  25.4 12.7 %copy-start.1 = (bf16[43,4,256,128]{3,2,1,0:T(8,128)(2,1)}, bf16[43,4,256,128]{3,2,1,0:T(8,128)(2,1)S(1)}, u32[]{:S(2)}) copy-start(bf16[43,4,256,128]{3,2,1,0:T(8,128)(2,1)S(1)} %get-tuple-element.33.tiles_ref.tiles_hbm) | copy-start | bytes 33816580
  25.4 6.1 %collective-permute-start.1 = (f32[16,1280]{1,0:T(8,128)S(1)}, f32[16,1280]{1,0:T(8,128)S(1)}, u32[]{:S(2)}, u32[]{:S(2)}) collective-permute-start(f32[16,1280]{1,0:T(8,128)S(1)} %get-tuple-element.31), channel_id=1, source_target_pairs={{0,4},{4,8},{8,12},{12,16},{16,20},{20,24},{24,28},{28,32},{32,36}... | collective-permute-start | bytes 245768 | tf_op jit(solution)/shard_map/ppermute | solution.py:522
  31.5 6.6 %collective-permute-start.2 = (f32[16,1280]{1,0:T(8,128)S(1)}, f32[16,1280]{1,0:T(8,128)S(1)}, u32[]{:S(2)}, u32[]{:S(2)}) collective-permute-start(f32[16,1280]{1,0:T(8,128)S(1)} %slice_add_fusion.1), channel_id=1, source_target_pairs={{4,0},{8,4},{12,8},{16,12},{20,16},{24,20},{28,24},{32,28},{36,32}... | collective-permute-start | bytes 245768 | tf_op jit(solution)/shard_map/ppermute | solution.py:522
  42.0 3.3 %collective-permute-start.3 = (f32[4,16]{1,0:T(4,128)S(1)}, f32[4,16]{1,0:T(4,128)S(1)}, u32[]{:S(2)}, u32[]{:S(2)}) collective-permute-start(f32[4,16]{1,0:T(4,128)S(1)} %pad_maximum_fusion.1), channel_id=1, source_target_pairs={{0,4},{4,0},{8,12},{12,8},{16,20},{20,16},{24,28},{28,24},{32,36},... | collective-permute-start | bytes 776 | tf_op jit(solution)/shard_map/ppermute | solution.py:527
  42.1 26.1 %collective-permute-start.4 = (f32[16,1280]{1,0:T(8,128)S(1)}, f32[16,1280]{1,0:T(8,128)S(1)}, u32[]{:S(2)}, u32[]{:S(2)}) collective-permute-start(f32[16,1280]{1,0:T(8,128)S(1)} %get-tuple-element.39), channel_id=1, source_target_pairs={{0,4},{4,8},{8,12},{12,16},{16,20},{20,24},{24,28},{28,32},{32,36}... | collective-permute-start | bytes 245768 | tf_op jit(solution)/shard_map/ppermute | solution.py:522
  46.0 21.9 %all-to-all-start = ((f32[32,1,64]{2,1,0:T(1,128)}), f32[32,1,64]{2,1,0:T(1,128)S(1)}, u32[]{:S(2)}, u32[]{:S(2)}) async-start(f32[32,1,64]{2,1,0:T(1,128)} %broadcast_in_dim.5), calls=%async_computation | async-start | bytes 32768 | tf_op jit(solution)/shard_map/all_to_all | solution.py:530

commit v11 on v10

--- a/solution.py
+++ b/solution.py
@@ -196,6 +196,11 @@
         out_ref[:, at] = x if own_ref is None else x + NUGGET * own_ref[:, at]
 
 
+def unrolled(start, stop, one):
+    for i in range(start, stop):
+        one(i, 0)
+
+
 def evaluate_kernel(i0, i1, leaf_dev, last, listed_ref, pts_ref, cols_ref, v_ref, center_ref, wide_ref, *rest):
     rest = list(rest)
     far = i1 + REACH > leaf_dev
@@ -229,7 +234,6 @@
         acc_ref[...] = prev_ref[...]
     else:
         acc_ref[...] = jnp.zeros_like(acc_ref)
-    tiles_ref[0] = jnp.zeros_like(tiles_ref[0])
 
     def finish(i, slot):
         to_row, to_col = products(
@@ -249,7 +253,8 @@
             make_tile(tiles_ref.at[slot + (1 + d)], block, d == 0)
 
         make(0)
-        finish(jnp.maximum(i - 1, i0), slot)
+        if i > i0:
+            finish(i - 1, slot)
         total = None
         for d in range(REACH):
             make(d + 1)
@@ -288,7 +293,7 @@
 
     @pl.when(compact)
     def _():
-        lax.fori_loop(i0, i1, near_leaf, 0)
+        unrolled(i0, i1, near_leaf)
 
     @pl.when(jnp.logical_not(compact))
     def _():
@@ -310,11 +315,6 @@
     for k in range(1, leaves):
         total += acc_ref[first + k] * field_ref[:, k * W : (k + 1) * W]
     return total
-
-
-def unrolled(start, stop, one):
-    for i in range(start, stop):
-        one(i, 0)
 
 
 def apply_kernel(i0, i1, leaf_dev, last, listed_ref, tiles_ref, w_ref, *rest):

time: 69.4 us -> 69.9 us (level)
  Pallas kernels: 38.2 us -> 38.9 us
    pallas_call x3, Pallas kernels: 20.9 us -> 21.7 us  [evaluate_call(): pl.pallas_call(functools.partial(evaluate_kernel, i0, i1, leaf_dev, last)...]
where the time goes in v11:
time: 69.9 us; the launch traced here: 69.7 us
  Pallas kernels  38.9 us (56%)
  starting transfers between devices  26.2 us (37%)
  other arithmetic  1.53 us (2%)
  between operations  1.44 us (2%)
  waiting for transfers between devices  0.9 us (1%)
  local copies, waits for them, and re-layouts  0.74 us (1%)
    pallas_call x3, Pallas kernels, evaluate_call(): pl.pallas_call(functools.partial(evaluate_kernel, i0, i1, leaf_dev, last)...  21.7 us
    pallas_call x4, Pallas kernels, small_call(): pl.pallas_call(kernel, out_shape=[jax.ShapeDtypeStruct(shape, jnp.float32...  15.2 us
    all_to_all x1, starting transfers between devices, sum_over_leaf(): lax.all_to_all(copies, 'leaf', split_axis=0, concat_axis=0, tiled=True, a...  13.4 us
    ppermute x4, starting transfers between devices, shift(): lax.ppermute(value, 'leaf', [(i, i + by) for i in range(length) if 0 <= i...  12.7 us
    pallas_call x1, Pallas kernels, prepare_call(): pl.pallas_call(prepare_kernel, out_shape=(jax.ShapeDtypeStruct((pairs.sha...  2.09 us
  transfers between devices with their start and end apart: 6, of which 1 were waited for; matrix products, arithmetic and copies ran while one was open for 2% of the time, Pallas kernels for 34%

profile of v11, /device:TPU:1, one launch (start us, length us, event | category | flops | bytes accessed | tf_op | source)
XLA Modules:
  0.0 69.7 jit_solution(14549395720281998847)
XLA Ops:
  1.3 2.1 %prepare.1 = (bf16[96,16,128]{2,1,0:T(8,128)(2,1)S(1)}, f32[16,8,256]{2,1,0:T(8,128)S(1)}, bf16[16,256,48]{2,1,0:T(8,128)(2,1)S(1)}, bf16[16,32,256]{2,1,0:T(8,1...) custom-call(s32[1]{0:T(128)S(6)} %copy.8.count_ref, s32[1]{0:T(128)} %bitcast.1.base_ref, ...), custom_call_target="tpu_custom_call" | custom-call | tf_op jit(solution)/shard_map/prepare/pallas_call | solution.py:405
  3.4 5.2 %collective-permute-start = (f32[19,1280]{1,0:T(8,128)S(1)}, f32[19,1280]{1,0:T(8,128)S(1)}, u32[]{:S(2)}, u32[]{:S(2)}) collective-permute-start(f32[19,1280]{1,0:T(8,128)S(1)} %get-tuple-element.27), channel_id=1, source_target_pairs={{4,0},{8,4},{12,8},{16,12},{20,16},{24,20},{28,24},{32,28},{36,32}... | collective-permute-start | bytes 291848 | tf_op jit(solution)/shard_map/ppermute | solution.py:522
  8.5 7.8 %evaluate_0.1 = (bf16[37,4,256,128]{3,2,1,0:T(8,128)(2,1)S(1)}, f32[21,16,256]{2,1,0:T(8,128)S(1)}) custom-call(bf16[96,16,128]{2,1,0:T(8,128)(2,1)S(1)} %get-tuple-element.21.listed_ref, f32[16,8,256]{2,1,0:T(8,128)S(1)} %get-tuple-element.22.pts_ref, bf16[16,256,48]{2,1,0:T(8,128)(2,1)S(1)} %get-tuple-element.23.cols_ref, ...), custom_call_target="tpu_custom_call" | custom-call | flops 9663676416 | bytes 9437184 | tf_op jit(solution)/shard_map/evaluate_0/pallas_call | solution.py:449
  16.3 0.0 collective-permute-done.rest_0_
  16.3 0.0 copy-start
  16.3 9.5 %evaluate_9.1 = (bf16[43,4,256,128]{3,2,1,0:T(8,128)(2,1)S(1)}, f32[21,16,256]{2,1,0:T(8,128)S(1)}, f32[16,1280]{1,0:T(8,128)S(1)}) custom-call(bf16[96,16,128]{2,1,0:T(8,128)(2,1)S(1)} %get-tuple-element.21.listed_ref, f32[16,8,256]{2,1,0:T(8,128)S(1)} %get-tuple-element.22.pts_ref, bf16[16,256,48]{2,1,0:T(8,128)(2,1)S(1)} %get-tuple-element.23.cols_ref, ...), custom_call_target="tpu_custom_call" | custom-call | flops 11274289152 | bytes 11010048 | tf_op jit(solution)/shard_map/evaluate_9/pallas_call | solution.py:449
  25.9 0.0 copy-start.1
  25.9 1.9 %collective-permute-start.1 = (f32[16,1280]{1,0:T(8,128)S(1)}, f32[16,1280]{1,0:T(8,128)S(1)}, u32[]{:S(2)}, u32[]{:S(2)}) collective-permute-start(f32[16,1280]{1,0:T(8,128)S(1)} %get-tuple-element.31), channel_id=1, source_target_pairs={{0,4},{4,8},{8,12},{12,16},{16,20},{20,24},{24,28},{28,32},{32,36}... | collective-permute-start | bytes 245768 | tf_op jit(solution)/shard_map/ppermute | solution.py:522
  27.8 0.0 copy-done
  27.8 4.3 %evaluate_6.1 = (bf16[19,4,256,128]{3,2,1,0:T(8,128)(2,1)S(1)}, f32[16,4096]{1,0:T(8,128)S(1)}) custom-call(bf16[96,16,128]{2,1,0:T(8,128)(2,1)S(1)} %get-tuple-element.21.listed_ref, f32[16,8,256]{2,1,0:T(8,128)S(1)} %get-tuple-element.22.pts_ref, bf16[16,256,48]{2,1,0:T(8,128)(2,1)S(1)} %get-tuple-element.23.cols_ref, ...), custom_call_target="tpu_custom_call" | custom-call | flops 4831838208 | bytes 4718592 | tf_op jit(solution)/shard_map/evaluate_6/pallas_call | solution.py:449
  32.2 0.0 collective-permute-done.1
  32.2 2.4 %collective-permute-start.2 = (f32[16,1280]{1,0:T(8,128)S(1)}, f32[16,1280]{1,0:T(8,128)S(1)}, u32[]{:S(2)}, u32[]{:S(2)}) collective-permute-start(f32[16,1280]{1,0:T(8,128)S(1)} %slice_add_fusion.1), channel_id=1, source_target_pairs={{4,0},{8,4},{12,8},{16,12},{20,16},{24,20},{28,24},{32,28},{36,32}... | collective-permute-start | bytes 245768 | tf_op jit(solution)/shard_map/ppermute | solution.py:522
  34.6 0.2 multiply_reduce_fusion.2
  34.8 3.8 %apply_0.1.prev_ref = f32[21,16,256]{2,1,0:T(8,128)S(1)} custom-call(bf16[96,16,128]{2,1,0:T(8,128)(2,1)S(1)} %get-tuple-element.21.listed_ref, bf16[37,4,256,128]{3,2,1,0:T(8,128)(2,1)S(1)} %get-tuple-element.34.tiles_ref, f32[16,4096]{1,0:T(8,128)S(1)} %get-tuple-element.49.w_ref), custom_call_target="tpu_custom_call" | custom-call | flops 4966055936 | bytes 9699328 | tf_op jit(solution)/shard_map/apply_0/pallas_call | solution.py:462
  38.6 0.0 collective-permute-done.2.far_ref.rest_0_
  38.7 0.0 copy-done.1
  38.7 1.7 %apply_edge.1 = (f32[21,16,256]{2,1,0:T(8,128)S(1)}, f32[16,1280]{1,0:T(8,128)S(1)}, f32[16,256]{1,0:T(8,128)S(1)}) custom-call(bf16[96,16,128]{2,1,0:T(8,128)(2,1)S(1)} %get-tuple-element.21.listed_ref, bf16[43,4,256,128]{3,2,1,0:T(8,128)(2,1)S(1)} %get-tuple-element.33.tiles_ref.tiles_hbm, f32[16,4096]{1,0:T(8,128)S(1)} %get-tuple-element.49.w_ref, ...), custom_call_target="tpu_custom_call" | custom-call | flops 5771362304 | bytes 11272192 | tf_op jit(solution)/shard_map/apply_edge/pallas_call | solution.py:462
  40.4 2.0 %apply_6.1 = (f32[21,16,256]{2,1,0:T(8,128)S(1)}, f32[16,256]{1,0:T(8,128)S(1)}) custom-call(bf16[96,16,128]{2,1,0:T(8,128)(2,1)S(1)} %get-tuple-element.21.listed_ref, bf16[19,4,256,128]{3,2,1,0:T(8,128)(2,1)S(1)} %get-tuple-element.32.tiles_ref, f32[16,4096]{1,0:T(8,128)S(1)} %get-tuple-element.49.w_ref, ...), custom_call_target="tpu_custom_call" | custom-call | flops 2550136832 | bytes 4980736 | tf_op jit(solution)/shard_map/apply_6/pallas_call | solution.py:462
  42.4 0.1 reduce_sum.50
  42.5 0.1 collective-permute-start.3
  42.6 3.2 %collective-permute-start.4 = (f32[16,1280]{1,0:T(8,128)S(1)}, f32[16,1280]{1,0:T(8,128)S(1)}, u32[]{:S(2)}, u32[]{:S(2)}) collective-permute-start(f32[16,1280]{1,0:T(8,128)S(1)} %get-tuple-element.39), channel_id=1, source_target_pairs={{0,4},{4,8},{8,12},{12,16},{16,20},{20,24},{24,28},{28,32},{32,36}... | collective-permute-start | bytes 245768 | tf_op jit(solution)/shard_map/ppermute | solution.py:522
  45.8 0.0 collective-permute-done.3
  45.9 0.1 broadcast_in_dim.4
  46.0 0.6 broadcast_in_dim.5
  46.6 13.4 %all-to-all-start = ((f32[32,1,64]{2,1,0:T(1,128)}), f32[32,1,64]{2,1,0:T(1,128)S(1)}, u32[]{:S(2)}, u32[]{:S(2)}) async-start(f32[32,1,64]{2,1,0:T(1,128)} %broadcast_in_dim.5), calls=%async_computation | async-start | bytes 32768 | tf_op jit(solution)/shard_map/all_to_all | solution.py:530
  59.9 7.7 %finish.1 = f32[16,4096]{1,0:T(8,128)S(1)} custom-call(bf16[96,16,128]{2,1,0:T(8,128)(2,1)S(1)} %get-tuple-element.21.listed_ref, bf16[43,4,256,128]{3,2,1,0:T(8,128)(2,1)} %copy-done.1, f32[16,4096]{1,0:T(8,128)S(1)} %get-tuple-element.49.w_ref, f32[16,1280]{1,0:T(8,128)S(1)} %collective-permute-done.2.far_ref.rest_0_, ...), custom_call_target="tpu_custom_call" | custom-call | flops 5771362304 | bytes 11272192 | tf_op jit(solution)/shard_map/finish/pallas_call | solution.py:462
  67.6 0.9 %all-to-all-done = f32[32,1,64]{2,1,0:T(1,128)S(1)} async-done(((f32[32,1,64]{2,1,0:T(1,128)}), f32[32,1,64]{2,1,0:T(1,128)S(1)}, u32[]{:S(2)}, u32[]{:S(2)}) %all-to-all-start) | async-done | bytes 8224 | tf_op jit(solution)/shard_map/all_to_all | solution.py:530
  68.5 0.1 multiply_add_fusion.1
  68.6 0.1 add_divide_fusion
  68.7 0.0 collective-permute-done.4
  68.7 1.0 %fusion.2 = (f32[16,4096]{1,0:T(8,128)}, f32[16,4096]{1,0:T(8,128)}) fusion(f32[16,2816]{1,0:T(8,128)S(1)} %slice.21, f32[16,1280]{1,0:T(8,128)S(1)} %slice_add_fusion, f32[16,4096]{1,0:T(8,128)S(1)} %copy-done, f32[16]{0:T(128)S(1)} %get-tuple-element.44, f32[16]{0:T(128)S(1)} %get-tuple-element.43, f32[16]{0:T(128)S(1)} %get-tuple-element.46, ...), kind=kLoop, calls=%fused_computation.4 | loop fusion | flops 917504 | bytes 1310912 | tf_op jit(solution)/shard_map/sub | solution.py:579
  (8 shorter events, 0.1 us)
Async XLA Ops:
  3.4 13.0 %collective-permute-start = (f32[19,1280]{1,0:T(8,128)S(1)}, f32[19,1280]{1,0:T(8,128)S(1)}, u32[]{:S(2)}, u32[]{:S(2)}) collective-permute-start(f32[19,1280]{1,0:T(8,128)S(1)} %get-tuple-element.27), channel_id=1, source_target_pairs={{4,0},{8,4},{12,8},{16,12},{20,16},{24,20},{28,24},{32,28},{36,32}... | collective-permute-start | bytes 291848 | tf_op jit(solution)/shard_map/ppermute | solution.py:522
  16.3 11.5 %copy-start = (f32[16,4096]{1,0:T(8,128)S(1)}, f32[16,4096]{1,0:T(8,128)}, u32[]{:S(2)}) copy-start(f32[16,4096]{1,0:T(8,128)} %rest_0_.1) | copy-start | bytes 786436
  25.9 12.8 %copy-start.1 = (bf16[43,4,256,128]{3,2,1,0:T(8,128)(2,1)}, bf16[43,4,256,128]{3,2,1,0:T(8,128)(2,1)S(1)}, u32[]{:S(2)}) copy-start(bf16[43,4,256,128]{3,2,1,0:T(8,128)(2,1)S(1)} %get-tuple-element.33.tiles_ref.tiles_hbm) | copy-start | bytes 33816580
  25.9 6.3 %collective-permute-start.1 = (f32[16,1280]{1,0:T(8,128)S(1)}, f32[16,1280]{1,0:T(8,128)S(1)}, u32[]{:S(2)}, u32[]{:S(2)}) collective-permute-start(f32[16,1280]{1,0:T(8,128)S(1)} %get-tuple-element.31), channel_id=1, source_target_pairs={{0,4},{4,8},{8,12},{12,16},{16,20},{20,24},{24,28},{28,32},{32,36}... | collective-permute-start | bytes 245768 | tf_op jit(solution)/shard_map/ppermute | solution.py:522
  32.2 6.5 %collective-permute-start.2 = (f32[16,1280]{1,0:T(8,128)S(1)}, f32[16,1280]{1,0:T(8,128)S(1)}, u32[]{:S(2)}, u32[]{:S(2)}) collective-permute-start(f32[16,1280]{1,0:T(8,128)S(1)} %slice_add_fusion.1), channel_id=1, source_target_pairs={{4,0},{8,4},{12,8},{16,12},{20,16},{24,20},{28,24},{32,28},{36,32}... | collective-permute-start | bytes 245768 | tf_op jit(solution)/shard_map/ppermute | solution.py:522
  42.5 3.3 %collective-permute-start.3 = (f32[4,16]{1,0:T(4,128)S(1)}, f32[4,16]{1,0:T(4,128)S(1)}, u32[]{:S(2)}, u32[]{:S(2)}) collective-permute-start(f32[4,16]{1,0:T(4,128)S(1)} %pad_maximum_fusion.1), channel_id=1, source_target_pairs={{0,4},{4,0},{8,12},{12,8},{16,20},{20,16},{24,28},{28,24},{32,36},... | collective-permute-start | bytes 776 | tf_op jit(solution)/shard_map/ppermute | solution.py:527
  42.6 26.1 %collective-permute-start.4 = (f32[16,1280]{1,0:T(8,128)S(1)}, f32[16,1280]{1,0:T(8,128)S(1)}, u32[]{:S(2)}, u32[]{:S(2)}) collective-permute-start(f32[16,1280]{1,0:T(8,128)S(1)} %get-tuple-element.39), channel_id=1, source_target_pairs={{0,4},{4,8},{8,12},{12,16},{16,20},{20,24},{24,28},{28,32},{32,36}... | collective-permute-start | bytes 245768 | tf_op jit(solution)/shard_map/ppermute | solution.py:522
  46.6 21.9 %all-to-all-start = ((f32[32,1,64]{2,1,0:T(1,128)}), f32[32,1,64]{2,1,0:T(1,128)S(1)}, u32[]{:S(2)}, u32[]{:S(2)}) async-start(f32[32,1,64]{2,1,0:T(1,128)} %broadcast_in_dim.5), calls=%async_computation | async-start | bytes 32768 | tf_op jit(solution)/shard_map/all_to_all | solution.py:530

commit v12 on v10

--- a/solution.py
+++ b/solution.py
@@ -517,20 +517,39 @@
     )[0]
 
 
+def add_edge_kernel(rows_ref, back_ref, out_ref):
+    edge = back_ref.shape[1]
+    out_ref[:, 0:edge] = rows_ref[:, 0:edge] + back_ref[...]
+    out_ref[:, edge:] = rows_ref[:, edge:]
+
+
+def add_edge_call(rows, back):
+    return pl.pallas_call(
+        add_edge_kernel,
+        out_shape=jax.ShapeDtypeStruct(rows.shape, jnp.float32),
+        in_specs=[VM, VM],
+        out_specs=VM,
+        compiler_params=PARAMS,
+        name="add_edge",
+    )(rows, back)
+
+
 def shift(value, by):
     length = lax.axis_size("leaf")
     return lax.ppermute(value, "leaf", [(i, i + by) for i in range(length) if 0 <= i + by < length])
 
 
-def sum_over_leaf(value):
+def sum_over_leaf(value, later, beside):
     length = lax.axis_size("leaf")
     value = value + lax.ppermute(value, "leaf", [(i, i ^ 1) for i in range(length)])
     copies = jnp.broadcast_to(value.reshape(-1), (length // 2, value.size))
+    copies, later = lax.optimization_barrier((copies, later))
     groups = [[i for i in range(length) if i % 2 == c] for c in range(2)]
     got = lax.all_to_all(
         copies, "leaf", split_axis=0, concat_axis=0, tiled=True, axis_index_groups=groups
     )
-    return jnp.sum(got, axis=0).reshape(value.shape)
+    got, done = lax.optimization_barrier((got, beside(later)))
+    return jnp.sum(got, axis=0).reshape(value.shape), done
 
 
 def body(coords, site_order, leaf_pairs, pair_count, probes):
@@ -552,7 +571,6 @@
     common = dict(leaf_dev=leaf_dev, n=n, listed=prepared[0], own=image)
     (acc,) = apply_call(0, cut0, tiles=tiles0, last=(), prev=None, **common)
     acc, send, edge_dots = edge_call(cut1, tiles=tiles1, far=image_far, prev=acc, **common)
-    back = shift(send, 1)
     acc, dots = apply_call(cut0, cut1, tiles=tiles2, last=(image_far, edge_dots), prev=acc, **common)
     square = jnp.sum(image * image, axis=1)
     sums = jnp.stack(
@@ -563,9 +581,12 @@
             jnp.sum(dots, axis=1) + NUGGET * square,
         ]
     )
-    image2 = finish_call(cut1, tiles=tiles1, far=image_far, prev=acc, **common)
-    image2 = jnp.concatenate([image2[:, :edge] + back, image2[:, edge:]], axis=1)
-    rr, bw, ww, wz = sum_over_leaf(sums)
+
+    def beside(send):
+        rows = finish_call(cut1, tiles=tiles1, far=image_far, prev=acc, **common)
+        return add_edge_call(rows, shift(send, 1))
+
+    (rr, bw, ww, wz), image2 = sum_over_leaf(sums, send, beside)
     alpha = rr / bw
     rr1 = rr - 2.0 * alpha * bw + alpha * alpha * ww
     beta = rr1 / rr

time: 69.4 us -> 69.3 us (level)
    ppermute x1, waiting for transfers between devices: 0.01 us -> 1.14 us  [sum_over_leaf(): lax.ppermute(value, 'leaf', [(i, i ^ 1) for i in range(length)])]
    all_to_all x1, waiting for transfers between devices: 0.88 us -> 0.01 us  [sum_over_leaf(): lax.all_to_all(copies, 'leaf', split_axis=0, concat_axis=0, tiled=True, a...]
    all_to_all x1, starting transfers between devices: 13.4 us -> 12.5 us  [sum_over_leaf(): lax.all_to_all(copies, 'leaf', split_axis=0, concat_axis=0, tiled=True, a...]
  transfers between devices with their start and end apart: 6 -> 6, of which waited for: 1 -> 1; matrix products, arithmetic and copies ran while one was open for 2% -> 0% of each run, Pallas kernels for 34% -> 34%
where the time goes in v12:
time: 69.3 us; the launch traced here: 69.1 us
  Pallas kernels  38.2 us (55%)
  starting transfers between devices  26.1 us (38%)
  other arithmetic  1.52 us (2%)
  between operations  1.43 us (2%)
  waiting for transfers between devices  1.16 us (2%)
  local copies, waits for them, and re-layouts  0.72 us (1%)
    pallas_call x3, Pallas kernels, evaluate_call(): pl.pallas_call(functools.partial(evaluate_kernel, i0, i1, leaf_dev, last)...  20.9 us
    pallas_call x4, Pallas kernels, small_call(): pl.pallas_call(kernel, out_shape=[jax.ShapeDtypeStruct(shape, jnp.float32...  15.2 us
    ppermute x4, starting transfers between devices, shift(): lax.ppermute(value, 'leaf', [(i, i + by) for i in range(length) if 0 <= i...  13.4 us
    all_to_all x1, starting transfers between devices, sum_over_leaf(): lax.all_to_all(copies, 'leaf', split_axis=0, concat_axis=0, tiled=True, a...  12.5 us
    pallas_call x1, Pallas kernels, prepare_call(): pl.pallas_call(prepare_kernel, out_shape=(jax.ShapeDtypeStruct((pairs.sha...  2.09 us
  transfers between devices with their start and end apart: 6, of which 1 were waited for; matrix products, arithmetic and copies ran while one was open for 0% of the time, Pallas kernels for 34%

profile of v12, /device:TPU:1, one launch (start us, length us, event | category | flops | bytes accessed | tf_op | source)
XLA Modules:
  0.0 69.1 jit_solution(11372856086590296826)
XLA Ops:
  1.3 2.1 %prepare.1 = (bf16[96,16,128]{2,1,0:T(8,128)(2,1)S(1)}, f32[16,8,256]{2,1,0:T(8,128)S(1)}, bf16[16,256,48]{2,1,0:T(8,128)(2,1)S(1)}, bf16[16,32,256]{2,1,0:T(8,1...) custom-call(s32[1]{0:T(128)S(6)} %copy.7.count_ref, s32[1]{0:T(128)} %bitcast.1.base_ref, ...), custom_call_target="tpu_custom_call" | custom-call | tf_op jit(solution)/shard_map/prepare/pallas_call | solution.py:405
  3.4 5.2 %collective-permute-start = (f32[19,1280]{1,0:T(8,128)S(1)}, f32[19,1280]{1,0:T(8,128)S(1)}, u32[]{:S(2)}, u32[]{:S(2)}) collective-permute-start(f32[19,1280]{1,0:T(8,128)S(1)} %get-tuple-element.31), channel_id=1, source_target_pairs={{4,0},{8,4},{12,8},{16,12},{20,16},{24,20},{28,24},{32,28},{36,32}... | collective-permute-start | bytes 291848 | tf_op jit(solution)/shard_map/ppermute | solution.py:539
  8.5 7.7 %evaluate_0.1 = (bf16[37,4,256,128]{3,2,1,0:T(8,128)(2,1)S(1)}, f32[21,16,256]{2,1,0:T(8,128)S(1)}) custom-call(bf16[96,16,128]{2,1,0:T(8,128)(2,1)S(1)} %get-tuple-element.25.listed_ref, f32[16,8,256]{2,1,0:T(8,128)S(1)} %get-tuple-element.26.pts_ref, bf16[16,256,48]{2,1,0:T(8,128)(2,1)S(1)} %get-tuple-element.27.cols_ref, ...), custom_call_target="tpu_custom_call" | custom-call | flops 9663676416 | bytes 9437184 | tf_op jit(solution)/shard_map/evaluate_0/pallas_call | solution.py:449
  16.3 0.0 collective-permute-done.rest_0_
  16.3 0.0 copy-start
  16.3 9.0 %evaluate_9.1 = (bf16[43,4,256,128]{3,2,1,0:T(8,128)(2,1)S(1)}, f32[21,16,256]{2,1,0:T(8,128)S(1)}, f32[16,1280]{1,0:T(8,128)S(1)}) custom-call(bf16[96,16,128]{2,1,0:T(8,128)(2,1)S(1)} %get-tuple-element.25.listed_ref, f32[16,8,256]{2,1,0:T(8,128)S(1)} %get-tuple-element.26.pts_ref, bf16[16,256,48]{2,1,0:T(8,128)(2,1)S(1)} %get-tuple-element.27.cols_ref, ...), custom_call_target="tpu_custom_call" | custom-call | flops 11274289152 | bytes 11010048 | tf_op jit(solution)/shard_map/evaluate_9/pallas_call | solution.py:449
  25.3 0.0 copy-start.1
  25.3 1.9 %collective-permute-start.1 = (f32[16,1280]{1,0:T(8,128)S(1)}, f32[16,1280]{1,0:T(8,128)S(1)}, u32[]{:S(2)}, u32[]{:S(2)}) collective-permute-start(f32[16,1280]{1,0:T(8,128)S(1)} %get-tuple-element.35), channel_id=1, source_target_pairs={{0,4},{4,8},{8,12},{12,16},{16,20},{20,24},{24,28},{28,32},{32,36}... | collective-permute-start | bytes 245768 | tf_op jit(solution)/shard_map/ppermute | solution.py:539
  27.3 0.0 copy-done
  27.3 4.1 %evaluate_6.1 = (bf16[19,4,256,128]{3,2,1,0:T(8,128)(2,1)S(1)}, f32[16,4096]{1,0:T(8,128)S(1)}) custom-call(bf16[96,16,128]{2,1,0:T(8,128)(2,1)S(1)} %get-tuple-element.25.listed_ref, f32[16,8,256]{2,1,0:T(8,128)S(1)} %get-tuple-element.26.pts_ref, bf16[16,256,48]{2,1,0:T(8,128)(2,1)S(1)} %get-tuple-element.27.cols_ref, ...), custom_call_target="tpu_custom_call" | custom-call | flops 4831838208 | bytes 4718592 | tf_op jit(solution)/shard_map/evaluate_6/pallas_call | solution.py:449
  31.4 0.0 collective-permute-done.1
  31.4 2.6 %collective-permute-start.2 = (f32[16,1280]{1,0:T(8,128)S(1)}, f32[16,1280]{1,0:T(8,128)S(1)}, u32[]{:S(2)}, u32[]{:S(2)}) collective-permute-start(f32[16,1280]{1,0:T(8,128)S(1)} %slice_add_fusion), channel_id=1, source_target_pairs={{4,0},{8,4},{12,8},{16,12},{20,16},{24,20},{28,24},{32,28},{36,32}... | collective-permute-start | bytes 245768 | tf_op jit(solution)/shard_map/ppermute | solution.py:539
  34.0 0.2 multiply_reduce_fusion.2
  34.2 3.8 %apply_0.1.prev_ref = f32[21,16,256]{2,1,0:T(8,128)S(1)} custom-call(bf16[96,16,128]{2,1,0:T(8,128)(2,1)S(1)} %get-tuple-element.25.listed_ref, bf16[37,4,256,128]{3,2,1,0:T(8,128)(2,1)S(1)} %get-tuple-element.38.tiles_ref, f32[16,4096]{1,0:T(8,128)S(1)} %get-tuple-element.57.w_ref), custom_call_target="tpu_custom_call" | custom-call | flops 4966055936 | bytes 9699328 | tf_op jit(solution)/shard_map/apply_0/pallas_call | solution.py:462
  38.1 0.0 collective-permute-done.2.far_ref.rest_0_
  38.1 0.0 copy-done.1
  38.1 1.7 %apply_edge.1 = (f32[21,16,256]{2,1,0:T(8,128)S(1)}, f32[16,1280]{1,0:T(8,128)S(1)}, f32[16,256]{1,0:T(8,128)S(1)}) custom-call(bf16[96,16,128]{2,1,0:T(8,128)(2,1)S(1)} %get-tuple-element.25.listed_ref, bf16[43,4,256,128]{3,2,1,0:T(8,128)(2,1)S(1)} %get-tuple-element.37.tiles_ref.tiles_hbm, f32[16,4096]{1,0:T(8,128)S(1)} %get-tuple-element.57.w_ref, ...), custom_call_target="tpu_custom_call" | custom-call | flops 5771362304 | bytes 11272192 | tf_op jit(solution)/shard_map/apply_edge/pallas_call | solution.py:462
  39.8 2.0 %apply_6.1 = (f32[21,16,256]{2,1,0:T(8,128)S(1)}, f32[16,256]{1,0:T(8,128)S(1)}) custom-call(bf16[96,16,128]{2,1,0:T(8,128)(2,1)S(1)} %get-tuple-element.25.listed_ref, bf16[19,4,256,128]{3,2,1,0:T(8,128)(2,1)S(1)} %get-tuple-element.36.tiles_ref, f32[16,4096]{1,0:T(8,128)S(1)} %get-tuple-element.57.w_ref, ...), custom_call_target="tpu_custom_call" | custom-call | flops 2550136832 | bytes 4980736 | tf_op jit(solution)/shard_map/apply_6/pallas_call | solution.py:462
  41.8 0.1 reduce_sum.50
  41.9 0.1 collective-permute-start.3
  42.0 1.1 %collective-permute-done.3 = f32[4,16]{1,0:T(4,128)S(1)} collective-permute-done((f32[4,16]{1,0:T(4,128)S(1)}, f32[4,16]{1,0:T(4,128)S(1)}, u32[]{:S(2)}, u32[]{:S(2)}) %collective-permute-start.3) | collective-permute-done | bytes 288 | tf_op jit(solution)/shard_map/ppermute | solution.py:544
  43.2 0.1 reshape.39
  43.3 0.6 broadcast_in_dim.2
  43.9 12.5 %all-to-all-start = ((f32[32,1,64]{2,1,0:T(1,128)}), f32[32,1,64]{2,1,0:T(1,128)S(1)}, u32[]{:S(2)}, u32[]{:S(2)}) async-start(f32[32,1,64]{2,1,0:T(1,128)} %bitcast.5), calls=%async_computation | async-start | bytes 32768 | tf_op jit(solution)/shard_map/all_to_all | solution.py:548
  56.4 3.8 %collective-permute-start.4 = (f32[16,1280]{1,0:T(8,128)S(1)}, f32[16,1280]{1,0:T(8,128)S(1)}, u32[]{:S(2)}, u32[]{:S(2)}) collective-permute-start(f32[16,1280]{1,0:T(8,128)S(1)} %get-tuple-element.45), channel_id=1, source_target_pairs={{0,4},{4,8},{8,12},{12,16},{16,20},{20,24},{24,28},{28,32},{32,36}... | collective-permute-start | bytes 245768 | tf_op jit(solution)/shard_map/ppermute | solution.py:539
  60.2 7.7 %finish.1.rows_ref = f32[16,4096]{1,0:T(8,128)S(1)} custom-call(bf16[96,16,128]{2,1,0:T(8,128)(2,1)S(1)} %get-tuple-element.25.listed_ref, bf16[43,4,256,128]{3,2,1,0:T(8,128)(2,1)} %copy-done.1, f32[16,4096]{1,0:T(8,128)S(1)} %get-tuple-element.57.w_ref, f32[16,1280]{1,0:T(8,128)S(1)} %collective-permute-done.2.far_ref.rest_0_, ...), custom_call_target="tpu_custom_call" | custom-call | flops 5771362304 | bytes 11272192 | tf_op jit(solution)/shard_map/finish/pallas_call | solution.py:462
  67.8 0.0 collective-permute-done.4.back_ref
  67.9 0.0 all-to-all-done
  67.9 0.1 multiply_add_fusion.1
  68.0 0.1 add_divide_fusion
  68.1 1.0 %multiply_subtract_fusion = (f32[16,4096]{1,0:T(8,128)}, f32[16,4096]{1,0:T(8,128)}) fusion(f32[16,4096]{1,0:T(8,128)S(1)} %add_edge.1, f32[16,4096]{1,0:T(8,128)S(1)} %copy-done, f32[16]{0:T(128)S(1)} %get-tuple-element.52, f32[16]{0:T(128)S(1)} %get-tuple-element.51, f32[16]{0:T(128)S(1)} %get-tuple-element.54, f32[16,2816]{1,0:T(8,128)S(1)} %slice.11, ...), kind=kLoop, calls=%fused_computation.1 | loop fusion | flops 851968 | bytes 1310912 | tf_op jit(solution)/shard_map/sub | solution.py:600
  (7 shorter events, 0.1 us)
Async XLA Ops:
  3.4 12.9 %collective-permute-start = (f32[19,1280]{1,0:T(8,128)S(1)}, f32[19,1280]{1,0:T(8,128)S(1)}, u32[]{:S(2)}, u32[]{:S(2)}) collective-permute-start(f32[19,1280]{1,0:T(8,128)S(1)} %get-tuple-element.31), channel_id=1, source_target_pairs={{4,0},{8,4},{12,8},{16,12},{20,16},{24,20},{28,24},{32,28},{36,32}... | collective-permute-start | bytes 291848 | tf_op jit(solution)/shard_map/ppermute | solution.py:539
  16.3 11.0 %copy-start = (f32[16,4096]{1,0:T(8,128)S(1)}, f32[16,4096]{1,0:T(8,128)}, u32[]{:S(2)}) copy-start(f32[16,4096]{1,0:T(8,128)} %rest_0_.1) | copy-start | bytes 786436
  25.3 12.7 %copy-start.1 = (bf16[43,4,256,128]{3,2,1,0:T(8,128)(2,1)}, bf16[43,4,256,128]{3,2,1,0:T(8,128)(2,1)S(1)}, u32[]{:S(2)}) copy-start(bf16[43,4,256,128]{3,2,1,0:T(8,128)(2,1)S(1)} %get-tuple-element.37.tiles_ref.tiles_hbm) | copy-start | bytes 33816580
  25.3 6.1 %collective-permute-start.1 = (f32[16,1280]{1,0:T(8,128)S(1)}, f32[16,1280]{1,0:T(8,128)S(1)}, u32[]{:S(2)}, u32[]{:S(2)}) collective-permute-start(f32[16,1280]{1,0:T(8,128)S(1)} %get-tuple-element.35), channel_id=1, source_target_pairs={{0,4},{4,8},{8,12},{12,16},{16,20},{20,24},{24,28},{28,32},{32,36}... | collective-permute-start | bytes 245768 | tf_op jit(solution)/shard_map/ppermute | solution.py:539
  31.4 6.6 %collective-permute-start.2 = (f32[16,1280]{1,0:T(8,128)S(1)}, f32[16,1280]{1,0:T(8,128)S(1)}, u32[]{:S(2)}, u32[]{:S(2)}) collective-permute-start(f32[16,1280]{1,0:T(8,128)S(1)} %slice_add_fusion), channel_id=1, source_target_pairs={{4,0},{8,4},{12,8},{16,12},{20,16},{24,20},{28,24},{32,28},{36,32}... | collective-permute-start | bytes 245768 | tf_op jit(solution)/shard_map/ppermute | solution.py:539
  41.9 1.2 %collective-permute-start.3 = (f32[4,16]{1,0:T(4,128)S(1)}, f32[4,16]{1,0:T(4,128)S(1)}, u32[]{:S(2)}, u32[]{:S(2)}) collective-permute-start(f32[4,16]{1,0:T(4,128)S(1)} %pad_maximum_fusion.1), channel_id=1, source_target_pairs={{0,4},{4,0},{8,12},{12,8},{16,20},{20,16},{24,28},{28,24},{32,36},... | collective-permute-start | bytes 776 | tf_op jit(solution)/shard_map/ppermute | solution.py:544
  43.9 24.0 %all-to-all-start = ((f32[32,1,64]{2,1,0:T(1,128)}), f32[32,1,64]{2,1,0:T(1,128)S(1)}, u32[]{:S(2)}, u32[]{:S(2)}) async-start(f32[32,1,64]{2,1,0:T(1,128)} %bitcast.5), calls=%async_computation | async-start | bytes 32768 | tf_op jit(solution)/shard_map/all_to_all | solution.py:548
  56.4 11.4 %collective-permute-start.4 = (f32[16,1280]{1,0:T(8,128)S(1)}, f32[16,1280]{1,0:T(8,128)S(1)}, u32[]{:S(2)}, u32[]{:S(2)}) collective-permute-start(f32[16,1280]{1,0:T(8,128)S(1)} %get-tuple-element.45), channel_id=1, source_target_pairs={{0,4},{4,8},{8,12},{12,16},{16,20},{20,24},{24,28},{28,32},{32,36}... | collective-permute-start | bytes 245768 | tf_op jit(solution)/shard_map/ppermute | solution.py:539

commit v13 on v12

--- a/solution.py
+++ b/solution.py
@@ -559,7 +559,7 @@
     base = (lax.axis_index("leaf") * leaf_dev).astype(jnp.int32).reshape(1)
     *prepared, packed = prepare_call(leaf_pairs, pair_count, base, coords, site_order, probes)
     far = shift(packed, -1)
-    cut0, cut1 = leaf_dev - REACH - 5, leaf_dev - REACH - 2
+    cut0, cut1 = leaf_dev - REACH - 5, leaf_dev - REACH - 1
     evaluate = functools.partial(evaluate_call, leaf_dev=leaf_dev, n=n, prepared=prepared)
     tiles0, acc = evaluate(0, cut0, far=(), own=None, prev=None)
     tiles1, acc, send = evaluate(cut1, leaf_dev, far=(far,), own=None, prev=acc)

time: 69.3 us -> 69.1 us (level)
  transfers between devices with their start and end apart: 6 -> 6, of which waited for: 1 -> 1; matrix products, arithmetic and copies ran while one was open for 0% -> 0% of each run, Pallas kernels for 34% -> 35%
where the time goes in v13:
time: 69.1 us; the launch traced here: 68.9 us
  Pallas kernels  38 us (55%)
  starting transfers between devices  26.1 us (38%)
  other arithmetic  1.52 us (2%)
  between operations  1.43 us (2%)
  waiting for transfers between devices  1.16 us (2%)
  local copies, waits for them, and re-layouts  0.72 us (1%)
    pallas_call x3, Pallas kernels, evaluate_call(): pl.pallas_call(functools.partial(evaluate_kernel, i0, i1, leaf_dev, last)...  20.9 us
    pallas_call x4, Pallas kernels, small_call(): pl.pallas_call(kernel, out_shape=[jax.ShapeDtypeStruct(shape, jnp.float32...  15 us
    ppermute x4, starting transfers between devices, shift(): lax.ppermute(value, 'leaf', [(i, i + by) for i in range(length) if 0 <= i...  13.4 us
    all_to_all x1, starting transfers between devices, sum_over_leaf(): lax.all_to_all(copies, 'leaf', split_axis=0, concat_axis=0, tiled=True, a...  12.5 us
    pallas_call x1, Pallas kernels, prepare_call(): pl.pallas_call(prepare_kernel, out_shape=(jax.ShapeDtypeStruct((pairs.sha...  2.09 us
  transfers between devices with their start and end apart: 6, of which 1 were waited for; matrix products, arithmetic and copies ran while one was open for 0% of the time, Pallas kernels for 35%

profile of v13, /device:TPU:1, one launch (start us, length us, event | category | flops | bytes accessed | tf_op | source)
XLA Modules:
  0.0 68.9 jit_solution(11184027571038940624)
XLA Ops:
  1.3 2.1 %prepare.1 = (bf16[96,16,128]{2,1,0:T(8,128)(2,1)S(1)}, f32[16,8,256]{2,1,0:T(8,128)S(1)}, bf16[16,256,48]{2,1,0:T(8,128)(2,1)S(1)}, bf16[16,32,256]{2,1,0:T(8,1...) custom-call(s32[1]{0:T(128)S(6)} %copy.7.count_ref, s32[1]{0:T(128)} %bitcast.1.base_ref, ...), custom_call_target="tpu_custom_call" | custom-call | tf_op jit(solution)/shard_map/prepare/pallas_call | solution.py:405
  3.4 5.2 %collective-permute-start = (f32[19,1280]{1,0:T(8,128)S(1)}, f32[19,1280]{1,0:T(8,128)S(1)}, u32[]{:S(2)}, u32[]{:S(2)}) collective-permute-start(f32[19,1280]{1,0:T(8,128)S(1)} %get-tuple-element.31), channel_id=1, source_target_pairs={{4,0},{8,4},{12,8},{16,12},{20,16},{24,20},{28,24},{32,28},{36,32}... | collective-permute-start | bytes 291848 | tf_op jit(solution)/shard_map/ppermute | solution.py:539
  8.5 7.7 %evaluate_0.1 = (bf16[37,4,256,128]{3,2,1,0:T(8,128)(2,1)S(1)}, f32[21,16,256]{2,1,0:T(8,128)S(1)}) custom-call(bf16[96,16,128]{2,1,0:T(8,128)(2,1)S(1)} %get-tuple-element.25.listed_ref, f32[16,8,256]{2,1,0:T(8,128)S(1)} %get-tuple-element.26.pts_ref, bf16[16,256,48]{2,1,0:T(8,128)(2,1)S(1)} %get-tuple-element.27.cols_ref, ...), custom_call_target="tpu_custom_call" | custom-call | flops 9663676416 | bytes 9437184 | tf_op jit(solution)/shard_map/evaluate_0/pallas_call | solution.py:449
  16.3 0.0 collective-permute-done.rest_0_
  16.3 0.0 copy-start
  16.3 7.8 %evaluate_10.1 = (bf16[37,4,256,128]{3,2,1,0:T(8,128)(2,1)S(1)}, f32[21,16,256]{2,1,0:T(8,128)S(1)}, f32[16,1280]{1,0:T(8,128)S(1)}) custom-call(bf16[96,16,128]{2,1,0:T(8,128)(2,1)S(1)} %get-tuple-element.25.listed_ref, f32[16,8,256]{2,1,0:T(8,128)S(1)} %get-tuple-element.26.pts_ref, bf16[16,256,48]{2,1,0:T(8,128)(2,1)S(1)} %get-tuple-element.27.cols_ref, ...), custom_call_target="tpu_custom_call" | custom-call | flops 9663676416 | bytes 9437184 | tf_op jit(solution)/shard_map/evaluate_10/pallas_call | solution.py:449
  24.1 0.0 copy-start.1
  24.1 1.9 %collective-permute-start.1 = (f32[16,1280]{1,0:T(8,128)S(1)}, f32[16,1280]{1,0:T(8,128)S(1)}, u32[]{:S(2)}, u32[]{:S(2)}) collective-permute-start(f32[16,1280]{1,0:T(8,128)S(1)} %get-tuple-element.35), channel_id=1, source_target_pairs={{0,4},{4,8},{8,12},{12,16},{16,20},{20,24},{24,28},{28,32},{32,36}... | collective-permute-start | bytes 245768 | tf_op jit(solution)/shard_map/ppermute | solution.py:539
  26.1 0.0 copy-done
  26.1 5.3 %evaluate_6.1 = (bf16[25,4,256,128]{3,2,1,0:T(8,128)(2,1)S(1)}, f32[16,4096]{1,0:T(8,128)S(1)}) custom-call(bf16[96,16,128]{2,1,0:T(8,128)(2,1)S(1)} %get-tuple-element.25.listed_ref, f32[16,8,256]{2,1,0:T(8,128)S(1)} %get-tuple-element.26.pts_ref, bf16[16,256,48]{2,1,0:T(8,128)(2,1)S(1)} %get-tuple-element.27.cols_ref, ...), custom_call_target="tpu_custom_call" | custom-call | flops 6442450944 | bytes 6291456 | tf_op jit(solution)/shard_map/evaluate_6/pallas_call | solution.py:449
  31.4 0.0 collective-permute-done.1
  31.5 2.6 %collective-permute-start.2 = (f32[16,1280]{1,0:T(8,128)S(1)}, f32[16,1280]{1,0:T(8,128)S(1)}, u32[]{:S(2)}, u32[]{:S(2)}) collective-permute-start(f32[16,1280]{1,0:T(8,128)S(1)} %slice_add_fusion), channel_id=1, source_target_pairs={{4,0},{8,4},{12,8},{16,12},{20,16},{24,20},{28,24},{32,28},{36,32}... | collective-permute-start | bytes 245768 | tf_op jit(solution)/shard_map/ppermute | solution.py:539
  34.0 0.2 multiply_reduce_fusion.2
  34.2 3.8 %apply_0.1.prev_ref = f32[21,16,256]{2,1,0:T(8,128)S(1)} custom-call(bf16[96,16,128]{2,1,0:T(8,128)(2,1)S(1)} %get-tuple-element.25.listed_ref, bf16[37,4,256,128]{3,2,1,0:T(8,128)(2,1)S(1)} %get-tuple-element.38.tiles_ref, f32[16,4096]{1,0:T(8,128)S(1)} %get-tuple-element.57.w_ref), custom_call_target="tpu_custom_call" | custom-call | flops 4966055936 | bytes 9699328 | tf_op jit(solution)/shard_map/apply_0/pallas_call | solution.py:462
  38.1 0.0 collective-permute-done.2.far_ref.rest_0_
  38.1 0.0 copy-done.1
  38.1 1.5 %apply_edge.1 = (f32[21,16,256]{2,1,0:T(8,128)S(1)}, f32[16,1280]{1,0:T(8,128)S(1)}, f32[16,256]{1,0:T(8,128)S(1)}) custom-call(bf16[96,16,128]{2,1,0:T(8,128)(2,1)S(1)} %get-tuple-element.25.listed_ref, bf16[37,4,256,128]{3,2,1,0:T(8,128)(2,1)S(1)} %get-tuple-element.37.tiles_ref.tiles_hbm, f32[16,4096]{1,0:T(8,128)S(1)} %get-tuple-element.57.w_ref, ...), custom_call_target="tpu_custom_call" | custom-call | flops 4966055936 | bytes 9699328 | tf_op jit(solution)/shard_map/apply_edge/pallas_call | solution.py:462
  39.6 2.6 %apply_6.1 = (f32[21,16,256]{2,1,0:T(8,128)S(1)}, f32[16,256]{1,0:T(8,128)S(1)}) custom-call(bf16[96,16,128]{2,1,0:T(8,128)(2,1)S(1)} %get-tuple-element.25.listed_ref, bf16[25,4,256,128]{3,2,1,0:T(8,128)(2,1)S(1)} %get-tuple-element.36.tiles_ref, f32[16,4096]{1,0:T(8,128)S(1)} %get-tuple-element.57.w_ref, ...), custom_call_target="tpu_custom_call" | custom-call | flops 3355443200 | bytes 6553600 | tf_op jit(solution)/shard_map/apply_6/pallas_call | solution.py:462
  42.2 0.1 reduce_sum.50
  42.3 0.1 collective-permute-start.3
  42.4 1.1 %collective-permute-done.3 = f32[4,16]{1,0:T(4,128)S(1)} collective-permute-done((f32[4,16]{1,0:T(4,128)S(1)}, f32[4,16]{1,0:T(4,128)S(1)}, u32[]{:S(2)}, u32[]{:S(2)}) %collective-permute-start.3) | collective-permute-done | bytes 288 | tf_op jit(solution)/shard_map/ppermute | solution.py:544
  43.6 0.1 reshape.39
  43.7 0.6 broadcast_in_dim.2
  44.3 12.5 %all-to-all-start = ((f32[32,1,64]{2,1,0:T(1,128)}), f32[32,1,64]{2,1,0:T(1,128)S(1)}, u32[]{:S(2)}, u32[]{:S(2)}) async-start(f32[32,1,64]{2,1,0:T(1,128)} %bitcast.5), calls=%async_computation | async-start | bytes 32768 | tf_op jit(solution)/shard_map/all_to_all | solution.py:548
  56.8 3.8 %collective-permute-start.4 = (f32[16,1280]{1,0:T(8,128)S(1)}, f32[16,1280]{1,0:T(8,128)S(1)}, u32[]{:S(2)}, u32[]{:S(2)}) collective-permute-start(f32[16,1280]{1,0:T(8,128)S(1)} %get-tuple-element.45), channel_id=1, source_target_pairs={{0,4},{4,8},{8,12},{12,16},{16,20},{20,24},{24,28},{28,32},{32,36}... | collective-permute-start | bytes 245768 | tf_op jit(solution)/shard_map/ppermute | solution.py:539
  60.6 7.0 %finish.1.rows_ref = f32[16,4096]{1,0:T(8,128)S(1)} custom-call(bf16[96,16,128]{2,1,0:T(8,128)(2,1)S(1)} %get-tuple-element.25.listed_ref, bf16[37,4,256,128]{3,2,1,0:T(8,128)(2,1)} %copy-done.1, f32[16,4096]{1,0:T(8,128)S(1)} %get-tuple-element.57.w_ref, f32[16,1280]{1,0:T(8,128)S(1)} %collective-permute-done.2.far_ref.rest_0_, ...), custom_call_target="tpu_custom_call" | custom-call | flops 4966055936 | bytes 9699328 | tf_op jit(solution)/shard_map/finish/pallas_call | solution.py:462
  67.6 0.0 collective-permute-done.4.back_ref
  67.7 0.0 all-to-all-done
  67.7 0.1 multiply_add_fusion.1
  67.8 0.1 add_divide_fusion
  67.9 1.0 %multiply_subtract_fusion = (f32[16,4096]{1,0:T(8,128)}, f32[16,4096]{1,0:T(8,128)}) fusion(f32[16,4096]{1,0:T(8,128)S(1)} %add_edge.1, f32[16,4096]{1,0:T(8,128)S(1)} %copy-done, f32[16]{0:T(128)S(1)} %get-tuple-element.52, f32[16]{0:T(128)S(1)} %get-tuple-element.51, f32[16]{0:T(128)S(1)} %get-tuple-element.54, f32[16,2816]{1,0:T(8,128)S(1)} %slice.11, ...), kind=kLoop, calls=%fused_computation.1 | loop fusion | flops 851968 | bytes 1310912 | tf_op jit(solution)/shard_map/sub | solution.py:600
  (7 shorter events, 0.1 us)
Async XLA Ops:
  3.4 12.9 %collective-permute-start = (f32[19,1280]{1,0:T(8,128)S(1)}, f32[19,1280]{1,0:T(8,128)S(1)}, u32[]{:S(2)}, u32[]{:S(2)}) collective-permute-start(f32[19,1280]{1,0:T(8,128)S(1)} %get-tuple-element.31), channel_id=1, source_target_pairs={{4,0},{8,4},{12,8},{16,12},{20,16},{24,20},{28,24},{32,28},{36,32}... | collective-permute-start | bytes 291848 | tf_op jit(solution)/shard_map/ppermute | solution.py:539
  16.3 9.8 %copy-start = (f32[16,4096]{1,0:T(8,128)S(1)}, f32[16,4096]{1,0:T(8,128)}, u32[]{:S(2)}) copy-start(f32[16,4096]{1,0:T(8,128)} %rest_0_.1) | copy-start | bytes 786436
  24.1 14.0 %copy-start.1 = (bf16[37,4,256,128]{3,2,1,0:T(8,128)(2,1)}, bf16[37,4,256,128]{3,2,1,0:T(8,128)(2,1)S(1)}, u32[]{:S(2)}) copy-start(bf16[37,4,256,128]{3,2,1,0:T(8,128)(2,1)S(1)} %get-tuple-element.37.tiles_ref.tiles_hbm) | copy-start | bytes 29097988
  24.1 7.3 %collective-permute-start.1 = (f32[16,1280]{1,0:T(8,128)S(1)}, f32[16,1280]{1,0:T(8,128)S(1)}, u32[]{:S(2)}, u32[]{:S(2)}) collective-permute-start(f32[16,1280]{1,0:T(8,128)S(1)} %get-tuple-element.35), channel_id=1, source_target_pairs={{0,4},{4,8},{8,12},{12,16},{16,20},{20,24},{24,28},{28,32},{32,36}... | collective-permute-start | bytes 245768 | tf_op jit(solution)/shard_map/ppermute | solution.py:539
  31.5 6.6 %collective-permute-start.2 = (f32[16,1280]{1,0:T(8,128)S(1)}, f32[16,1280]{1,0:T(8,128)S(1)}, u32[]{:S(2)}, u32[]{:S(2)}) collective-permute-start(f32[16,1280]{1,0:T(8,128)S(1)} %slice_add_fusion), channel_id=1, source_target_pairs={{4,0},{8,4},{12,8},{16,12},{20,16},{24,20},{28,24},{32,28},{36,32}... | collective-permute-start | bytes 245768 | tf_op jit(solution)/shard_map/ppermute | solution.py:539
  42.3 1.2 %collective-permute-start.3 = (f32[4,16]{1,0:T(4,128)S(1)}, f32[4,16]{1,0:T(4,128)S(1)}, u32[]{:S(2)}, u32[]{:S(2)}) collective-permute-start(f32[4,16]{1,0:T(4,128)S(1)} %pad_maximum_fusion.1), channel_id=1, source_target_pairs={{0,4},{4,0},{8,12},{12,8},{16,20},{20,16},{24,28},{28,24},{32,36},... | collective-permute-start | bytes 776 | tf_op jit(solution)/shard_map/ppermute | solution.py:544
  44.3 23.4 %all-to-all-start = ((f32[32,1,64]{2,1,0:T(1,128)}), f32[32,1,64]{2,1,0:T(1,128)S(1)}, u32[]{:S(2)}, u32[]{:S(2)}) async-start(f32[32,1,64]{2,1,0:T(1,128)} %bitcast.5), calls=%async_computation | async-start | bytes 32768 | tf_op jit(solution)/shard_map/all_to_all | solution.py:548
  56.8 10.8 %collective-permute-start.4 = (f32[16,1280]{1,0:T(8,128)S(1)}, f32[16,1280]{1,0:T(8,128)S(1)}, u32[]{:S(2)}, u32[]{:S(2)}) collective-permute-start(f32[16,1280]{1,0:T(8,128)S(1)} %get-tuple-element.45), channel_id=1, source_target_pairs={{0,4},{4,8},{8,12},{12,16},{16,20},{20,24},{24,28},{28,32},{32,36}... | collective-permute-start | bytes 245768 | tf_op jit(solution)/shard_map/ppermute | solution.py:539

commit v14 on v13

--- a/solution.py
+++ b/solution.py
@@ -559,7 +559,7 @@
     base = (lax.axis_index("leaf") * leaf_dev).astype(jnp.int32).reshape(1)
     *prepared, packed = prepare_call(leaf_pairs, pair_count, base, coords, site_order, probes)
     far = shift(packed, -1)
-    cut0, cut1 = leaf_dev - REACH - 5, leaf_dev - REACH - 1
+    cut0, cut1 = leaf_dev - REACH - 5, leaf_dev - REACH
     evaluate = functools.partial(evaluate_call, leaf_dev=leaf_dev, n=n, prepared=prepared)
     tiles0, acc = evaluate(0, cut0, far=(), own=None, prev=None)
     tiles1, acc, send = evaluate(cut1, leaf_dev, far=(far,), own=None, prev=acc)

time: 69.1 us -> 68.3 us (0.988)
  Pallas kernels: 38 us -> 37.2 us
    pallas_call x4, Pallas kernels: 15 us -> 14.1 us  [small_call(): pl.pallas_call(kernel, out_shape=[jax.ShapeDtypeStruct(shape, jnp.float32...]
where the time goes in v14:
time: 68.3 us; the launch traced here: 68.1 us
  Pallas kernels  37.2 us (54%)
  starting transfers between devices  26 us (38%)
  other arithmetic  1.52 us (2%)
  between operations  1.43 us (2%)
  waiting for transfers between devices  1.16 us (2%)
  local copies, waits for them, and re-layouts  0.72 us (1%)
    pallas_call x3, Pallas kernels, evaluate_call(): pl.pallas_call(functools.partial(evaluate_kernel, i0, i1, leaf_dev, last)...  21 us
    pallas_call x4, Pallas kernels, small_call(): pl.pallas_call(kernel, out_shape=[jax.ShapeDtypeStruct(shape, jnp.float32...  14.1 us
    ppermute x4, starting transfers between devices, shift(): lax.ppermute(value, 'leaf', [(i, i + by) for i in range(length) if 0 <= i...  13.4 us
    all_to_all x1, starting transfers between devices, sum_over_leaf(): lax.all_to_all(copies, 'leaf', split_axis=0, concat_axis=0, tiled=True, a...  12.5 us
    pallas_call x1, Pallas kernels, prepare_call(): pl.pallas_call(prepare_kernel, out_shape=(jax.ShapeDtypeStruct((pairs.sha...  2.09 us
  transfers between devices with their start and end apart: 6, of which 1 were waited for; matrix products, arithmetic and copies ran while one was open for 0% of the time, Pallas kernels for 35%

profile of v14, /device:TPU:1, one launch (start us, length us, event | category | flops | bytes accessed | tf_op | source)
XLA Modules:
  0.0 68.1 jit_solution(1023158679467264622)
XLA Ops:
  1.3 2.1 %prepare.1 = (bf16[96,16,128]{2,1,0:T(8,128)(2,1)S(1)}, f32[16,8,256]{2,1,0:T(8,128)S(1)}, bf16[16,256,48]{2,1,0:T(8,128)(2,1)S(1)}, bf16[16,32,256]{2,1,0:T(8,1...) custom-call(s32[1]{0:T(128)S(6)} %copy.7.count_ref, s32[1]{0:T(128)} %bitcast.1.base_ref, ...), custom_call_target="tpu_custom_call" | custom-call | tf_op jit(solution)/shard_map/prepare/pallas_call | solution.py:405
  3.4 5.2 %collective-permute-start = (f32[19,1280]{1,0:T(8,128)S(1)}, f32[19,1280]{1,0:T(8,128)S(1)}, u32[]{:S(2)}, u32[]{:S(2)}) collective-permute-start(f32[19,1280]{1,0:T(8,128)S(1)} %get-tuple-element.31), channel_id=1, source_target_pairs={{4,0},{8,4},{12,8},{16,12},{20,16},{24,20},{28,24},{32,28},{36,32}... | collective-permute-start | bytes 291848 | tf_op jit(solution)/shard_map/ppermute | solution.py:539
  8.5 7.8 %evaluate_0.1 = (bf16[37,4,256,128]{3,2,1,0:T(8,128)(2,1)S(1)}, f32[21,16,256]{2,1,0:T(8,128)S(1)}) custom-call(bf16[96,16,128]{2,1,0:T(8,128)(2,1)S(1)} %get-tuple-element.25.listed_ref, f32[16,8,256]{2,1,0:T(8,128)S(1)} %get-tuple-element.26.pts_ref, bf16[16,256,48]{2,1,0:T(8,128)(2,1)S(1)} %get-tuple-element.27.cols_ref, ...), custom_call_target="tpu_custom_call" | custom-call | flops 9663676416 | bytes 9437184 | tf_op jit(solution)/shard_map/evaluate_0/pallas_call | solution.py:449
  16.3 0.0 collective-permute-done.rest_0_
  16.3 0.0 copy-start
  16.3 6.6 %evaluate_11.1 = (bf16[31,4,256,128]{3,2,1,0:T(8,128)(2,1)S(1)}, f32[21,16,256]{2,1,0:T(8,128)S(1)}, f32[16,1280]{1,0:T(8,128)S(1)}) custom-call(bf16[96,16,128]{2,1,0:T(8,128)(2,1)S(1)} %get-tuple-element.25.listed_ref, f32[16,8,256]{2,1,0:T(8,128)S(1)} %get-tuple-element.26.pts_ref, bf16[16,256,48]{2,1,0:T(8,128)(2,1)S(1)} %get-tuple-element.27.cols_ref, ...), custom_call_target="tpu_custom_call" | custom-call | flops 8053063680 | bytes 7864320 | tf_op jit(solution)/shard_map/evaluate_11/pallas_call | solution.py:449
  22.9 0.0 copy-start.1
  22.9 1.9 %collective-permute-start.1 = (f32[16,1280]{1,0:T(8,128)S(1)}, f32[16,1280]{1,0:T(8,128)S(1)}, u32[]{:S(2)}, u32[]{:S(2)}) collective-permute-start(f32[16,1280]{1,0:T(8,128)S(1)} %get-tuple-element.35), channel_id=1, source_target_pairs={{0,4},{4,8},{8,12},{12,16},{16,20},{20,24},{24,28},{28,32},{32,36}... | collective-permute-start | bytes 245768 | tf_op jit(solution)/shard_map/ppermute | solution.py:539
  24.9 0.0 copy-done
  24.9 6.6 %evaluate_6.1 = (bf16[31,4,256,128]{3,2,1,0:T(8,128)(2,1)S(1)}, f32[16,4096]{1,0:T(8,128)S(1)}) custom-call(bf16[96,16,128]{2,1,0:T(8,128)(2,1)S(1)} %get-tuple-element.25.listed_ref, f32[16,8,256]{2,1,0:T(8,128)S(1)} %get-tuple-element.26.pts_ref, bf16[16,256,48]{2,1,0:T(8,128)(2,1)S(1)} %get-tuple-element.27.cols_ref, ...), custom_call_target="tpu_custom_call" | custom-call | flops 8053063680 | bytes 7864320 | tf_op jit(solution)/shard_map/evaluate_6/pallas_call | solution.py:449
  31.5 0.0 collective-permute-done.1
  31.5 2.6 %collective-permute-start.2 = (f32[16,1280]{1,0:T(8,128)S(1)}, f32[16,1280]{1,0:T(8,128)S(1)}, u32[]{:S(2)}, u32[]{:S(2)}) collective-permute-start(f32[16,1280]{1,0:T(8,128)S(1)} %slice_add_fusion), channel_id=1, source_target_pairs={{4,0},{8,4},{12,8},{16,12},{20,16},{24,20},{28,24},{32,28},{36,32}... | collective-permute-start | bytes 245768 | tf_op jit(solution)/shard_map/ppermute | solution.py:539
  34.1 0.2 multiply_reduce_fusion.2
  34.3 3.8 %apply_0.1.prev_ref = f32[21,16,256]{2,1,0:T(8,128)S(1)} custom-call(bf16[96,16,128]{2,1,0:T(8,128)(2,1)S(1)} %get-tuple-element.25.listed_ref, bf16[37,4,256,128]{3,2,1,0:T(8,128)(2,1)S(1)} %get-tuple-element.38.tiles_ref, f32[16,4096]{1,0:T(8,128)S(1)} %get-tuple-element.57.w_ref), custom_call_target="tpu_custom_call" | custom-call | flops 4966055936 | bytes 9699328 | tf_op jit(solution)/shard_map/apply_0/pallas_call | solution.py:462
  38.2 0.0 collective-permute-done.2.far_ref.rest_0_
  38.2 0.0 copy-done.1
  38.2 1.3 %apply_edge.1 = (f32[21,16,256]{2,1,0:T(8,128)S(1)}, f32[16,1280]{1,0:T(8,128)S(1)}, f32[16,256]{1,0:T(8,128)S(1)}) custom-call(bf16[96,16,128]{2,1,0:T(8,128)(2,1)S(1)} %get-tuple-element.25.listed_ref, bf16[31,4,256,128]{3,2,1,0:T(8,128)(2,1)S(1)} %get-tuple-element.37.tiles_ref.tiles_hbm, f32[16,4096]{1,0:T(8,128)S(1)} %get-tuple-element.57.w_ref, ...), custom_call_target="tpu_custom_call" | custom-call | flops 4160749568 | bytes 8126464 | tf_op jit(solution)/shard_map/apply_edge/pallas_call | solution.py:462
  39.4 3.2 %apply_6.1 = (f32[21,16,256]{2,1,0:T(8,128)S(1)}, f32[16,256]{1,0:T(8,128)S(1)}) custom-call(bf16[96,16,128]{2,1,0:T(8,128)(2,1)S(1)} %get-tuple-element.25.listed_ref, bf16[31,4,256,128]{3,2,1,0:T(8,128)(2,1)S(1)} %get-tuple-element.36.tiles_ref, f32[16,4096]{1,0:T(8,128)S(1)} %get-tuple-element.57.w_ref, ...), custom_call_target="tpu_custom_call" | custom-call | flops 4160749568 | bytes 8126464 | tf_op jit(solution)/shard_map/apply_6/pallas_call | solution.py:462
  42.7 0.1 reduce_sum.50
  42.8 0.1 collective-permute-start.3
  42.9 1.1 %collective-permute-done.3 = f32[4,16]{1,0:T(4,128)S(1)} collective-permute-done((f32[4,16]{1,0:T(4,128)S(1)}, f32[4,16]{1,0:T(4,128)S(1)}, u32[]{:S(2)}, u32[]{:S(2)}) %collective-permute-start.3) | collective-permute-done | bytes 288 | tf_op jit(solution)/shard_map/ppermute | solution.py:544
  44.1 0.1 reshape.39
  44.2 0.6 broadcast_in_dim.2
  44.8 12.5 %all-to-all-start = ((f32[32,1,64]{2,1,0:T(1,128)}), f32[32,1,64]{2,1,0:T(1,128)S(1)}, u32[]{:S(2)}, u32[]{:S(2)}) async-start(f32[32,1,64]{2,1,0:T(1,128)} %bitcast.5), calls=%async_computation | async-start | bytes 32768 | tf_op jit(solution)/shard_map/all_to_all | solution.py:548
  57.3 3.8 %collective-permute-start.4 = (f32[16,1280]{1,0:T(8,128)S(1)}, f32[16,1280]{1,0:T(8,128)S(1)}, u32[]{:S(2)}, u32[]{:S(2)}) collective-permute-start(f32[16,1280]{1,0:T(8,128)S(1)} %get-tuple-element.45), channel_id=1, source_target_pairs={{0,4},{4,8},{8,12},{12,16},{16,20},{20,24},{24,28},{28,32},{32,36}... | collective-permute-start | bytes 245768 | tf_op jit(solution)/shard_map/ppermute | solution.py:539
  61.1 5.8 %finish.1.rows_ref = f32[16,4096]{1,0:T(8,128)S(1)} custom-call(bf16[96,16,128]{2,1,0:T(8,128)(2,1)S(1)} %get-tuple-element.25.listed_ref, bf16[31,4,256,128]{3,2,1,0:T(8,128)(2,1)} %copy-done.1, f32[16,4096]{1,0:T(8,128)S(1)} %get-tuple-element.57.w_ref, f32[16,1280]{1,0:T(8,128)S(1)} %collective-permute-done.2.far_ref.rest_0_, ...), custom_call_target="tpu_custom_call" | custom-call | flops 4160749568 | bytes 8126464 | tf_op jit(solution)/shard_map/finish/pallas_call | solution.py:462
  66.9 0.0 collective-permute-done.4.back_ref
  66.9 0.0 all-to-all-done
  66.9 0.1 multiply_add_fusion.1
  67.0 0.1 add_divide_fusion
  67.1 1.0 %multiply_subtract_fusion = (f32[16,4096]{1,0:T(8,128)}, f32[16,4096]{1,0:T(8,128)}) fusion(f32[16,4096]{1,0:T(8,128)S(1)} %add_edge.1, f32[16,4096]{1,0:T(8,128)S(1)} %copy-done, f32[16]{0:T(128)S(1)} %get-tuple-element.52, f32[16]{0:T(128)S(1)} %get-tuple-element.51, f32[16]{0:T(128)S(1)} %get-tuple-element.54, f32[16,2816]{1,0:T(8,128)S(1)} %slice.11, ...), kind=kLoop, calls=%fused_computation.1 | loop fusion | flops 851968 | bytes 1310912 | tf_op jit(solution)/shard_map/sub | solution.py:600
  (7 shorter events, 0.1 us)
Async XLA Ops:
  3.4 12.9 %collective-permute-start = (f32[19,1280]{1,0:T(8,128)S(1)}, f32[19,1280]{1,0:T(8,128)S(1)}, u32[]{:S(2)}, u32[]{:S(2)}) collective-permute-start(f32[19,1280]{1,0:T(8,128)S(1)} %get-tuple-element.31), channel_id=1, source_target_pairs={{4,0},{8,4},{12,8},{16,12},{20,16},{24,20},{28,24},{32,28},{36,32}... | collective-permute-start | bytes 291848 | tf_op jit(solution)/shard_map/ppermute | solution.py:539
  16.3 8.6 %copy-start = (f32[16,4096]{1,0:T(8,128)S(1)}, f32[16,4096]{1,0:T(8,128)}, u32[]{:S(2)}) copy-start(f32[16,4096]{1,0:T(8,128)} %rest_0_.1) | copy-start | bytes 786436
  22.9 15.3 %copy-start.1 = (bf16[31,4,256,128]{3,2,1,0:T(8,128)(2,1)}, bf16[31,4,256,128]{3,2,1,0:T(8,128)(2,1)S(1)}, u32[]{:S(2)}) copy-start(bf16[31,4,256,128]{3,2,1,0:T(8,128)(2,1)S(1)} %get-tuple-element.37.tiles_ref.tiles_hbm) | copy-start | bytes 24379396
  22.9 8.6 %collective-permute-start.1 = (f32[16,1280]{1,0:T(8,128)S(1)}, f32[16,1280]{1,0:T(8,128)S(1)}, u32[]{:S(2)}, u32[]{:S(2)}) collective-permute-start(f32[16,1280]{1,0:T(8,128)S(1)} %get-tuple-element.35), channel_id=1, source_target_pairs={{0,4},{4,8},{8,12},{12,16},{16,20},{20,24},{24,28},{28,32},{32,36}... | collective-permute-start | bytes 245768 | tf_op jit(solution)/shard_map/ppermute | solution.py:539
  31.5 6.6 %collective-permute-start.2 = (f32[16,1280]{1,0:T(8,128)S(1)}, f32[16,1280]{1,0:T(8,128)S(1)}, u32[]{:S(2)}, u32[]{:S(2)}) collective-permute-start(f32[16,1280]{1,0:T(8,128)S(1)} %slice_add_fusion), channel_id=1, source_target_pairs={{4,0},{8,4},{12,8},{16,12},{20,16},{24,20},{28,24},{32,28},{36,32}... | collective-permute-start | bytes 245768 | tf_op jit(solution)/shard_map/ppermute | solution.py:539
  42.8 1.2 %collective-permute-start.3 = (f32[4,16]{1,0:T(4,128)S(1)}, f32[4,16]{1,0:T(4,128)S(1)}, u32[]{:S(2)}, u32[]{:S(2)}) collective-permute-start(f32[4,16]{1,0:T(4,128)S(1)} %pad_maximum_fusion.1), channel_id=1, source_target_pairs={{0,4},{4,0},{8,12},{12,8},{16,20},{20,16},{24,28},{28,24},{32,36},... | collective-permute-start | bytes 776 | tf_op jit(solution)/shard_map/ppermute | solution.py:544
  44.8 22.1 %all-to-all-start = ((f32[32,1,64]{2,1,0:T(1,128)}), f32[32,1,64]{2,1,0:T(1,128)S(1)}, u32[]{:S(2)}, u32[]{:S(2)}) async-start(f32[32,1,64]{2,1,0:T(1,128)} %bitcast.5), calls=%async_computation | async-start | bytes 32768 | tf_op jit(solution)/shard_map/all_to_all | solution.py:548
  57.3 9.6 %collective-permute-start.4 = (f32[16,1280]{1,0:T(8,128)S(1)}, f32[16,1280]{1,0:T(8,128)S(1)}, u32[]{:S(2)}, u32[]{:S(2)}) collective-permute-start(f32[16,1280]{1,0:T(8,128)S(1)} %get-tuple-element.45), channel_id=1, source_target_pairs={{0,4},{4,8},{8,12},{12,16},{16,20},{20,24},{24,28},{28,32},{32,36}... | collective-permute-start | bytes 245768 | tf_op jit(solution)/shard_map/ppermute | solution.py:539
